TPU v7x, 256 devices: a whole 4x4x8 slice. The times are simulated.
256 devices in a mesh: dp: 4 (over x), space: 64 (over y, z, core).
Axes of the slice: x: 4, y: 4, z: 8, core: 2. Of those that a mesh axis runs over, the one named last changes fastest.
Arguments:
- features: bfloat16 [4, 64, 96, 1024], P('dp', 'space'), may hold values from -6 to 6
- cotangent: bfloat16 [4, 64, 192, 128], P('dp', 'space'), may hold values from -6 to 6
- conv_weight: bfloat16 [96, 2592], replicated, may hold values from -0.125 to 0.125
- down_weight: bfloat16 [192, 768], replicated, may hold values from -0.21875 to 0.21875
- neighbours: int32 [4, 64, 26], P('dp', 'space'), may hold values from -1 to 63, as said below
Outputs:
- coarse_out: bfloat16 [4, 64, 192, 128], P('dp', 'space')
- grad_features: float32 [4, 64, 96, 1024], P('dp', 'space')
- grad_conv: float32 [96, 2592], replicated
- grad_down: float32 [192, 768], replicated
Inputs may be any that keep to these rules, and one draw needn't show every extreme that they name: The blocks of a tile sit at distinct cells of a grid; if neighbours[t, s, d] = p is not -1 then neighbours[t, p, 25 - d] = s; a row never names its own block and names a device at most once.
All inputs are finite; a program needn't handle non-finite values.
Results may differ from a plain program's by a relative error of at most 0.0095.
Values may be sent and summed in bfloat16 or wider, within the bound.
No kernel may reach another device: no remote copies, remote signals or barrier semaphores. Data moves between devices by JAX's collectives and lax.ppermute only.
A program may use at most 128 MiB of HBM per device.

v0:
```python
import jax
import jax.numpy as jnp
from jax import lax
from jax.sharding import PartitionSpec as P

BRICK = 8


DIRECTIONS = [
    (step_x, step_y, step_z)
    for step_x in (-1, 0, 1)
    for step_y in (-1, 0, 1)
    for step_z in (-1, 0, 1)
    if (step_x, step_y, step_z) != (0, 0, 0)
]
EPSILON = 1e-06


def cut_inner(offset, extent):
    if offset < 0:
        return slice(0, 1)
    if offset > 0:
        return slice(extent - 1, extent)
    return slice(0, extent)


def cut_outer(offset, extent):
    if offset < 0:
        return slice(0, 1)
    if offset > 0:
        return slice(extent + 1, extent + 2)
    return slice(1, extent + 1)


def inner_layer(block_data, offset):
    return block_data[
        :,
        cut_inner(offset[0], block_data.shape[1]),
        cut_inner(offset[1], block_data.shape[2]),
        cut_inner(offset[2], block_data.shape[3]),
    ]


def outer_layer(padded, offset):
    return padded[
        :,
        cut_outer(offset[0], padded.shape[1] - 2),
        cut_outer(offset[1], padded.shape[2] - 2),
        cut_outer(offset[2], padded.shape[3] - 2),
    ]


def conv_taps(padded, weight_matrix):
    channels = padded.shape[0]
    size_x, size_y, size_z = (padded.shape[1] - 2, padded.shape[2] - 2, padded.shape[3] - 2)
    accumulated = jnp.zeros((weight_matrix.shape[0], size_x * size_y * size_z), jnp.float32)
    for step_x in range(3):
        for step_y in range(3):
            columns = jnp.concatenate(
                [
                    padded[
                        :,
                        step_x : step_x + size_x,
                        step_y : step_y + size_y,
                        step_z : step_z + size_z,
                    ]
                    for step_z in range(3)
                ],
                axis=0,
            ).reshape(3 * channels, size_x * size_y * size_z)
            start_col = (step_x * 3 + step_y) * 3 * channels
            accumulated = accumulated + jnp.dot(
                weight_matrix[:, start_col : start_col + 3 * channels],
                columns,
                preferred_element_type=jnp.float32,
            )
    return accumulated


def weight_taps(padded, grad_out):
    channels = padded.shape[0]
    size_x, size_y, size_z = (padded.shape[1] - 2, padded.shape[2] - 2, padded.shape[3] - 2)
    blocks_out = []
    for step_x in range(3):
        for step_y in range(3):
            columns = jnp.concatenate(
                [
                    padded[
                        :,
                        step_x : step_x + size_x,
                        step_y : step_y + size_y,
                        step_z : step_z + size_z,
                    ]
                    for step_z in range(3)
                ],
                axis=0,
            ).reshape(3 * channels, size_x * size_y * size_z)
            blocks_out.append(
                lax.dot_general(
                    grad_out, columns, (((1,), (1,)), ((), ())), preferred_element_type=jnp.float32
                )
            )
    return jnp.concatenate(blocks_out, axis=1)


def flipped(weight_matrix):
    channels = weight_matrix.shape[0]
    return (
        weight_matrix.reshape(channels, 27, channels)[:, ::-1, :]
        .transpose(2, 1, 0)
        .reshape(channels, 27 * channels)
    )


def coarse_patches(hidden_block):
    channels, size_x, size_y, size_z = hidden_block.shape
    split = hidden_block.reshape(channels, size_x // 2, 2, size_y // 2, 2, size_z // 2, 2)
    return split.transpose(2, 4, 6, 0, 1, 3, 5).reshape(
        8 * channels, size_x // 2 * (size_y // 2) * (size_z // 2)
    )


def from_patches(patch_data, channels, size_x, size_y, size_z):
    split = patch_data.reshape(2, 2, 2, channels, size_x // 2, size_y // 2, size_z // 2)
    return split.transpose(3, 4, 0, 5, 1, 6, 2).reshape(channels, size_x * size_y * size_z)


def silu_slope(activation):
    sigmoid_value = jax.nn.sigmoid(activation)
    return sigmoid_value * (1.0 + activation * (1.0 - sigmoid_value))


def normalized(accumulated):
    return accumulated * lax.rsqrt(jnp.mean(accumulated * accumulated) + EPSILON)


def shards(features, cotangent, conv_weight, down_weight, neighbours):
    channels = features.shape[2]
    block_side = BRICK
    block_depth = features.shape[3] // (block_side * block_side)
    peer_count = lax.axis_size("space")
    capacity = max(block_side * block_side, block_side * block_depth)
    owner_row = neighbours[0, 0]
    present = owner_row >= 0
    target = jnp.where(present, owner_row, peer_count)
    source = jnp.clip(owner_row, 0, peer_count - 1)

    def pack_faces(face_layers, wire_type):
        stacked = jnp.stack(
            [
                jnp.pad(
                    face_layer.reshape(channels, -1), ((0, 0), (0, capacity - face_layer[0].size))
                )
                for face_layer in face_layers
            ]
        )
        return (
            jnp.zeros((peer_count, channels, capacity), wire_type)
            .at[target]
            .set(stacked, mode="drop")
        )

    def unpack_faces(received, shapes):
        picked = jnp.take(received, source, axis=0) * present[:, None, None].astype(received.dtype)
        pieces = []
        for number, shape in enumerate(shapes):
            count = shape[1] * shape[2] * shape[3]
            pieces.append(picked[number, :, :count].reshape(shape))
        return pieces

    def fill_rim(block_data, received):
        padded = jnp.pad(block_data, ((0, 0), (1, 1), (1, 1), (1, 1)))
        pieces = unpack_faces(
            received, [inner_layer(block_data, offset).shape for offset in DIRECTIONS]
        )
        for offset, face_piece in zip(DIRECTIONS, pieces):
            padded = padded.at[
                :,
                cut_outer(offset[0], block_side),
                cut_outer(offset[1], block_side),
                cut_outer(offset[2], block_depth),
            ].set(face_piece)
        return padded

    own_block = features[0, 0].reshape(channels, block_side, block_side, block_depth)
    sent = pack_faces([inner_layer(own_block, offset) for offset in DIRECTIONS], jnp.bfloat16)
    received = lax.all_to_all(sent, "space", split_axis=0, concat_axis=0, tiled=True)
    padded = fill_rim(own_block, received)
    preact = conv_taps(padded, conv_weight)
    hidden = jax.nn.silu(preact).astype(jnp.bfloat16)
    patches = coarse_patches(hidden.reshape(channels, block_side, block_side, block_depth))
    coarse_out = jnp.dot(down_weight, patches, preferred_element_type=jnp.float32).astype(
        jnp.bfloat16
    )
    cot_block = cotangent[0, 0]
    down_part = lax.dot_general(
        cot_block, patches, (((1,), (1,)), ((), ())), preferred_element_type=jnp.float32
    )
    spread_back = from_patches(
        jnp.dot(down_weight.T, cot_block, preferred_element_type=jnp.float32),
        channels,
        block_side,
        block_side,
        block_depth,
    )
    grad_pre = (spread_back * silu_slope(preact)).astype(jnp.bfloat16)
    conv_part = weight_taps(padded, grad_pre)
    flip_weight = flipped(conv_weight)
    grad_block = grad_pre.reshape(channels, block_side, block_side, block_depth)
    widened = jnp.pad(grad_block, ((0, 0), (2, 2), (2, 2), (2, 2)))
    full_grad = conv_taps(widened, flip_weight).reshape(
        channels, block_side + 2, block_side + 2, block_depth + 2
    )
    spill_buffer = pack_faces(
        [outer_layer(full_grad, offset) for offset in DIRECTIONS], jnp.float32
    )
    got_spill = lax.all_to_all(
        spill_buffer.astype(jnp.bfloat16), "space", split_axis=0, concat_axis=0, tiled=True
    ).astype(spill_buffer.dtype)
    inner_part = full_grad[:, 1:-1, 1:-1, 1:-1]
    pieces = unpack_faces(
        got_spill, [inner_layer(inner_part, offset).shape for offset in DIRECTIONS]
    )
    for offset, face_piece in zip(DIRECTIONS, pieces):
        inner_part = inner_part.at[
            :,
            cut_inner(offset[0], block_side),
            cut_inner(offset[1], block_side),
            cut_inner(offset[2], block_depth),
        ].add(face_piece)
    grad_features = inner_part.reshape(channels, -1)
    conv_sum, down_sum = lax.psum((conv_part, down_part), ("dp", "space"))
    return (
        coarse_out[None, None],
        grad_features[None, None],
        normalized(conv_sum),
        normalized(down_sum),
    )


def solution(mesh):
    placed = (
        P("dp", "space", None, None),
        P("dp", "space", None, None),
        P(),
        P(),
        P("dp", "space", None),
    )
    return jax.shard_map(
        shards,
        mesh=mesh,
        in_specs=placed,
        out_specs=(P("dp", "space", None, None), P("dp", "space", None, None), P(), P()),
        check_vma=False,
    )
```

profile of v0, /device:TPU:1, one launch (start us, length us, event | category | flops | bytes accessed | tf_op | source)
XLA Modules:
  0.0 608.5 jit_solution(4286179501511224729)
XLA Ops:
  10.8 5.5 scatter_fusion
  16.2 13.3 %all-to-all-start = ((bf16[64,96,128]{2,1,0:T(8,128)(2,1)}), bf16[64,96,128]{2,1,0:T(8,128)(2,1)S(1)}, u32[]{:S(2)}, u32[]{:S(2)}) async-start(bf16[64,96,128]{2,1,0:T(8,128)(2,1)} %scatter_fusion), calls=%async_computation | async-start | bytes 3145728 | tf_op jit(solution)/shard_map/all_to_all | solution.py:187
  33.1 36.2 %all-to-all-done = bf16[64,96,128]{2,1,0:T(8,128)(2,1)S(1)} async-done(((bf16[64,96,128]{2,1,0:T(8,128)(2,1)}), bf16[64,96,128]{2,1,0:T(8,128)(2,1)S(1)}, u32[]{:S(2)}, u32[]{:S(2)}) %all-to-all-start) | async-done | bytes 1572896 | tf_op jit(solution)/shard_map/all_to_all | solution.py:187
  91.0 2.0 multiply_convert_fusion
  97.9 5.5 pad_slice_fusion.2
  103.4 2.2 pad_slice_fusion.1
  107.4 2.4 pad_maximum_fusion.7
  109.8 1.9 reshape.2479
  111.7 2.4 pad_maximum_fusion.6
  114.1 1.9 reshape.2478
  116.0 2.4 pad_maximum_fusion.5
  120.2 2.4 pad_maximum_fusion.4
  124.5 2.4 pad_maximum_fusion.3
  128.8 2.6 pad_maximum_fusion.2
  133.2 2.4 pad_maximum_fusion.1
  137.5 2.4 pad_maximum_fusion
  141.8 2.1 fusion.13
  156.4 3.7 scatter_fusion.1
  161.6 6.4 %all-to-all-start.1 = ((bf16[64,96,128]{2,1,0:T(8,128)(2,1)}), bf16[64,96,128]{2,1,0:T(8,128)(2,1)}, u32[]{:S(2)}, u32[]{:S(2)}) async-start(bf16[64,96,128]{2,1,0:T(8,128)(2,1)} %convert_element_type.100), calls=%async_computation.1 | async-start | bytes 3145728 | tf_op jit(solution)/shard_map/all_to_all | solution.py:217
  176.1 2.0 and_reduce_fusion
  178.1 2.0 slice.2776
  180.2 1.9 copy.225
  184.0 254.5 %all-reduce.49.cloned.1.call-done = (f32[96,2592]{1,0:T(8,128)}, f32[192,768]{1,0:T(8,128)}) async-done(((f32[96,2592]{1,0:T(8,128)}, f32[192,768]{1,0:T(8,128)}), (f32[96,2592]{1,0:T(8,128)}, f32[192,768]{1,0:T(8,128)})) %all-reduce.49.cloned.1.call-update) | async-done | bytes 1585168 | tf_op jit(solution)/shard_map/psum | solution.py:232
  441.0 2.1 multiply_reduce_fusion
  443.8 2.0 broadcast_multiply_fusion.1
  446.8 3.5 convert_element_type.101
  450.3 3.6 gather_fusion.1
  467.1 2.6 scatter-add.91
  474.0 2.8 add_select_fusion.1
  476.8 4.6 scatter-add.95
  482.5 2.6 fusion.25
  486.5 2.2 copy.169
  489.7 3.0 scatter-add.101
  497.1 2.8 add_select_fusion
  499.8 4.8 scatter-add.105
  505.5 2.3 copy.175
  507.7 4.2 slice_add_fusion.1
  511.9 18.6 %scatter-add.106 = f32[96,8,8,16]{3,0,2,1:T(8,128)S(1)} dynamic-update-slice(f32[96,8,8,16]{3,0,2,1:T(8,128)S(1)} %scatter-add.105, f32[96,8,8,1]{3,0,2,1:T(8,128)} %slice_add_fusion.1, s32[]{:T(128)} %constant.1634.clone.1, s32[]{:T(128)} %constant.1634.clone.1, s32[]{:T(128)} %constant.1634.clone.1, s32[]{:T(128)} %constant.1634.clone.1) | dynamic-update-slice | bytes 49156 | tf_op jit(solution)/shard_map/scatter-add | solution.py:230
  530.6 2.2 copy.177
  532.9 4.4 slice_add_fusion
  537.3 23.3 %scatter-add.109 = f32[96,8,8,16]{3,0,2,1:T(8,128)S(1)} dynamic-update-slice(f32[96,8,8,16]{3,0,2,1:T(8,128)S(1)} %scatter-add.106, f32[96,8,8,1]{3,0,2,1:T(8,128)} %slice_add_fusion, s32[]{:T(128)} %constant.1634.clone.1, s32[]{:T(128)} %constant.1634.clone.1, s32[]{:T(128)} %constant.1634.clone.1, s32[]{:T(128)} %constant.1644.clone.1) | dynamic-update-slice | bytes 49156 | tf_op jit(solution)/shard_map/scatter-add | solution.py:230
  563.0 3.0 scatter-add.110
  568.5 2.2 copy.183
  571.9 3.6 scatter-add.114
  582.5 2.6 scatter-add.120
  587.6 2.2 copy.191
  591.0 3.3 scatter-add.124
  599.2 2.0 copy.195
  (339 shorter events, 120.3 us)
Async XLA Ops:
  8.3 1.1 copy-start.39
  16.2 13.4 %copy-start.22 = (bf16[192,768]{1,0:T(8,128)(2,1)S(1)}, bf16[192,768]{1,0:T(8,128)(2,1)}, u32[]{:S(2)}) copy-start(bf16[192,768]{1,0:T(8,128)(2,1)} %param.112) | copy-start | bytes 884740
  16.2 13.6 %copy-start.32 = (bf16[1,1,192,128]{3,2,1,0:T(8,128)(2,1)S(1)}, bf16[1,1,192,128]{3,2,1,0:T(8,128)(2,1)}, u32[]{:S(2)}) copy-start(bf16[1,1,192,128]{3,2,1,0:T(8,128)(2,1)} %param.110) | copy-start | bytes 147460
  16.2 53.1 %all-to-all-start = ((bf16[64,96,128]{2,1,0:T(8,128)(2,1)}), bf16[64,96,128]{2,1,0:T(8,128)(2,1)S(1)}, u32[]{:S(2)}, u32[]{:S(2)}) async-start(bf16[64,96,128]{2,1,0:T(8,128)(2,1)} %scatter_fusion), calls=%async_computation | async-start | bytes 3145728 | tf_op jit(solution)/shard_map/all_to_all | solution.py:187
  29.8 1.8 copy-start.19
  76.8 3.2 copy-start
  78.6 3.2 copy-start.2
  80.4 3.2 copy-start.4
  82.3 3.1 copy-start.6
  89.2 1.8 copy-start.30
  141.8 2.1 copy-start.14
  141.8 2.1 copy-start.18
  143.9 1.3 copy-start.13
  145.2 1.3 copy-start.12
  146.5 1.3 copy-start.11
  147.9 1.3 copy-start.10
  149.2 1.3 copy-start.9
  150.6 1.3 copy-start.8
  153.5 1.1 copy-start.17
  161.6 6.5 %copy-start.7 = (bf16[288,8,8,16]{0,3,2,1:T(8,128)(2,1)S(1)}, bf16[288,8,8,16]{0,3,2,1:T(8,128)(2,1)}, u32[]{:S(2)}) copy-start(bf16[288,8,8,16]{0,3,2,1:T(8,128)(2,1)} %copy-done.6) | copy-start | bytes 1769476
  161.6 7.5 %copy-start.31 = (bf16[96,1024]{1,0:T(8,128)(2,1)S(1)}, bf16[96,1024]{1,0:T(8,128)(2,1)}, u32[]{:S(2)}) copy-start(bf16[96,1024]{1,0:T(8,128)(2,1)} %get-tuple-element.737) | copy-start | bytes 589828
  161.6 285.2 %all-to-all-start.1 = ((bf16[64,96,128]{2,1,0:T(8,128)(2,1)}), bf16[64,96,128]{2,1,0:T(8,128)(2,1)}, u32[]{:S(2)}, u32[]{:S(2)}) async-start(bf16[64,96,128]{2,1,0:T(8,128)(2,1)} %convert_element_type.100), calls=%async_computation.1 | async-start | bytes 3145728 | tf_op jit(solution)/shard_map/all_to_all | solution.py:217
  168.1 1.7 copy-start.5
  168.1 2.7 copy-start.3
  168.1 270.4 %all-reduce.49.cloned.1.call-start = ((), (), s32[]{:S(2)}) async-start(), calls=%async_computation.2 | async-start | bytes 3244032 | tf_op jit(solution)/shard_map/psum | solution.py:232
  169.3 1.8 copy-start.1
  169.8 1.6 copy-start.23
  169.8 1.6 copy-start.24
  169.8 1.6 copy-start.25
  169.8 1.6 copy-start.26
  169.8 1.6 copy-start.27
  170.8 0.9 copy-start.28
  170.8 1.0 copy-start.29
  171.1 2.0 copy-start.33
  173.1 2.3 copy-start.36
  173.1 3.1 copy-start.37
  173.1 3.1 copy-start.38
  443.8 2.0 copy-start.16
  455.4 1.1 copy-start.15
  511.9 18.6 %copy-start.35 = (f32[1,96,64]{2,1,0:T(8,128)S(1)}, f32[1,96,64]{2,1,0:T(8,128)}, u32[]{:S(2)}) copy-start(f32[1,96,64]{2,1,0:T(8,128)} %get-tuple-element.662) | copy-start | bytes 73732
  537.3 23.3 %copy-start.34 = (f32[96,8,1,1]{1,0,3,2:T(8,128)S(1)}, f32[96,8,1,1]{1,0,3,2:T(8,128)}, u32[]{:S(2)}) copy-start(f32[96,8,1,1]{1,0,3,2:T(8,128)} %get-tuple-element.653) | copy-start | bytes 9220
  570.7 1.0 copy-start.20
  589.8 1.0 copy-start.21
Sparse Core Ops, SparseCore 0:
  175.0 263.4 all-reduce.48
where the time goes:
time: 620 us; the launch traced here: 608 us
  waiting for transfers between devices  291 us (47%)
  local copies, waits for them, and re-layouts  178 us (29%)
  other arithmetic  73.2 us (12%)
  matrix products  29.7 us (5%)
  starting transfers between devices  19.7 us (3%)
  between operations  17.5 us (3%)
    psum x1, waiting for transfers between devices, shards(): conv_sum, down_sum = lax.psum((conv_part, down_part), ('dp', 'space'))  254 us
    scatter-add x22, local copies, waits for them, and re-layouts, shards(): inner_part = inner_part.at[:, cut_inner(offset[0], block_side), cut_inner...  75.3 us
    all_to_all x1, waiting for transfers between devices, shards(): lax.all_to_all(sent, 'space', split_axis=0, concat_axis=0, tiled=True)  36.2 us
    another operation x33, local copies, waits for them, and re-layouts  26 us
    concatenate x18, other arithmetic, conv_taps(): jnp.concatenate([padded[:, step_x:step_x + size_x, step_y:step_y + size_y...  24 us
    add x19, other arithmetic, shards(): inner_part = inner_part.at[:, cut_inner(offset[0], block_side), cut_inner...  22.2 us
    dot_general x18, matrix products, conv_taps(): jnp.dot(weight_matrix[:, start_col:start_col + 3 * channels], columns, pr...  19.3 us
    reshape x9, local copies, waits for them, and re-layouts, conv_taps(): columns = jnp.concatenate([padded[:, step_x:step_x + size_x, step_y:step_...  15.8 us
  transfers between devices with their start and end apart: 3, of which 2 were waited for; matrix products, arithmetic and copies ran while one was open for 4% of the time, Pallas kernels for 0%

commit v1 on v0

v1 whole, which is shorter than its diff:
```python
import jax
import jax.numpy as jnp
import numpy as np
from jax import lax
from jax.experimental import pallas as pl
from jax.experimental.pallas import tpu as pltpu
from jax.sharding import Mesh, PartitionSpec as P

C = 96
C2 = 192
SIDE = 8
DEPTH = 16
VOX = 1024
LANES = 128
SLOTS = 1024
COL = 24
HALF_ROWS = 1664
CONV_ROWS = 1008
EPSILON = 1e-06
F32 = jnp.float32
BF16 = jnp.bfloat16
PARAMS = pltpu.CompilerParams(vmem_limit_bytes=56 << 20)


def slot_tables():
    directions = [
        (ex, ey, ez)
        for ex in (-1, 0, 1)
        for ey in (-1, 0, 1)
        for ez in (-1, 0, 1)
        if (ex, ey, ez) != (0, 0, 0)
    ]
    natural = np.full((SLOTS, 1), -1, np.int32)
    parity = np.full((SLOTS, 1), -1, np.int32)
    number = np.full((SLOTS, 1), -1, np.int32)

    def side(position, extent):
        if position == 0:
            return -1, extent - 1
        if position == extent + 1:
            return 1, 0
        return 0, position - 1

    def fill(slot, px, py, pz):
        (ex, x), (ey, y), (ez, z) = side(px, SIDE), side(py, SIDE), side(pz, DEPTH)
        natural[slot] = (x * SIDE + y) * DEPTH + z
        parity[slot] = (x * SIDE + y) * DEPTH + z % 2 * 8 + z // 2
        number[slot] = directions.index((ex, ey, ez))

    rim = [(x, y) for x in range(10) for y in range(10) if x in (0, 9) or y in (0, 9)]
    for place, (x, y) in enumerate(rim):
        for z in range(DEPTH + 2):
            fill(place * COL + z, x, y, z)
    for x in range(SIDE):
        for y in range(SIDE):
            fill(864 + x * 8 + y, x + 1, y + 1, 0)
            fill(928 + x * 8 + y, x + 1, y + 1, DEPTH + 1)
    return natural, parity, number


NATURAL, PARITY, NUMBER = slot_tables()


def one_hot(index, count):
    wide = lax.broadcasted_iota(jnp.int32, (index.shape[0], count), 1)
    return jnp.where(wide == index, 1.0, 0.0).astype(BF16)


def dot(a, b, ca=1, cb=0):
    return lax.dot_general(a, b, (((ca,), (cb,)), ((), ())), preferred_element_type=F32)


def spread_kernel(f_ref, nbr_ref, vox_ref, num_ref, out_ref):
    wide = jnp.concatenate([f_ref[...], jnp.zeros((LANES - C, VOX), BF16)], axis=0)
    for part in range(4):
        rows = pl.ds(part * 256, 256)
        got = dot(one_hot(vox_ref[rows, :], VOX), wide, 1, 1)
        match = lax.broadcasted_iota(jnp.int32, (256, 26), 1) == num_ref[rows, :]
        owner = jnp.sum(
            jnp.where(match, (nbr_ref[...] + 1).astype(F32), 0.0), axis=1, keepdims=True
        ) - 1.0
        lane = lax.broadcasted_iota(jnp.int32, (256, LANES), 1)
        out_ref[rows, :] = jnp.where(lane >= C, owner, got).astype(BF16)


def route_kernel(owner_ref, rows_ref, out_ref):
    for part in range(4):
        rows = pl.ds(part * 256, 256)
        owner = owner_ref[rows, C : C + 1].astype(F32).astype(jnp.int32)
        place = lax.broadcasted_iota(jnp.int32, (256, 1), 0) & 15
        pick = one_hot(owner * 16 + place, SLOTS)
        out_ref[rows, :] = dot(pick, rows_ref[...]).astype(BF16)


def fill_halo(pad_ref, halo_ref):
    def put(first, count, place):
        pad_ref[pl.ds(first * COL, count * COL), :] = halo_ref[
            pl.ds(place * COL, count * COL), :
        ].astype(F32)

    put(0, 11, 0)
    for x in range(1, 8):
        put(x * 10 + 9, 2, 11 + 2 * (x - 1))
    put(89, 11, 25)
    for x in range(SIDE):
        start = ((x + 1) * 10 + 1) * COL
        pad_ref[pl.ds(start, 8, stride=COL), :] = halo_ref[pl.ds(864 + x * 8, 8), :].astype(F32)
        pad_ref[pl.ds(start + DEPTH + 1, 8, stride=COL), :] = halo_ref[
            pl.ds(928 + x * 8, 8), :
        ].astype(F32)


def shifted_columns(pad_ref, cols_ref):
    for x in range(10):
        for y in range(10):
            base = (x * 10 + y) * COL
            rows = [pad_ref[pl.ds(base + s, 8, stride=2), :] for s in range(4)]
            for dz in range(3):
                cols_ref[x, y, :, pl.ds(dz * LANES, LANES)] = jnp.concatenate(
                    [rows[dz], rows[dz + 1]], axis=0
                ).astype(BF16)


def window(cols_ref, dx, dy):
    return cols_ref[dx : dx + 8, dy : dy + 8].reshape(VOX, 3 * LANES)


def conv(cols_ref, w_ref):
    total = None
    for tap in range(9):
        part = dot(window(cols_ref, tap // 3, tap % 3), w_ref[tap])
        total = part if total is None else total + part
    return total


def forward_kernel(
    f_ref, halo_ref, cot_ref, w_ref, dw_ref, vox_ref,
    coarse_ref, grad_ref, cols_ref, patch_ref, send_ref,
    pad_ref, act_ref,
):
    wide = jnp.concatenate([f_ref[...].astype(F32), jnp.zeros((LANES - C, VOX), F32)], axis=0)
    own = wide.T
    for x in range(SIDE):
        for y in range(SIDE):
            pad_ref[pl.ds(((x + 1) * 10 + y + 1) * COL + 1, DEPTH), :] = own[
                (x * 8 + y) * 16 : (x * 8 + y + 1) * 16, :
            ]
    fill_halo(pad_ref, halo_ref)
    shifted_columns(pad_ref, cols_ref)
    act_ref[...] = conv(cols_ref, w_ref)
    back = dot(cot_ref[...], dw_ref[...], 0, 0)
    for j in range(8):
        jx, jy, jz = j // 4, j // 2 % 2, j % 2
        spots = [
            ((2 * ux + jx) * 8 + 2 * uy + jy) * 16 + jz * 8 for ux in range(4) for uy in range(4)
        ]
        a = jnp.concatenate([act_ref[pl.ds(s, 8), :] for s in spots], axis=0)
        g = 1.0 / (1.0 + jnp.exp(-a))
        patch_ref[:, pl.ds(j * LANES, LANES)] = (a * g).astype(BF16)
        slope = g * (1.0 + a * (1.0 - g))
        grad = back[:, j * LANES : (j + 1) * LANES] * slope
        for n, s in enumerate(spots):
            act_ref[pl.ds(s, 8), :] = grad[n * 8 : n * 8 + 8, :]
    grad_ref[...] = act_ref[...].astype(BF16)
    for part in range(4):
        rows = pl.ds(part * 256, 256)
        send_ref[rows, :] = dot(one_hot(vox_ref[rows, :], VOX), grad_ref[...]).astype(BF16)
    coarse_ref[...] = dot(dw_ref[...], patch_ref[...], 1, 1).astype(BF16)


def weight_kernel(core_ref, grad_ref, cols_ref, patch_ref, cot_ref, keep_ref, send_ref, conv_ref, down_ref):
    turned = grad_ref[...].astype(F32).T[:C, :].astype(BF16)
    conv_ref[:, pl.ds(20 * LANES, LANES)] = jnp.zeros((C, LANES), F32)
    for tap in range(9):
        part = dot(turned, window(cols_ref, tap // 3, tap % 3))
        for dz in range(3):
            conv_ref[:, pl.ds((tap * 3 + dz) * C, C)] = part[:, dz * LANES : dz * LANES + C]
    part = dot(cot_ref[...], patch_ref[...])
    for j in range(8):
        down_ref[:, pl.ds(j * C, C)] = part[:, j * LANES : j * LANES + C]
    core = core_ref[0]
    for ref, half in ((keep_ref, core), (send_ref, 1 - core)):
        for lt in range(21):
            ref[pl.ds(lt * 48, 48), :] = conv_ref[
                pl.ds(pl.multiple_of(half * 48, 16), 48), pl.ds(lt * LANES, LANES)
            ].astype(ref.dtype)
        for lt in range(6):
            ref[pl.ds(CONV_ROWS + lt * 96, 96), :] = down_ref[
                pl.ds(pl.multiple_of(half * 96, 32), 96), pl.ds(lt * LANES, LANES)
            ].astype(ref.dtype)
        ref[pl.ds(1584, HALF_ROWS - 1584), :] = jnp.zeros((HALF_ROWS - 1584, LANES), ref.dtype)


def backward_kernel(grad_ref, halo_ref, w_ref, out_ref, pad_ref, cols_ref, act_ref):
    for x in range(SIDE):
        for y in range(SIDE):
            base = ((x + 1) * 10 + y + 1) * COL
            for par in range(2):
                pad_ref[pl.ds(base + 1 + par, 8, stride=2), :] = grad_ref[
                    pl.ds((x * 8 + y) * 16 + par * 8, 8), :
                ].astype(F32)
    fill_halo(pad_ref, halo_ref)
    shifted_columns(pad_ref, cols_ref)
    full = conv(cols_ref, w_ref)
    for n in range(64):
        for par in range(2):
            act_ref[pl.ds(n * 16 + par, 8, stride=2), :] = full[n * 16 + par * 8 : n * 16 + par * 8 + 8, :]
    out_ref[...] = act_ref[...].T[:C, :]


def finish_kernel(core_ref, mine_ref, other_ref, conv_ref, down_ref):
    def scale(first, last, count):
        total = jnp.zeros((8, LANES), F32)
        for ref in (mine_ref, other_ref):
            values = ref[pl.ds(first, last - first), :].astype(F32)
            total = total + jnp.sum((values * values).reshape(-1, 8, LANES), axis=0)
        return lax.rsqrt(jnp.sum(total, keepdims=True) * (1.0 / count) + EPSILON)

    conv_scale = scale(0, CONV_ROWS, C * 27 * C)
    down_scale = scale(CONV_ROWS, 1584, C2 * 8 * C)
    core = core_ref[0]
    for ref, half in ((mine_ref, core), (other_ref, 1 - core)):
        for lt in range(21):
            width = min(LANES, 27 * C - lt * LANES)
            values = ref[pl.ds(lt * 48, 48), :].astype(F32) * conv_scale
            conv_ref[pl.ds(pl.multiple_of(half * 48, 16), 48), pl.ds(lt * LANES, width)] = values[:, :width]
        for lt in range(6):
            values = ref[pl.ds(CONV_ROWS + lt * 96, 96), :].astype(F32) * down_scale
            down_ref[pl.ds(pl.multiple_of(half * 96, 32), 96), pl.ds(lt * LANES, LANES)] = values


def call(body, outs, scratch=(), scalars=0, ins=0, name=None):
    specs = [pl.BlockSpec(memory_space=pltpu.SMEM)] * scalars + [
        pl.BlockSpec(memory_space=pltpu.VMEM)
    ] * ins
    return pl.pallas_call(
        body,
        out_shape=[jax.ShapeDtypeStruct(shape, kind) for shape, kind in outs],
        in_specs=specs,
        out_specs=[pl.BlockSpec(memory_space=pltpu.VMEM)] * len(outs),
        scratch_shapes=list(scratch),
        compiler_params=PARAMS,
        name=name,
    )


SPACE = ("y", "z", "c")
PLANE = ("x", "y")


def trade(rows, axes, count):
    moved = lax.all_to_all(rows.reshape(count, -1, LANES), axes, 0, 0, tiled=True)
    return moved.reshape(-1, LANES)


def shards(features, cotangent, conv_weight, down_weight, neighbours):
    block = features[0, 0]
    cot = cotangent[0, 0]
    row = neighbours[0]
    core = lax.axis_index("c").astype(jnp.int32).reshape(1)
    other = [(0, 1), (1, 0)]
    rows_shape = ((SLOTS, LANES), BF16)
    natural, parity, number = jnp.asarray(NATURAL), jnp.asarray(PARITY), jnp.asarray(NUMBER)

    (spread,) = call(spread_kernel, [rows_shape], ins=4, name="spread")(block, row, natural, number)
    middle = trade(spread, SPACE, 64)
    route = call(route_kernel, [rows_shape], ins=2, name="route")
    (routed,) = route(middle, middle)
    halo = trade(routed, SPACE, 64)

    taps = conv_weight.reshape(C, 27, C)
    pad = ((0, 0), (0, LANES - C), (0, LANES - C))
    forward_w = jnp.pad(taps.transpose(1, 2, 0), pad).reshape(9, 3 * LANES, LANES)
    backward_w = jnp.pad(taps.transpose(1, 0, 2)[::-1], pad).reshape(9, 3 * LANES, LANES)
    down_w = jnp.pad(down_weight.reshape(C2, 8, C), ((0, 0), (0, 0), (0, LANES - C))).reshape(C2, 8 * LANES)

    pad_scratch = pltpu.VMEM((100 * COL, LANES), F32)
    act_scratch = pltpu.VMEM((VOX, LANES), F32)
    cols_shape = ((10, 10, DEPTH, 3 * LANES), BF16)
    coarse, grad, cols, patch, spread2 = call(
        forward_kernel,
        [((C2, LANES), BF16), rows_shape, cols_shape, ((LANES, 8 * LANES), BF16), rows_shape],
        [pad_scratch, act_scratch],
        ins=6,
        name="forward",
    )(block, halo, cot, forward_w, down_w, parity)

    keep, send = call(
        weight_kernel,
        [((HALF_ROWS, LANES), F32), ((HALF_ROWS, LANES), BF16)],
        [pltpu.VMEM((C, 21 * LANES), F32), pltpu.VMEM((C2, 8 * C), F32)],
        scalars=1,
        ins=4,
        name="weight_grad",
    )(core, grad, cols, patch, cot)
    got = lax.ppermute(send, "c", other)
    pair = (keep + got.astype(F32)).astype(BF16)
    plane = trade(pair, PLANE, 16).reshape(16, 104, LANES)
    part = jnp.sum(plane.astype(F32), axis=0).astype(BF16)
    line = trade(jnp.broadcast_to(part, (8, 104, LANES)), "z", 8).reshape(8, 104, LANES)
    whole = jnp.sum(line.astype(F32), axis=0).astype(BF16)
    mine = trade(jnp.broadcast_to(whole, (16, 104, LANES)), PLANE, 16)
    theirs = lax.ppermute(mine, "c", other)

    middle2 = trade(spread2, SPACE, 64)
    (routed2,) = route(middle, middle2)
    halo2 = trade(routed2, SPACE, 64)
    (grad_features,) = call(
        backward_kernel,
        [((C, VOX), F32)],
        [pad_scratch, pltpu.VMEM(*cols_shape), act_scratch],
        ins=3,
        name="backward",
    )(grad, halo2, backward_w)

    grad_conv, grad_down = call(
        finish_kernel, [((C, 27 * C), F32), ((C2, 8 * C), F32)], scalars=1, ins=2, name="finish"
    )(core, mine, theirs)
    return coarse[None, None], grad_features[None, None], grad_conv, grad_down


def solution(mesh):
    devices = mesh.devices
    fine = Mesh(devices.reshape(devices.shape[0], 4, -1, 2), ("x", "y", "z", "c"))
    block = P("x", SPACE, None, None)
    return jax.shard_map(
        shards,
        mesh=fine,
        in_specs=(block, block, P(), P(), P("x", SPACE, None)),
        out_specs=(block, block, P(), P()),
        check_vma=False,
    )
```

time: 620 us -> 151 us (0.24); the launches traced: 608 us -> 151 us
  waiting for transfers between devices: 291 us -> 39.7 us
  local copies, waits for them, and re-layouts: 178 us -> 7.41 us
  other arithmetic: 73.2 us -> 1.36 us
  blocking collectives: 0 us -> 52.2 us
  matrix products: 29.7 us -> 0 us
  Pallas kernels: 0 us -> 24.4 us
  between operations: 17.5 us -> 0.74 us
    psum x1 -> x0, waiting for transfers between devices: 254 us -> none  [shards(): conv_sum, down_sum = lax.psum((conv_part, down_part), ('dp', 'space'))]
    scatter-add x22 -> x0, local copies, waits for them, and re-layouts: 75.3 us -> none  [shards(): inner_part = inner_part.at[:, cut_inner(offset[0], block_side), cut_inner...]
    all_to_all x0 -> x3, blocking collectives: none -> 52.2 us  [trade(): lax.all_to_all(rows.reshape(count, -1, LANES), axes, 0, 0, tiled=True)]
    dot_general x30 -> x0, matrix products: 29.7 us -> none  [the longest x18 19.3 us: conv_taps(): jnp.dot(weight_matrix[:, start_col:start_col + 3 * channels], columns, pr...]
    another operation x37 -> x0, local copies, waits for them, and re-layouts: 28 us -> none
    pallas_call x0 -> x7, Pallas kernels: none -> 24.4 us  [the longest x1 5.39 us: shards(): call(forward_kernel, [((C2, LANES), BF16), rows_shape, cols_shape, ((LANE...]
    concatenate x18 -> x0, other arithmetic: 24 us -> none  [conv_taps(): jnp.concatenate([padded[:, step_x:step_x + size_x, step_y:step_y + size_y...]
    add x19 -> x0, other arithmetic: 22.2 us -> none  [shards(): inner_part = inner_part.at[:, cut_inner(offset[0], block_side), cut_inner...]
  transfers between devices with their start and end apart: 3 -> 6, of which waited for: 2 -> 5; matrix products, arithmetic and copies ran while one was open for 4% -> 3% of each run, Pallas kernels for 0% -> 5%
where the time goes in v1:
time: 151 us
  blocking collectives  52.2 us (35%)
  waiting for transfers between devices  39.7 us (26%)
  starting transfers between devices  24.9 us (16%)
  Pallas kernels  24.4 us (16%)
  local copies, waits for them, and re-layouts  7.41 us (5%)
    all_to_all x3, blocking collectives, trade(): lax.all_to_all(rows.reshape(count, -1, LANES), axes, 0, 0, tiled=True)  52.2 us
    all_to_all x4, waiting for transfers between devices, trade(): lax.all_to_all(rows.reshape(count, -1, LANES), axes, 0, 0, tiled=True)  38 us
    all_to_all x4, starting transfers between devices, trade(): lax.all_to_all(rows.reshape(count, -1, LANES), axes, 0, 0, tiled=True)  23.9 us
    pallas_call x1, Pallas kernels, shards(): call(forward_kernel, [((C2, LANES), BF16), rows_shape, cols_shape, ((LANE...  5.39 us
    pallas_call x1, Pallas kernels, shards(): call(backward_kernel, [((C, VOX), F32)], [pad_scratch, pltpu.VMEM(*cols_s...  4.25 us
    pallas_call x1, Pallas kernels, shards(): call(weight_kernel, [((HALF_ROWS, LANES), F32), ((HALF_ROWS, LANES), BF16...  4.07 us
    unnamed x17, local copies, waits for them, and re-layouts  3.68 us
  transfers between devices with their start and end apart: 6, of which 5 were waited for; matrix products, arithmetic and copies ran while one was open for 3% of the time, Pallas kernels for 5%

profile of v1, /device:TPU:1, one launch (start us, length us, event | category | flops | bytes accessed | tf_op | source)
XLA Modules:
  0.0 150.7 jit_solution(1754580045651873392)
XLA Ops:
  0.6 2.9 %spread.1 = bf16[1024,128]{1,0:T(8,128)(2,1)} custom-call(bf16[96,1024]{1,0:T(8,128)(2,1)} %bitcast.45, s32[1,26]{1,0:T(1,128)} %bitcast.50, s32[1024,1]{1,0:T(8,128)} %constant.16.clone.vox_ref, s32[1024,1]{1,0:T(8,128)} %constant.18.clone.num_ref), custom_call_target="tpu_custom_call" | custom-call | tf_op jit(solution)/shard_map/spread/pallas_call | solution.py:265
  3.6 0.0 copy-start.4
  3.6 25.4 %all_to_all.35 = bf16[64,16,128]{2,1,0:T(8,128)(2,1)} all-to-all(bf16[64,16,128]{2,1,0:T(8,128)(2,1)} %bitcast.44), channel_id=1, replica_groups=mesh['x'=4,'y'=4,'z'=8,'c'=2] {'y','z','c'}, dimensions={0} | all-to-all | bytes 524288 | tf_op jit(solution)/shard_map/all_to_all | solution.py:252
  29.0 0.0 copy-start.6
  29.0 2.6 %route.2 = bf16[1024,128]{1,0:T(8,128)(2,1)} custom-call(bf16[1024,128]{1,0:T(8,128)(2,1)} %bitcast.29, bf16[1024,128]{1,0:T(8,128)(2,1)} %bitcast.30), custom_call_target="tpu_custom_call" | custom-call | tf_op jit(solution)/shard_map/route/pallas_call | solution.py:268
  31.5 6.0 %all-to-all-start.1 = ((bf16[64,16,128]{2,1,0:T(8,128)(2,1)}), bf16[64,16,128]{2,1,0:T(8,128)(2,1)S(1)}, u32[]{:S(2)}, u32[]{:S(2)}) async-start(bf16[64,16,128]{2,1,0:T(8,128)(2,1)} %bitcast.43), calls=%async_computation.1 | async-start | bytes 524288 | tf_op jit(solution)/shard_map/all_to_all | solution.py:252
  37.6 0.0 copy-done.4
  37.6 0.3 copy.16
  37.9 0.0 copy-done.6
  37.9 0.4 reshape.62
  38.4 1.1 pad.11
  39.5 0.1 pad.12
  39.6 0.8 copy.21
  40.4 9.1 %all-to-all-done.1 = bf16[64,16,128]{2,1,0:T(8,128)(2,1)S(1)} async-done(((bf16[64,16,128]{2,1,0:T(8,128)(2,1)}), bf16[64,16,128]{2,1,0:T(8,128)(2,1)S(1)}, u32[]{:S(2)}, u32[]{:S(2)}) %all-to-all-start.1) | async-done | bytes 262176 | tf_op jit(solution)/shard_map/all_to_all | solution.py:252
  49.6 0.0 copy-start.1
  49.6 0.7 copy-done.1
  50.3 5.4 %forward.1 = (bf16[192,128]{1,0:T(8,128)(2,1)}, bf16[1024,128]{1,0:T(8,128)(2,1)}, bf16[10,10,16,384]{3,2,1,0:T(8,128)(2,1)}, bf16[128,1024]{1,0:T(8,128)(2,1)}, bf16[1024,128]{1,0:T(8,128)(2,1)}) custom-call(bf16[96,1024]{1,0:T(8,128)(2,1)} %bitcast.46, bf16[1024,128]{1,0:T(8,128)(2,1)} %bitcast.39, bf16[192,128]{1,0:T(8,128)(2,1)} %bitcast.48, ...), custom_call_target="tpu_custom_call" | custom-call | tf_op jit(solution)/shard_map/forward/pallas_call | solution.py:280
  55.7 4.1 %weight_grad.1 = (f32[1664,128]{1,0:T(8,128)}, bf16[1664,128]{1,0:T(8,128)(2,1)}) custom-call(s32[1]{0:T(128)} %bitcast.18.core_ref, bf16[1024,128]{1,0:T(8,128)(2,1)} %get-tuple-element.14.grad_ref, bf16[10,10,16,384]{3,2,1,0:T(8,128)(2,1)} %get-tuple-element.16.cols_ref, bf16[128,1024]{1,0:T(8,128)(2,1)} %get-tuple-element.17.patch_ref, ...), custom_call_target="tpu_custom_call" | custom-call | tf_op jit(solution)/shard_map/weight_grad/pallas_call | solution.py:288
  59.7 0.4 collective-permute-start
  60.2 1.6 %collective-permute-done = bf16[1664,128]{1,0:T(8,128)(2,1)S(1)} collective-permute-done((bf16[1664,128]{1,0:T(8,128)(2,1)}, bf16[1664,128]{1,0:T(8,128)(2,1)S(1)}, u32[]{:S(2)}, u32[]{:S(2)}) %collective-permute-start) | collective-permute-done | bytes 426016 | tf_op jit(solution)/shard_map/ppermute | solution.py:296
  61.8 1.3 add_convert_fusion
  63.0 15.7 %all_to_all.36 = bf16[16,104,128]{2,1,0:T(8,128)(2,1)S(1)} all-to-all(bf16[16,104,128]{2,1,0:T(8,128)(2,1)S(1)} %bitcast.36), channel_id=1, replica_groups=mesh['x'=4,'y'=4,'z'=8,'c'=2] {'x','y'}, dimensions={0} | all-to-all | bytes 851968 | tf_op jit(solution)/shard_map/all_to_all | solution.py:252
  78.7 0.1 reduce_sum.24
  78.8 11.1 %all_to_all.37 = bf16[8,104,128]{2,1,0:T(8,128)(2,1)S(1)} all-to-all(bf16[8,104,128]{2,1,0:T(8,128)(2,1)S(1)} %broadcast_in_dim.14), channel_id=1, replica_groups=mesh['x'=4,'y'=4,'z'=8,'c'=2] {'z'}, dimensions={0} | all-to-all | bytes 425984 | tf_op jit(solution)/shard_map/all_to_all | solution.py:252
  90.0 7.1 %all-to-all-start.2 = ((bf16[64,16,128]{2,1,0:T(8,128)(2,1)}), bf16[64,16,128]{2,1,0:T(8,128)(2,1)S(1)}, u32[]{:S(2)}, u32[]{:S(2)}) async-start(bf16[64,16,128]{2,1,0:T(8,128)(2,1)} %bitcast.11), calls=%async_computation.2 | async-start | bytes 524288 | tf_op jit(solution)/shard_map/all_to_all | solution.py:252
  97.1 12.0 %all-to-all-done.2 = bf16[64,16,128]{2,1,0:T(8,128)(2,1)S(1)} async-done(((bf16[64,16,128]{2,1,0:T(8,128)(2,1)}), bf16[64,16,128]{2,1,0:T(8,128)(2,1)S(1)}, u32[]{:S(2)}, u32[]{:S(2)}) %all-to-all-start.2) | async-done | bytes 262176 | tf_op jit(solution)/shard_map/all_to_all | solution.py:252
  109.1 0.0 copy-start.3
  109.1 0.8 broadcast_in_dim.15
  110.0 4.8 %all-to-all-start.6 = ((bf16[16,104,128]{2,1,0:T(8,128)(2,1)}), bf16[16,104,128]{2,1,0:T(8,128)(2,1)S(1)}, u32[]{:S(2)}, u32[]{:S(2)}) async-start(bf16[16,104,128]{2,1,0:T(8,128)(2,1)} %broadcast_in_dim.15), calls=%async_computation.6 | async-start | bytes 851968 | tf_op jit(solution)/shard_map/all_to_all | solution.py:252
  114.7 0.0 copy-done.3
  114.8 2.5 %route.3 = bf16[1024,128]{1,0:T(8,128)(2,1)} custom-call(bf16[1024,128]{1,0:T(8,128)(2,1)} %bitcast.31, bf16[1024,128]{1,0:T(8,128)(2,1)} %bitcast.42), custom_call_target="tpu_custom_call" | custom-call | tf_op jit(solution)/shard_map/route/pallas_call | solution.py:306
  117.3 7.0 %all-to-all-done.6 = bf16[16,104,128]{2,1,0:T(8,128)(2,1)S(1)} async-done(((bf16[16,104,128]{2,1,0:T(8,128)(2,1)}), bf16[16,104,128]{2,1,0:T(8,128)(2,1)S(1)}, u32[]{:S(2)}, u32[]{:S(2)}) %all-to-all-start.6) | async-done | bytes 426016 | tf_op jit(solution)/shard_map/all_to_all | solution.py:252
  124.3 0.0 copy-start
  124.3 6.0 %all-to-all-start.3 = ((bf16[64,16,128]{2,1,0:T(8,128)(2,1)}), bf16[64,16,128]{2,1,0:T(8,128)(2,1)S(1)}, u32[]{:S(2)}, u32[]{:S(2)}) async-start(bf16[64,16,128]{2,1,0:T(8,128)(2,1)} %bitcast.40), calls=%async_computation.3 | async-start | bytes 524288 | tf_op jit(solution)/shard_map/all_to_all | solution.py:252
  130.3 0.5 collective-permute-start.1
  130.9 0.3 copy.18
  131.2 0.0 copy-done
  131.2 1.1 pad.13.clone
  132.4 9.9 %all-to-all-done.3 = bf16[64,16,128]{2,1,0:T(8,128)(2,1)S(1)} async-done(((bf16[64,16,128]{2,1,0:T(8,128)(2,1)}), bf16[64,16,128]{2,1,0:T(8,128)(2,1)S(1)}, u32[]{:S(2)}, u32[]{:S(2)}) %all-to-all-start.3) | async-done | bytes 262176 | tf_op jit(solution)/shard_map/all_to_all | solution.py:252
  142.3 0.0 copy-start.2
  142.3 0.7 copy-done.2
  143.0 4.3 %backward.1 = f32[96,1024]{1,0:T(8,128)} custom-call(bf16[1024,128]{1,0:T(8,128)(2,1)} %get-tuple-element.14.grad_ref, bf16[1024,128]{1,0:T(8,128)(2,1)} %bitcast.41, bf16[9,384,128]{2,1,0:T(8,128)(2,1)} %bitcast.33), custom_call_target="tpu_custom_call" | custom-call | tf_op jit(solution)/shard_map/backward/pallas_call | solution.py:308
  147.2 0.0 collective-permute-done.1.other_ref
  147.2 0.0 copy-start.5
  147.2 0.8 copy-done.5
  148.0 2.7 %finish.1 = (f32[96,2592]{1,0:T(8,128)}, f32[192,768]{1,0:T(8,128)}) custom-call(s32[1]{0:T(128)} %bitcast.18.core_ref, bf16[1664,128]{1,0:T(8,128)(2,1)} %bitcast.35, bf16[1664,128]{1,0:T(8,128)(2,1)} %copy-done.5), custom_call_target="tpu_custom_call" | custom-call | tf_op jit(solution)/shard_map/finish/pallas_call | solution.py:316
  (3 shorter events, 0.1 us)
Async XLA Ops:
  3.6 34.0 %copy-start.4 = (bf16[96,2592]{1,0:T(8,128)(2,1)S(1)}, bf16[96,2592]{1,0:T(8,128)(2,1)}, u32[]{:S(2)}) copy-start(bf16[96,2592]{1,0:T(8,128)(2,1)} %param.10) | copy-start | bytes 1492996
  29.0 9.0 %copy-start.6 = (bf16[192,768]{1,0:T(8,128)(2,1)S(1)}, bf16[192,768]{1,0:T(8,128)(2,1)}, u32[]{:S(2)}) copy-start(bf16[192,768]{1,0:T(8,128)(2,1)} %param.11) | copy-start | bytes 884740
  31.5 18.0 %all-to-all-start.1 = ((bf16[64,16,128]{2,1,0:T(8,128)(2,1)}), bf16[64,16,128]{2,1,0:T(8,128)(2,1)S(1)}, u32[]{:S(2)}, u32[]{:S(2)}) async-start(bf16[64,16,128]{2,1,0:T(8,128)(2,1)} %bitcast.43), calls=%async_computation.1 | async-start | bytes 524288 | tf_op jit(solution)/shard_map/all_to_all | solution.py:252
  49.6 0.7 copy-start.1
  59.7 2.1 %collective-permute-start = (bf16[1664,128]{1,0:T(8,128)(2,1)}, bf16[1664,128]{1,0:T(8,128)(2,1)S(1)}, u32[]{:S(2)}, u32[]{:S(2)}) collective-permute-start(bf16[1664,128]{1,0:T(8,128)(2,1)} %get-tuple-element.19), channel_id=1, source_target_pairs={{0,1},{1,0},{2,3},{3,2},{4,5},{5,4},{6,7},{7,6},{8,9},{9,8},{10,11... | collective-permute-start | bytes 1277960 | tf_op jit(solution)/shard_map/ppermute | solution.py:296
  90.0 19.2 %all-to-all-start.2 = ((bf16[64,16,128]{2,1,0:T(8,128)(2,1)}), bf16[64,16,128]{2,1,0:T(8,128)(2,1)S(1)}, u32[]{:S(2)}, u32[]{:S(2)}) async-start(bf16[64,16,128]{2,1,0:T(8,128)(2,1)} %bitcast.11), calls=%async_computation.2 | async-start | bytes 524288 | tf_op jit(solution)/shard_map/all_to_all | solution.py:252
  109.1 5.6 %copy-start.3 = (bf16[64,16,128]{2,1,0:T(8,128)(2,1)}, bf16[64,16,128]{2,1,0:T(8,128)(2,1)S(1)}, u32[]{:S(2)}) copy-start(bf16[64,16,128]{2,1,0:T(8,128)(2,1)S(1)} %all-to-all-done.2) | copy-start | bytes 786436
  110.0 14.3 %all-to-all-start.6 = ((bf16[16,104,128]{2,1,0:T(8,128)(2,1)}), bf16[16,104,128]{2,1,0:T(8,128)(2,1)S(1)}, u32[]{:S(2)}, u32[]{:S(2)}) async-start(bf16[16,104,128]{2,1,0:T(8,128)(2,1)} %broadcast_in_dim.15), calls=%async_computation.6 | async-start | bytes 851968 | tf_op jit(solution)/shard_map/all_to_all | solution.py:252
  124.3 6.9 %copy-start = (bf16[16,104,128]{2,1,0:T(8,128)(2,1)}, bf16[16,104,128]{2,1,0:T(8,128)(2,1)S(1)}, u32[]{:S(2)}) copy-start(bf16[16,104,128]{2,1,0:T(8,128)(2,1)S(1)} %all-to-all-done.6) | copy-start | bytes 1277956
  124.3 18.0 %all-to-all-start.3 = ((bf16[64,16,128]{2,1,0:T(8,128)(2,1)}), bf16[64,16,128]{2,1,0:T(8,128)(2,1)S(1)}, u32[]{:S(2)}, u32[]{:S(2)}) async-start(bf16[64,16,128]{2,1,0:T(8,128)(2,1)} %bitcast.40), calls=%async_computation.3 | async-start | bytes 524288 | tf_op jit(solution)/shard_map/all_to_all | solution.py:252
  130.3 17.0 %collective-permute-start.1 = (bf16[1664,128]{1,0:T(8,128)(2,1)S(1)}, bf16[1664,128]{1,0:T(8,128)(2,1)S(1)}, u32[]{:S(2)}, u32[]{:S(2)}) collective-permute-start(bf16[1664,128]{1,0:T(8,128)(2,1)S(1)} %bitcast.34), channel_id=1, source_target_pairs={{0,1},{1,0},{2,3},{3,2},{4,5},{5,4},{6,7},{7,6},{8,9},{9,8},{10,11... | collective-permute-start | bytes 1277960 | tf_op jit(solution)/shard_map/ppermute | solution.py:303
  142.3 0.7 copy-start.2
  147.2 0.8 copy-start.5

commit v2 on v1

--- a/solution.py
+++ b/solution.py
@@ -1,6 +1,5 @@
 import jax
 import jax.numpy as jnp
-import numpy as np
 from jax import lax
 from jax.experimental import pallas as pl
 from jax.experimental.pallas import tpu as pltpu
@@ -14,7 +13,7 @@
 LANES = 128
 SLOTS = 1024
 COL = 24
-HALF_ROWS = 1664
+HALF_ROWS = 1792
 CONV_ROWS = 1008
 EPSILON = 1e-06
 F32 = jnp.float32
@@ -22,43 +21,20 @@
 PARAMS = pltpu.CompilerParams(vmem_limit_bytes=56 << 20)
 
 
-def slot_tables():
-    directions = [
-        (ex, ey, ez)
-        for ex in (-1, 0, 1)
-        for ey in (-1, 0, 1)
-        for ez in (-1, 0, 1)
-        if (ex, ey, ez) != (0, 0, 0)
-    ]
-    natural = np.full((SLOTS, 1), -1, np.int32)
-    parity = np.full((SLOTS, 1), -1, np.int32)
-    number = np.full((SLOTS, 1), -1, np.int32)
-
-    def side(position, extent):
-        if position == 0:
-            return -1, extent - 1
-        if position == extent + 1:
-            return 1, 0
-        return 0, position - 1
-
-    def fill(slot, px, py, pz):
-        (ex, x), (ey, y), (ez, z) = side(px, SIDE), side(py, SIDE), side(pz, DEPTH)
-        natural[slot] = (x * SIDE + y) * DEPTH + z
-        parity[slot] = (x * SIDE + y) * DEPTH + z % 2 * 8 + z // 2
-        number[slot] = directions.index((ex, ey, ez))
-
-    rim = [(x, y) for x in range(10) for y in range(10) if x in (0, 9) or y in (0, 9)]
-    for place, (x, y) in enumerate(rim):
-        for z in range(DEPTH + 2):
-            fill(place * COL + z, x, y, z)
-    for x in range(SIDE):
-        for y in range(SIDE):
-            fill(864 + x * 8 + y, x + 1, y + 1, 0)
-            fill(928 + x * 8 + y, x + 1, y + 1, DEPTH + 1)
-    return natural, parity, number
-
-
-NATURAL, PARITY, NUMBER = slot_tables()
+RIM = [(x, y) for x in range(10) for y in range(10) if x in (0, 9) or y in (0, 9)]
+
+
+def side(position, extent):
+    if position == 0:
+        return -1, extent - 1
+    if position == extent + 1:
+        return 1, 0
+    return 0, position - 1
+
+
+def direction(ex, ey, ez):
+    place = ((ex + 1) * 3 + ey + 1) * 3 + ez + 1
+    return place - (place > 13)
 
 
 def one_hot(index, count):
@@ -70,26 +46,63 @@
     return lax.dot_general(a, b, (((ca,), (cb,)), ((), ())), preferred_element_type=F32)
 
 
-def spread_kernel(f_ref, nbr_ref, vox_ref, num_ref, out_ref):
-    wide = jnp.concatenate([f_ref[...], jnp.zeros((LANES - C, VOX), BF16)], axis=0)
-    for part in range(4):
-        rows = pl.ds(part * 256, 256)
-        got = dot(one_hot(vox_ref[rows, :], VOX), wide, 1, 1)
-        match = lax.broadcasted_iota(jnp.int32, (256, 26), 1) == num_ref[rows, :]
-        owner = jnp.sum(
-            jnp.where(match, (nbr_ref[...] + 1).astype(F32), 0.0), axis=1, keepdims=True
-        ) - 1.0
-        lane = lax.broadcasted_iota(jnp.int32, (256, LANES), 1)
-        out_ref[rows, :] = jnp.where(lane >= C, owner, got).astype(BF16)
-
-
-def route_kernel(owner_ref, rows_ref, out_ref):
-    for part in range(4):
-        rows = pl.ds(part * 256, 256)
-        owner = owner_ref[rows, C : C + 1].astype(F32).astype(jnp.int32)
-        place = lax.broadcasted_iota(jnp.int32, (256, 1), 0) & 15
-        pick = one_hot(owner * 16 + place, SLOTS)
-        out_ref[rows, :] = dot(pick, rows_ref[...]).astype(BF16)
+def spread_rows(src_ref, out_ref, parity):
+    for place, (px, py) in enumerate(RIM):
+        base = (side(px, SIDE)[1] * SIDE + side(py, SIDE)[1]) * DEPTH
+        first = place * COL
+        if parity:
+            for par in range(2):
+                out_ref[pl.ds(first + 1 + par, 8, stride=2), :] = src_ref[pl.ds(base + par * 8, 8), :]
+        else:
+            out_ref[pl.ds(first + 1, DEPTH), :] = src_ref[pl.ds(base, DEPTH), :]
+        out_ref[pl.ds(first, 1), :] = src_ref[pl.ds(base + 15, 1), :]
+        out_ref[pl.ds(first + 17, 1), :] = src_ref[pl.ds(base, 1), :]
+        out_ref[pl.ds(first + 18, 6), :] = jnp.zeros((6, LANES), F32)
+    for x in range(SIDE):
+        out_ref[pl.ds(864 + x * 8, 8), :] = src_ref[pl.ds(x * 128 + 15, 8, stride=DEPTH), :]
+        out_ref[pl.ds(928 + x * 8, 8), :] = src_ref[pl.ds(x * 128, 8, stride=DEPTH), :]
+    out_ref[pl.ds(992, 32), :] = jnp.zeros((32, LANES), F32)
+
+
+def spread_kernel(nbr_ref, f_ref, out_ref, src_ref, row_ref):
+    wide = jnp.concatenate([f_ref[...].astype(F32), jnp.zeros((LANES - C, VOX), F32)], axis=0)
+    src_ref[...] = wide.T
+    spread_rows(src_ref, row_ref, False)
+
+    def owner(ex, ey, ez):
+        return nbr_ref[0, direction(ex, ey, ez)].astype(F32)
+
+    lane = lax.broadcasted_iota(jnp.int32, (COL, LANES), 1)
+    z = lax.broadcasted_iota(jnp.int32, (COL, LANES), 0)
+    for place, (px, py) in enumerate(RIM):
+        ex, ey = side(px, SIDE)[0], side(py, SIDE)[0]
+        low, mid, high = (owner(ex, ey, ez) for ez in (-1, 0, 1))
+        held = jnp.where(z == 0, low, jnp.where(z < 17, mid, jnp.where(z == 17, high, -1.0)))
+        rows = pl.ds(place * COL, COL)
+        row_ref[rows, :] = jnp.where(lane >= C, held, row_ref[rows, :])
+    lane = lax.broadcasted_iota(jnp.int32, (64, LANES), 1)
+    for first, ez in ((864, -1), (928, 1)):
+        rows = pl.ds(first, 64)
+        row_ref[rows, :] = jnp.where(lane >= C, owner(0, 0, ez), row_ref[rows, :])
+    out_ref[...] = row_ref[...].astype(BF16)
+
+
+def route_kernel(core_ref, owner_ref, mine_ref, other_ref, out_ref, row_ref):
+    core = core_ref[0]
+    for group in range(4):
+        slots = slice(group * 8, group * 8 + 8)
+
+        def pick(ref):
+            return ref[...].astype(F32)[:, slots].reshape(256, LANES)
+
+        owner = pick(owner_ref)[:, C : C + 1].astype(jnp.int32)
+        place = lax.broadcasted_iota(jnp.int32, (256, 1), 0) & 7
+        held = jnp.bitwise_and(owner, 1)
+        spot = lax.shift_right_arithmetic(owner, 1) * 8 + place + jnp.where(held == core, 0, 256)
+        spot = jnp.where(owner < 0, -1, spot)
+        source = jnp.concatenate([pick(mine_ref), pick(other_ref)], axis=0).astype(BF16)
+        row_ref[:, slots] = dot(one_hot(spot, 512), source).reshape(32, 8, LANES)
+    out_ref[...] = row_ref[...].astype(BF16)
 
 
 def fill_halo(pad_ref, halo_ref):
@@ -134,9 +147,9 @@
 
 
 def forward_kernel(
-    f_ref, halo_ref, cot_ref, w_ref, dw_ref, vox_ref,
-    coarse_ref, grad_ref, cols_ref, patch_ref, send_ref,
-    pad_ref, act_ref,
+    core_ref, f_ref, halo_ref, cot_ref, w_ref, dw_ref,
+    grad_ref, patch_ref, keep_ref, send_ref,
+    pad_ref, cols_ref, act_ref, conv_ref, down_ref,
 ):
     wide = jnp.concatenate([f_ref[...].astype(F32), jnp.zeros((LANES - C, VOX), F32)], axis=0)
     own = wide.T
@@ -162,14 +175,8 @@
         for n, s in enumerate(spots):
             act_ref[pl.ds(s, 8), :] = grad[n * 8 : n * 8 + 8, :]
     grad_ref[...] = act_ref[...].astype(BF16)
-    for part in range(4):
-        rows = pl.ds(part * 256, 256)
-        send_ref[rows, :] = dot(one_hot(vox_ref[rows, :], VOX), grad_ref[...]).astype(BF16)
-    coarse_ref[...] = dot(dw_ref[...], patch_ref[...], 1, 1).astype(BF16)
-
-
-def weight_kernel(core_ref, grad_ref, cols_ref, patch_ref, cot_ref, keep_ref, send_ref, conv_ref, down_ref):
-    turned = grad_ref[...].astype(F32).T[:C, :].astype(BF16)
+
+    turned = act_ref[...].T[:C, :].astype(BF16)
     conv_ref[:, pl.ds(20 * LANES, LANES)] = jnp.zeros((C, LANES), F32)
     for tap in range(9):
         part = dot(turned, window(cols_ref, tap // 3, tap % 3))
@@ -191,6 +198,13 @@
         ref[pl.ds(1584, HALF_ROWS - 1584), :] = jnp.zeros((HALF_ROWS - 1584, LANES), ref.dtype)
 
 
+def side_kernel(grad_ref, patch_ref, dw_ref, send_ref, coarse_ref, src_ref, row_ref):
+    src_ref[...] = grad_ref[...].astype(F32)
+    spread_rows(src_ref, row_ref, True)
+    send_ref[...] = row_ref[...].astype(BF16)
+    coarse_ref[...] = dot(dw_ref[...], patch_ref[...], 1, 1).astype(BF16)
+
+
 def backward_kernel(grad_ref, halo_ref, w_ref, out_ref, pad_ref, cols_ref, act_ref):
     for x in range(SIDE):
         for y in range(SIDE):
@@ -244,29 +258,32 @@
     )
 
 
+CHIPS = ("y", "z")
 SPACE = ("y", "z", "c")
-PLANE = ("x", "y")
-
-
-def trade(rows, axes, count):
-    moved = lax.all_to_all(rows.reshape(count, -1, LANES), axes, 0, 0, tiled=True)
-    return moved.reshape(-1, LANES)
+
+
+def trade(rows, axes):
+    return lax.all_to_all(rows, axes, 0, 0, tiled=True)
 
 
 def shards(features, cotangent, conv_weight, down_weight, neighbours):
     block = features[0, 0]
     cot = cotangent[0, 0]
-    row = neighbours[0]
     core = lax.axis_index("c").astype(jnp.int32).reshape(1)
-    other = [(0, 1), (1, 0)]
     rows_shape = ((SLOTS, LANES), BF16)
-    natural, parity, number = jnp.asarray(NATURAL), jnp.asarray(PARITY), jnp.asarray(NUMBER)
-
-    (spread,) = call(spread_kernel, [rows_shape], ins=4, name="spread")(block, row, natural, number)
-    middle = trade(spread, SPACE, 64)
-    route = call(route_kernel, [rows_shape], ins=2, name="route")
-    (routed,) = route(middle, middle)
-    halo = trade(routed, SPACE, 64)
+    by_chip = (32, 32, LANES)
+    row_scratch = pltpu.VMEM((SLOTS, LANES), F32)
+
+    def swap(rows):
+        return lax.ppermute(rows, "c", [(0, 1), (1, 0)])
+
+    (spread,) = call(spread_kernel, [rows_shape], [row_scratch, row_scratch], scalars=1, ins=1, name="spread")(
+        neighbours[0], block
+    )
+    middle = trade(spread.reshape(by_chip), CHIPS)
+    route = call(route_kernel, [(by_chip, BF16)], [pltpu.VMEM(by_chip, F32)], scalars=1, ins=3, name="route")
+    (routed,) = route(core, middle, middle, swap(middle))
+    halo = trade(routed, CHIPS).reshape(SLOTS, LANES)
 
     taps = conv_weight.reshape(C, 27, C)
     pad = ((0, 0), (0, LANES - C), (0, LANES - C))
@@ -275,44 +292,39 @@
     down_w = jnp.pad(down_weight.reshape(C2, 8, C), ((0, 0), (0, 0), (0, LANES - C))).reshape(C2, 8 * LANES)
 
     pad_scratch = pltpu.VMEM((100 * COL, LANES), F32)
-    act_scratch = pltpu.VMEM((VOX, LANES), F32)
-    cols_shape = ((10, 10, DEPTH, 3 * LANES), BF16)
-    coarse, grad, cols, patch, spread2 = call(
+    cols_scratch = pltpu.VMEM((10, 10, DEPTH, 3 * LANES), BF16)
+    grad, patch, keep, send = call(
         forward_kernel,
-        [((C2, LANES), BF16), rows_shape, cols_shape, ((LANES, 8 * LANES), BF16), rows_shape],
-        [pad_scratch, act_scratch],
-        ins=6,
+        [rows_shape, ((LANES, 8 * LANES), BF16), ((HALF_ROWS, LANES), F32), ((HALF_ROWS, LANES), BF16)],
+        [pad_scratch, cols_scratch, row_scratch, pltpu.VMEM((C, 21 * LANES), F32), pltpu.VMEM((C2, 8 * C), F32)],
+        scalars=1,
+        ins=5,
         name="forward",
-    )(block, halo, cot, forward_w, down_w, parity)
-
-    keep, send = call(
-        weight_kernel,
-        [((HALF_ROWS, LANES), F32), ((HALF_ROWS, LANES), BF16)],
-        [pltpu.VMEM((C, 21 * LANES), F32), pltpu.VMEM((C2, 8 * C), F32)],
-        scalars=1,
-        ins=4,
-        name="weight_grad",
-    )(core, grad, cols, patch, cot)
-    got = lax.ppermute(send, "c", other)
-    pair = (keep + got.astype(F32)).astype(BF16)
-    plane = trade(pair, PLANE, 16).reshape(16, 104, LANES)
-    part = jnp.sum(plane.astype(F32), axis=0).astype(BF16)
-    line = trade(jnp.broadcast_to(part, (8, 104, LANES)), "z", 8).reshape(8, 104, LANES)
-    whole = jnp.sum(line.astype(F32), axis=0).astype(BF16)
-    mine = trade(jnp.broadcast_to(whole, (16, 104, LANES)), PLANE, 16)
-    theirs = lax.ppermute(mine, "c", other)
-
-    middle2 = trade(spread2, SPACE, 64)
-    (routed2,) = route(middle, middle2)
-    halo2 = trade(routed2, SPACE, 64)
+    )(core, block, halo, cot, forward_w, down_w)
+    spread2, coarse = call(
+        side_kernel, [rows_shape, ((C2, LANES), BF16)], [row_scratch, row_scratch], ins=3, name="side"
+    )(grad, patch, down_w)
+
+    pair = (keep + swap(send).astype(F32)).astype(BF16)
+    out = jnp.concatenate([spread2.reshape(by_chip), pair.reshape(32, 56, LANES)], axis=1)
+    got = trade(out, CHIPS)
+    middle2 = got[:, :32]
+    part = jnp.sum(got[:, 32:].astype(F32), axis=0)
+    line = trade(jnp.broadcast_to(part, (4, 56, LANES)), "x")
+    whole = jnp.sum(line, axis=0).astype(BF16)
+    (routed2,) = route(core, middle, middle2, swap(middle2))
+    out = jnp.concatenate([routed2, jnp.broadcast_to(whole, (32, 56, LANES))], axis=1)
+    got = trade(out, CHIPS)
+    halo2 = got[:, :32].reshape(SLOTS, LANES)
+    mine = got[:, 32:].reshape(HALF_ROWS, LANES)
+    theirs = swap(mine)
     (grad_features,) = call(
         backward_kernel,
         [((C, VOX), F32)],
-        [pad_scratch, pltpu.VMEM(*cols_shape), act_scratch],
+        [pad_scratch, cols_scratch, row_scratch],
         ins=3,
         name="backward",
     )(grad, halo2, backward_w)
-
     grad_conv, grad_down = call(
         finish_kernel, [((C, 27 * C), F32), ((C2, 8 * C), F32)], scalars=1, ins=2, name="finish"
     )(core, mine, theirs)

time: 151 us -> 138 us (0.914)
  waiting for transfers between devices: 39.7 us -> 8 us
  blocking collectives: 52.2 us -> 76.1 us
  starting transfers between devices: 24.9 us -> 20.5 us
  Pallas kernels: 24.4 us -> 21.9 us
    all_to_all x4 -> x1, waiting for transfers between devices: 38 us -> 6.83 us  [trade(): return lax.all_to_all(rows, axes, 0, 0, tiled=True)]
    all_to_all x3 -> x4, blocking collectives: 52.2 us -> 76.1 us  [trade(): return lax.all_to_all(rows, axes, 0, 0, tiled=True)]
    all_to_all x4 -> x1, starting transfers between devices: 23.9 us -> 4.24 us  [trade(): return lax.all_to_all(rows, axes, 0, 0, tiled=True)]
    ppermute x2 -> x4, starting transfers between devices: 0.99 us -> 16.2 us  [swap(): return lax.ppermute(rows, 'c', [(0, 1), (1, 0)])]
    pallas_call x6, Pallas kernels: 21.8 us -> 19.2 us  [the longest x1 6.24 us: shards(): call(forward_kernel, [rows_shape, ((LANES, 8 * LANES), BF16), ((HALF_ROWS...]
    unnamed x17 -> x25, local copies, waits for them, and re-layouts: 3.68 us -> 5.21 us
  transfers between devices with their start and end apart: 6 -> 5, of which waited for: 5 -> 2; matrix products, arithmetic and copies ran while one was open for 3% -> 4% of each run, Pallas kernels for 5% -> 5%
where the time goes in v2:
time: 138 us; the launch traced here: 137 us
  blocking collectives  76.1 us (55%)
  Pallas kernels  21.9 us (16%)
  starting transfers between devices  20.5 us (15%)
  local copies, waits for them, and re-layouts  8.91 us (6%)
  waiting for transfers between devices  8 us (6%)
    all_to_all x4, blocking collectives, trade(): return lax.all_to_all(rows, axes, 0, 0, tiled=True)  76.1 us
    ppermute x4, starting transfers between devices, swap(): return lax.ppermute(rows, 'c', [(0, 1), (1, 0)])  16.2 us
    all_to_all x1, waiting for transfers between devices, trade(): return lax.all_to_all(rows, axes, 0, 0, tiled=True)  6.83 us
    pallas_call x1, Pallas kernels, shards(): call(forward_kernel, [rows_shape, ((LANES, 8 * LANES), BF16), ((HALF_ROWS...  6.24 us
    unnamed x25, local copies, waits for them, and re-layouts  5.21 us
    pallas_call x1, Pallas kernels, shards(): call(backward_kernel, [((C, VOX), F32)], [pad_scratch, cols_scratch, row_...  4.25 us
    all_to_all x1, starting transfers between devices, trade(): return lax.all_to_all(rows, axes, 0, 0, tiled=True)  4.24 us
  transfers between devices with their start and end apart: 5, of which 2 were waited for; matrix products, arithmetic and copies ran while one was open for 4% of the time, Pallas kernels for 5%

profile of v2, /device:TPU:1, one launch (start us, length us, event | category | flops | bytes accessed | tf_op | source)
XLA Modules:
  0.0 137.4 jit_solution(14885215672108706241)
XLA Ops:
  0.6 1.9 %spread.1 = bf16[1024,128]{1,0:T(8,128)(2,1)} custom-call(s32[1,26]{1,0:T(1,128)} %bitcast.41, bf16[96,1024]{1,0:T(8,128)(2,1)} %bitcast.36), custom_call_target="tpu_custom_call" | custom-call | tf_op jit(solution)/shard_map/spread/pallas_call | solution.py:280
  2.5 21.9 %all_to_all.25.owner_ref.mine_ref = bf16[32,32,128]{2,1,0:T(8,128)(2,1)S(1)} all-to-all(bf16[32,32,128]{2,1,0:T(8,128)(2,1)} %bitcast.34), channel_id=1, replica_groups=mesh['x'=4,'y'=4,'z'=8,'c'=2] {'y','z'}, dimensions={0} | all-to-all | bytes 524288 | tf_op jit(solution)/shard_map/all_to_all | solution.py:266
  24.4 3.7 %collective-permute-start = (bf16[32,32,128]{2,1,0:T(8,128)(2,1)S(1)}, bf16[32,32,128]{2,1,0:T(8,128)(2,1)S(1)}, u32[]{:S(2)}, u32[]{:S(2)}) collective-permute-start(bf16[32,32,128]{2,1,0:T(8,128)(2,1)S(1)} %all_to_all.25.owner_ref.mine_ref), channel_id=1, source_target_pairs={{0,1},{1,0},{2,3},{3,2},{4,5},{5,4},{6,7},{7,6},{8,9},{9,8},{10,11... | collective-permute-start | bytes 786440 | tf_op jit(solution)/shard_map/ppermute | solution.py:278
  28.1 1.2 collective-permute-done.other_ref
  29.3 0.0 copy-done
  29.3 0.7 copy-done.10
  30.0 2.4 %route.2 = bf16[32,32,128]{2,1,0:T(8,128)(2,1)} custom-call(s32[1]{0:T(128)} %bitcast.core_ref, bf16[32,32,128]{2,1,0:T(8,128)(2,1)} %copy-done, bf16[32,32,128]{2,1,0:T(8,128)(2,1)} %copy-done, bf16[32,32,128]{2,1,0:T(8,128)(2,1)} %copy-done.10), custom_call_target="tpu_custom_call" | custom-call | tf_op jit(solution)/shard_map/route/pallas_call | solution.py:285
  32.3 4.2 %all-to-all-start.1 = ((bf16[32,32,128]{2,1,0:T(8,128)(2,1)}), bf16[32,32,128]{2,1,0:T(8,128)(2,1)S(1)}, u32[]{:S(2)}, u32[]{:S(2)}) async-start(bf16[32,32,128]{2,1,0:T(8,128)(2,1)} %route.2), calls=%async_computation.1 | async-start | bytes 524288 | tf_op jit(solution)/shard_map/all_to_all | solution.py:266
  36.6 0.0 copy-done.5
  36.6 0.3 copy.13
  36.9 0.0 copy-done.7
  36.9 0.4 reshape.49
  37.4 1.1 pad.11
  38.5 0.1 pad.12
  38.6 0.8 copy.18
  39.4 6.8 %all-to-all-done.1 = bf16[32,32,128]{2,1,0:T(8,128)(2,1)S(1)} async-done(((bf16[32,32,128]{2,1,0:T(8,128)(2,1)}), bf16[32,32,128]{2,1,0:T(8,128)(2,1)S(1)}, u32[]{:S(2)}, u32[]{:S(2)}) %all-to-all-start.1) | async-done | bytes 262176 | tf_op jit(solution)/shard_map/all_to_all | solution.py:266
  46.3 0.7 copy-done.2
  47.0 6.2 %forward.1 = (bf16[1024,128]{1,0:T(8,128)(2,1)}, bf16[128,1024]{1,0:T(8,128)(2,1)}, f32[1792,128]{1,0:T(8,128)}, bf16[1792,128]{1,0:T(8,128)(2,1)}) custom-call(s32[1]{0:T(128)} %bitcast.core_ref, bf16[96,1024]{1,0:T(8,128)(2,1)} %bitcast.37, bf16[1024,128]{1,0:T(8,128)(2,1)} %bitcast.35, bf16[192,128]{1,0:T(8,128)(2,1)} %bitcast.40, ...), custom_call_target="tpu_custom_call" | custom-call | tf_op jit(solution)/shard_map/forward/pallas_call | solution.py:296
  53.2 3.7 %collective-permute-start.1 = (bf16[1792,128]{1,0:T(8,128)(2,1)}, bf16[1792,128]{1,0:T(8,128)(2,1)S(1)}, u32[]{:S(2)}, u32[]{:S(2)}) collective-permute-start(bf16[1792,128]{1,0:T(8,128)(2,1)} %get-tuple-element.17), channel_id=1, source_target_pairs={{0,1},{1,0},{2,3},{3,2},{4,5},{5,4},{6,7},{7,6},{8,9},{9,8},{10,11... | collective-permute-start | bytes 1376264 | tf_op jit(solution)/shard_map/ppermute | solution.py:278
  56.9 2.1 %side.1 = (bf16[1024,128]{1,0:T(8,128)(2,1)}, bf16[192,128]{1,0:T(8,128)(2,1)}) custom-call(bf16[1024,128]{1,0:T(8,128)(2,1)} %get-tuple-element.12.grad_ref, bf16[128,1024]{1,0:T(8,128)(2,1)} %get-tuple-element.13.patch_ref, bf16[192,1024]{1,0:T(8,128)(2,1)} %bitcast.27), custom_call_target="tpu_custom_call" | custom-call | tf_op jit(solution)/shard_map/side/pallas_call | solution.py:304
  59.0 0.0 collective-permute-done.1
  59.0 0.0 copy-done.4
  59.1 0.1 add_convert_fusion
  59.2 0.8 copy-done.9
  60.0 0.1 pad_maximum_fusion
  60.0 22.7 %all_to_all.26 = bf16[32,88,128]{2,1,0:T(8,128)(2,1)S(1)} all-to-all(bf16[32,88,128]{2,1,0:T(8,128)(2,1)S(1)} %pad_maximum_fusion), channel_id=1, replica_groups=mesh['x'=4,'y'=4,'z'=8,'c'=2] {'y','z'}, dimensions={0} | all-to-all | bytes 1441792 | tf_op jit(solution)/shard_map/all_to_all | solution.py:266
  82.8 0.0 copy-start.3
  82.8 3.3 %collective-permute-start.2 = (bf16[32,32,128]{2,1,0:T(8,128)(2,1)S(1)}, bf16[32,32,128]{2,1,0:T(8,128)(2,1)S(1)}, u32[]{:S(2)}, u32[]{:S(2)}) collective-permute-start(bf16[32,32,128]{2,1,0:T(8,128)(2,1)S(1)} %slice.16.mine_ref), channel_id=1, source_target_pairs={{0,1},{1,0},{2,3},{3,2},{4,5},{5,4},{6,7},{7,6},{8,9},{9,8},{10,11... | collective-permute-start | bytes 786440 | tf_op jit(solution)/shard_map/ppermute | solution.py:278
  86.1 0.1 convert_reduce_fusion
  86.2 8.6 %all_to_all.27 = f32[4,56,128]{2,1,0:T(8,128)S(1)} all-to-all(f32[4,56,128]{2,1,0:T(8,128)S(1)} %broadcast_in_dim.13), channel_id=1, replica_groups=mesh['x'=4,'y'=4,'z'=8,'c'=2] {'x'}, dimensions={0} | all-to-all | bytes 229376 | tf_op jit(solution)/shard_map/all_to_all | solution.py:266
  94.8 0.0 collective-permute-done.2.other_ref
  94.8 0.0 copy-done.3
  94.8 0.0 copy-start.8
  94.8 0.7 copy-done.8
  95.5 2.4 %route.3 = bf16[32,32,128]{2,1,0:T(8,128)(2,1)} custom-call(s32[1]{0:T(128)} %bitcast.core_ref, bf16[32,32,128]{2,1,0:T(8,128)(2,1)} %copy-done, bf16[32,32,128]{2,1,0:T(8,128)(2,1)} %copy-done.3, bf16[32,32,128]{2,1,0:T(8,128)(2,1)} %copy-done.8), custom_call_target="tpu_custom_call" | custom-call | tf_op jit(solution)/shard_map/route/pallas_call | solution.py:315
  97.9 0.1 broadcast_in_dim.14
  97.9 1.0 pad_maximum_fusion.1
  98.9 22.9 %all_to_all.28 = bf16[32,88,128]{2,1,0:T(8,128)(2,1)S(1)} all-to-all(bf16[32,88,128]{2,1,0:T(8,128)(2,1)S(1)} %pad_maximum_fusion.1), channel_id=1, replica_groups=mesh['x'=4,'y'=4,'z'=8,'c'=2] {'y','z'}, dimensions={0} | all-to-all | bytes 1441792 | tf_op jit(solution)/shard_map/all_to_all | solution.py:266
  121.9 0.0 copy-start.1
  121.9 5.5 %collective-permute-start.3 = (bf16[1792,128]{1,0:T(8,128)(2,1)S(1)}, bf16[1792,128]{1,0:T(8,128)(2,1)S(1)}, u32[]{:S(2)}, u32[]{:S(2)}) collective-permute-start(bf16[1792,128]{1,0:T(8,128)(2,1)S(1)} %bitcast.29), channel_id=1, source_target_pairs={{0,1},{1,0},{2,3},{3,2},{4,5},{5,4},{6,7},{7,6},{8,9},{9,8},{10,11... | collective-permute-start | bytes 1376264 | tf_op jit(solution)/shard_map/ppermute | solution.py:278
  127.5 0.3 copy.15
  127.8 0.0 copy-done.1
  127.8 1.1 pad.13.clone
  129.0 0.7 slice.18
  129.7 4.3 %backward.1 = f32[96,1024]{1,0:T(8,128)} custom-call(bf16[1024,128]{1,0:T(8,128)(2,1)} %get-tuple-element.12.grad_ref, bf16[1024,128]{1,0:T(8,128)(2,1)} %bitcast.33, bf16[9,384,128]{2,1,0:T(8,128)(2,1)} %bitcast.25), custom_call_target="tpu_custom_call" | custom-call | tf_op jit(solution)/shard_map/backward/pallas_call | solution.py:321
  133.9 0.0 collective-permute-done.3.other_ref
  133.9 0.8 copy-done.6
  134.7 2.7 %finish.1 = (f32[96,2592]{1,0:T(8,128)}, f32[192,768]{1,0:T(8,128)}) custom-call(s32[1]{0:T(128)} %bitcast.core_ref, bf16[1792,128]{1,0:T(8,128)(2,1)} %bitcast.30, bf16[1792,128]{1,0:T(8,128)(2,1)} %copy-done.6), custom_call_target="tpu_custom_call" | custom-call | tf_op jit(solution)/shard_map/finish/pallas_call | solution.py:328
  (13 shorter events, 0.1 us)
Async XLA Ops:
  2.5 34.1 %copy-start.5 = (bf16[96,2592]{1,0:T(8,128)(2,1)S(1)}, bf16[96,2592]{1,0:T(8,128)(2,1)}, u32[]{:S(2)}) copy-start(bf16[96,2592]{1,0:T(8,128)(2,1)} %param.7) | copy-start | bytes 1492996
  24.4 4.9 %copy-start = (bf16[32,32,128]{2,1,0:T(8,128)(2,1)}, bf16[32,32,128]{2,1,0:T(8,128)(2,1)S(1)}, u32[]{:S(2)}) copy-start(bf16[32,32,128]{2,1,0:T(8,128)(2,1)S(1)} %all_to_all.25.owner_ref.mine_ref) | copy-start | bytes 786436
  24.4 4.9 %collective-permute-start = (bf16[32,32,128]{2,1,0:T(8,128)(2,1)S(1)}, bf16[32,32,128]{2,1,0:T(8,128)(2,1)S(1)}, u32[]{:S(2)}, u32[]{:S(2)}) collective-permute-start(bf16[32,32,128]{2,1,0:T(8,128)(2,1)S(1)} %all_to_all.25.owner_ref.mine_ref), channel_id=1, source_target_pairs={{0,1},{1,0},{2,3},{3,2},{4,5},{5,4},{6,7},{7,6},{8,9},{9,8},{10,11... | collective-permute-start | bytes 786440 | tf_op jit(solution)/shard_map/ppermute | solution.py:278
  29.2 0.7 copy-start.10
  32.3 4.6 %copy-start.7 = (bf16[192,768]{1,0:T(8,128)(2,1)S(1)}, bf16[192,768]{1,0:T(8,128)(2,1)}, u32[]{:S(2)}) copy-start(bf16[192,768]{1,0:T(8,128)(2,1)} %param.8) | copy-start | bytes 884740
  32.3 13.9 %all-to-all-start.1 = ((bf16[32,32,128]{2,1,0:T(8,128)(2,1)}), bf16[32,32,128]{2,1,0:T(8,128)(2,1)S(1)}, u32[]{:S(2)}, u32[]{:S(2)}) async-start(bf16[32,32,128]{2,1,0:T(8,128)(2,1)} %route.2), calls=%async_computation.1 | async-start | bytes 524288 | tf_op jit(solution)/shard_map/all_to_all | solution.py:266
  46.3 0.7 copy-start.2
  53.2 5.8 %copy-start.4 = (f32[1792,128]{1,0:T(8,128)S(1)}, f32[1792,128]{1,0:T(8,128)}, u32[]{:S(2)}) copy-start(f32[1792,128]{1,0:T(8,128)} %get-tuple-element.16) | copy-start | bytes 2752516
  53.2 5.8 %collective-permute-start.1 = (bf16[1792,128]{1,0:T(8,128)(2,1)}, bf16[1792,128]{1,0:T(8,128)(2,1)S(1)}, u32[]{:S(2)}, u32[]{:S(2)}) collective-permute-start(bf16[1792,128]{1,0:T(8,128)(2,1)} %get-tuple-element.17), channel_id=1, source_target_pairs={{0,1},{1,0},{2,3},{3,2},{4,5},{5,4},{6,7},{7,6},{8,9},{9,8},{10,11... | collective-permute-start | bytes 1376264 | tf_op jit(solution)/shard_map/ppermute | solution.py:278
  59.0 1.0 copy-start.9
  82.8 12.0 %copy-start.3 = (bf16[32,32,128]{2,1,0:T(8,128)(2,1)}, bf16[32,32,128]{2,1,0:T(8,128)(2,1)S(1)}, u32[]{:S(2)}) copy-start(bf16[32,32,128]{2,1,0:T(8,128)(2,1)S(1)} %slice.16.mine_ref) | copy-start | bytes 786436
  82.8 11.9 %collective-permute-start.2 = (bf16[32,32,128]{2,1,0:T(8,128)(2,1)S(1)}, bf16[32,32,128]{2,1,0:T(8,128)(2,1)S(1)}, u32[]{:S(2)}, u32[]{:S(2)}) collective-permute-start(bf16[32,32,128]{2,1,0:T(8,128)(2,1)S(1)} %slice.16.mine_ref), channel_id=1, source_target_pairs={{0,1},{1,0},{2,3},{3,2},{4,5},{5,4},{6,7},{7,6},{8,9},{9,8},{10,11... | collective-permute-start | bytes 786440 | tf_op jit(solution)/shard_map/ppermute | solution.py:278
  94.8 0.7 copy-start.8
  121.9 5.9 %copy-start.1 = (bf16[32,56,128]{2,1,0:T(8,128)(2,1)}, bf16[32,56,128]{2,1,0:T(8,128)(2,1)S(1)}, u32[]{:S(2)}) copy-start(bf16[32,56,128]{2,1,0:T(8,128)(2,1)S(1)} %slice.19) | copy-start | bytes 1376260
  121.9 12.0 %collective-permute-start.3 = (bf16[1792,128]{1,0:T(8,128)(2,1)S(1)}, bf16[1792,128]{1,0:T(8,128)(2,1)S(1)}, u32[]{:S(2)}, u32[]{:S(2)}) collective-permute-start(bf16[1792,128]{1,0:T(8,128)(2,1)S(1)} %bitcast.29), channel_id=1, source_target_pairs={{0,1},{1,0},{2,3},{3,2},{4,5},{5,4},{6,7},{7,6},{8,9},{9,8},{10,11... | collective-permute-start | bytes 1376264 | tf_op jit(solution)/shard_map/ppermute | solution.py:278
  133.9 0.8 copy-start.6

commit v3 on v2

--- a/solution.py
+++ b/solution.py
@@ -18,7 +18,7 @@
 EPSILON = 1e-06
 F32 = jnp.float32
 BF16 = jnp.bfloat16
-PARAMS = pltpu.CompilerParams(vmem_limit_bytes=56 << 20)
+PARAMS = pltpu.CompilerParams(vmem_limit_bytes=32 << 20)
 
 
 RIM = [(x, y) for x in range(10) for y in range(10) if x in (0, 9) or y in (0, 9)]
@@ -243,13 +243,20 @@
             down_ref[pl.ds(pl.multiple_of(half * 96, 32), 96), pl.ds(lt * LANES, LANES)] = values
 
 
+def here(rows):
+    return pltpu.with_memory_space_constraint(rows, pltpu.VMEM)
+
+
 def call(body, outs, scratch=(), scalars=0, ins=0, name=None):
     specs = [pl.BlockSpec(memory_space=pltpu.SMEM)] * scalars + [
         pl.BlockSpec(memory_space=pltpu.VMEM)
     ] * ins
     return pl.pallas_call(
         body,
-        out_shape=[jax.ShapeDtypeStruct(shape, kind) for shape, kind in outs],
+        out_shape=[
+            jax.ShapeDtypeStruct(shape, kind) if leaves else pltpu.VMEM(shape, kind)
+            for shape, kind, *leaves in outs
+        ],
         in_specs=specs,
         out_specs=[pl.BlockSpec(memory_space=pltpu.VMEM)] * len(outs),
         scratch_shapes=list(scratch),
@@ -280,9 +287,9 @@
     (spread,) = call(spread_kernel, [rows_shape], [row_scratch, row_scratch], scalars=1, ins=1, name="spread")(
         neighbours[0], block
     )
-    middle = trade(spread.reshape(by_chip), CHIPS)
+    middle = here(trade(spread.reshape(by_chip), CHIPS))
     route = call(route_kernel, [(by_chip, BF16)], [pltpu.VMEM(by_chip, F32)], scalars=1, ins=3, name="route")
-    (routed,) = route(core, middle, middle, swap(middle))
+    (routed,) = route(core, middle, middle, here(swap(middle)))
     halo = trade(routed, CHIPS).reshape(SLOTS, LANES)
 
     taps = conv_weight.reshape(C, 27, C)
@@ -290,6 +297,8 @@
     forward_w = jnp.pad(taps.transpose(1, 2, 0), pad).reshape(9, 3 * LANES, LANES)
     backward_w = jnp.pad(taps.transpose(1, 0, 2)[::-1], pad).reshape(9, 3 * LANES, LANES)
     down_w = jnp.pad(down_weight.reshape(C2, 8, C), ((0, 0), (0, 0), (0, LANES - C))).reshape(C2, 8 * LANES)
+    halo, forward_w, backward_w, down_w = lax.optimization_barrier((halo, forward_w, backward_w, down_w))
+    forward_w, backward_w, down_w = here(forward_w), here(backward_w), here(down_w)
 
     pad_scratch = pltpu.VMEM((100 * COL, LANES), F32)
     cols_scratch = pltpu.VMEM((10, 10, DEPTH, 3 * LANES), BF16)
@@ -300,9 +309,9 @@
         scalars=1,
         ins=5,
         name="forward",
-    )(core, block, halo, cot, forward_w, down_w)
+    )(core, block, here(halo), cot, forward_w, down_w)
     spread2, coarse = call(
-        side_kernel, [rows_shape, ((C2, LANES), BF16)], [row_scratch, row_scratch], ins=3, name="side"
+        side_kernel, [rows_shape, ((C2, LANES), BF16, True)], [row_scratch, row_scratch], ins=3, name="side"
     )(grad, patch, down_w)
 
     pair = (keep + swap(send).astype(F32)).astype(BF16)
@@ -310,9 +319,10 @@
     got = trade(out, CHIPS)
     middle2 = got[:, :32]
     part = jnp.sum(got[:, 32:].astype(F32), axis=0)
+    other2, part = lax.optimization_barrier((swap(middle2), part))
     line = trade(jnp.broadcast_to(part, (4, 56, LANES)), "x")
     whole = jnp.sum(line, axis=0).astype(BF16)
-    (routed2,) = route(core, middle, middle2, swap(middle2))
+    (routed2,) = route(core, middle, here(middle2), here(other2))
     out = jnp.concatenate([routed2, jnp.broadcast_to(whole, (32, 56, LANES))], axis=1)
     got = trade(out, CHIPS)
     halo2 = got[:, :32].reshape(SLOTS, LANES)
@@ -320,14 +330,14 @@
     theirs = swap(mine)
     (grad_features,) = call(
         backward_kernel,
-        [((C, VOX), F32)],
+        [((C, VOX), F32, True)],
         [pad_scratch, cols_scratch, row_scratch],
         ins=3,
         name="backward",
-    )(grad, halo2, backward_w)
+    )(grad, here(halo2), backward_w)
     grad_conv, grad_down = call(
-        finish_kernel, [((C, 27 * C), F32), ((C2, 8 * C), F32)], scalars=1, ins=2, name="finish"
-    )(core, mine, theirs)
+        finish_kernel, [((C, 27 * C), F32, True), ((C2, 8 * C), F32, True)], scalars=1, ins=2, name="finish"
+    )(core, here(mine), here(theirs))
     return coarse[None, None], grad_features[None, None], grad_conv, grad_down
 
 

time: 138 us -> 124 us (0.90)
  blocking collectives: 76.1 us -> 65.9 us
  Pallas kernels: 21.9 us -> 11.9 us
  starting transfers between devices: 20.5 us -> 25.5 us
  waiting for transfers between devices: 8 us -> 12.7 us
  local copies, waits for them, and re-layouts: 8.91 us -> 6.12 us
    all_to_all x4 -> x3, blocking collectives: 76.1 us -> 65.9 us  [trade(): return lax.all_to_all(rows, axes, 0, 0, tiled=True)]
    pallas_call x5, Pallas kernels: 13.8 us -> 7.3 us  [the longest x1 2.92 us: shards(): call(backward_kernel, [((C, VOX), F32, True)], [pad_scratch, cols_scratch...]
    all_to_all x1 -> x2, starting transfers between devices: 4.24 us -> 8.13 us  [trade(): return lax.all_to_all(rows, axes, 0, 0, tiled=True)]
    all_to_all x1 -> x2, waiting for transfers between devices: 6.83 us -> 10 us  [trade(): return lax.all_to_all(rows, axes, 0, 0, tiled=True)]
    pallas_call x1, Pallas kernels: 6.24 us -> 3.8 us  [shards(): call(forward_kernel, [rows_shape, ((LANES, 8 * LANES), BF16), ((HALF_ROWS...]
    unnamed x25 -> x17, local copies, waits for them, and re-layouts: 5.21 us -> 3.19 us
    ppermute x4, waiting for transfers between devices: 1.17 us -> 2.68 us  [swap(): return lax.ppermute(rows, 'c', [(0, 1), (1, 0)])]
  transfers between devices with their start and end apart: 5 -> 6, of which waited for: 2 -> 5; matrix products, arithmetic and copies ran while one was open for 4% -> 2% of each run, Pallas kernels for 5% -> 4%
where the time goes in v3:
time: 124 us; the launch traced here: 123 us
  blocking collectives  65.9 us (53%)
  starting transfers between devices  25.5 us (21%)
  waiting for transfers between devices  12.7 us (10%)
  Pallas kernels  11.9 us (10%)
  local copies, waits for them, and re-layouts  6.12 us (5%)
    all_to_all x3, blocking collectives, trade(): return lax.all_to_all(rows, axes, 0, 0, tiled=True)  65.9 us
    ppermute x4, starting transfers between devices, swap(): return lax.ppermute(rows, 'c', [(0, 1), (1, 0)])  17.4 us
    all_to_all x2, waiting for transfers between devices, trade(): return lax.all_to_all(rows, axes, 0, 0, tiled=True)  10 us
    all_to_all x2, starting transfers between devices, trade(): return lax.all_to_all(rows, axes, 0, 0, tiled=True)  8.13 us
    pallas_call x1, Pallas kernels, shards(): call(forward_kernel, [rows_shape, ((LANES, 8 * LANES), BF16), ((HALF_ROWS...  3.8 us
    unnamed x17, local copies, waits for them, and re-layouts  3.19 us
    pallas_call x1, Pallas kernels, shards(): call(backward_kernel, [((C, VOX), F32, True)], [pad_scratch, cols_scratch...  2.92 us
    ppermute x4, waiting for transfers between devices, swap(): return lax.ppermute(rows, 'c', [(0, 1), (1, 0)])  2.68 us
  transfers between devices with their start and end apart: 6, of which 5 were waited for; matrix products, arithmetic and copies ran while one was open for 2% of the time, Pallas kernels for 4%

profile of v3, /device:TPU:1, one launch (start us, length us, event | category | flops | bytes accessed | tf_op | source)
XLA Modules:
  0.0 123.2 jit_solution(13970825635843389044)
XLA Ops:
  0.6 0.0 copy-start
  0.6 0.9 copy-done
  1.6 0.7 copy-done.3
  2.2 0.8 spread.1
  3.0 0.0 copy-start.6
  3.0 21.7 %all_to_all.25.owner_ref.mine_ref = bf16[32,32,128]{2,1,0:T(8,128)(2,1)S(1)} all-to-all(bf16[32,32,128]{2,1,0:T(8,128)(2,1)S(1)} %bitcast.30), channel_id=1, replica_groups=mesh['x'=4,'y'=4,'z'=8,'c'=2] {'y','z'}, dimensions={0} | all-to-all | bytes 524288 | tf_op jit(solution)/shard_map/all_to_all | solution.py:273
  24.7 3.7 %collective-permute-start = (bf16[32,32,128]{2,1,0:T(8,128)(2,1)S(1)}, bf16[32,32,128]{2,1,0:T(8,128)(2,1)S(1)}, u32[]{:S(2)}, u32[]{:S(2)}) collective-permute-start(bf16[32,32,128]{2,1,0:T(8,128)(2,1)S(1)} %all_to_all.25.owner_ref.mine_ref), channel_id=1, source_target_pairs={{0,1},{1,0},{2,3},{3,2},{4,5},{5,4},{6,7},{7,6},{8,9},{9,8},{10,11... | collective-permute-start | bytes 786440 | tf_op jit(solution)/shard_map/ppermute | solution.py:285
  28.4 1.2 collective-permute-done.other_ref
  29.5 1.3 %route.2 = bf16[32,32,128]{2,1,0:T(8,128)(2,1)} custom-call(s32[1]{0:T(128)} %bitcast.core_ref, bf16[32,32,128]{2,1,0:T(8,128)(2,1)S(1)} %all_to_all.25.owner_ref.mine_ref, bf16[32,32,128]{2,1,0:T(8,128)(2,1)S(1)} %all_to_all.25.owner_ref.mine_ref, bf16[32,32,128]{2,1,0:T(8,128)(2,1)S(1)} %collective-permute-done.other_ref), custom_call_target="tpu_custom_call" | custom-call | tf_op jit(solution)/shard_map/route/pallas_call | solution.py:292
  30.8 4.1 %all-to-all-start.1 = ((bf16[32,32,128]{2,1,0:T(8,128)(2,1)}), bf16[32,32,128]{2,1,0:T(8,128)(2,1)S(1)}, u32[]{:S(2)}, u32[]{:S(2)}) async-start(bf16[32,32,128]{2,1,0:T(8,128)(2,1)} %route.2), calls=%async_computation.1 | async-start | bytes 524288 | tf_op jit(solution)/shard_map/all_to_all | solution.py:273
  34.9 0.0 copy-done.6
  35.0 0.0 copy-start.5
  35.0 0.4 reshape.50
  35.4 0.1 pad.13
  35.5 0.1 copy.18
  35.6 0.4 copy-done.5
  36.0 0.3 copy.13
  36.3 0.0 copy-start.4
  36.4 0.3 copy.15
  36.7 0.5 copy-done.4
  37.2 0.2 pad.12.clone
  37.4 0.0 copy-start.1
  37.4 0.0 copy-start.2
  37.4 1.3 %pad.11 = bf16[27,128,128]{2,1,0:T(8,128)(2,1)S(1)} pad(bf16[27,96,96]{2,1,0:T(8,128)(2,1)} %bitcast.38, bf16[]{:T(256)} %constant.2.clone.1), padding=0_0x0_32x0_32 | pad | bytes 1382402 | tf_op jit(solution)/shard_map/jit(_pad)/pad | solution.py:297
  38.8 5.8 %all-to-all-done.1 = bf16[32,32,128]{2,1,0:T(8,128)(2,1)S(1)} async-done(((bf16[32,32,128]{2,1,0:T(8,128)(2,1)}), bf16[32,32,128]{2,1,0:T(8,128)(2,1)S(1)}, u32[]{:S(2)}, u32[]{:S(2)}) %all-to-all-start.1) | async-done | bytes 262176 | tf_op jit(solution)/shard_map/all_to_all | solution.py:273
  44.6 0.0 copy-done.1
  44.6 0.0 copy-done.2
  44.6 3.8 %forward.1 = (bf16[1024,128]{1,0:T(8,128)(2,1)S(1)}, bf16[128,1024]{1,0:T(8,128)(2,1)S(1)}, f32[1792,128]{1,0:T(8,128)S(1)}, bf16[1792,128]{1,0:T(8,128)(2,1)S(1)}) custom-call(s32[1]{0:T(128)} %bitcast.core_ref, bf16[96,1024]{1,0:T(8,128)(2,1)S(1)} %bitcast.33, bf16[1024,128]{1,0:T(8,128)(2,1)S(1)} %bitcast.31, bf16[192,128]{1,0:T(8,128)(2,1)S(1)} %bitcast.35, ...), custom_call_target="tpu_custom_call" | custom-call | tf_op jit(solution)/shard_map/forward/pallas_call | solution.py:305
  48.4 3.8 %collective-permute-start.1 = (bf16[1792,128]{1,0:T(8,128)(2,1)S(1)}, bf16[1792,128]{1,0:T(8,128)(2,1)S(1)}, u32[]{:S(2)}, u32[]{:S(2)}) collective-permute-start(bf16[1792,128]{1,0:T(8,128)(2,1)S(1)} %get-tuple-element.26), channel_id=1, source_target_pairs={{0,1},{1,0},{2,3},{3,2},{4,5},{5,4},{6,7},{7,6},{8,9},{9,8},{10,11... | collective-permute-start | bytes 1376264 | tf_op jit(solution)/shard_map/ppermute | solution.py:285
  52.2 1.0 side.1
  53.2 0.4 collective-permute-done.1
  53.7 0.1 add_convert_fusion
  53.8 0.1 pad_maximum_fusion
  53.8 21.7 %all_to_all.26 = bf16[32,88,128]{2,1,0:T(8,128)(2,1)S(1)} all-to-all(bf16[32,88,128]{2,1,0:T(8,128)(2,1)S(1)} %pad_maximum_fusion), channel_id=1, replica_groups=mesh['x'=4,'y'=4,'z'=8,'c'=2] {'y','z'}, dimensions={0} | all-to-all | bytes 1441792 | tf_op jit(solution)/shard_map/all_to_all | solution.py:273
  75.6 4.8 %collective-permute-start.2 = (bf16[32,32,128]{2,1,0:T(8,128)(2,1)S(1)}, bf16[32,32,128]{2,1,0:T(8,128)(2,1)S(1)}, u32[]{:S(2)}, u32[]{:S(2)}) collective-permute-start(bf16[32,32,128]{2,1,0:T(8,128)(2,1)S(1)} %slice.16.mine_ref), channel_id=1, source_target_pairs={{0,1},{1,0},{2,3},{3,2},{4,5},{5,4},{6,7},{7,6},{8,9},{9,8},{10,11... | collective-permute-start | bytes 786440 | tf_op jit(solution)/shard_map/ppermute | solution.py:285
  80.3 0.1 convert_reduce_fusion
  80.4 1.1 collective-permute-done.2.other_ref
  81.5 0.7 broadcast_in_dim.13
  82.2 4.0 %all-to-all-start.3 = ((f32[4,56,128]{2,1,0:T(8,128)}), f32[4,56,128]{2,1,0:T(8,128)S(1)}, u32[]{:S(2)}, u32[]{:S(2)}) async-start(f32[4,56,128]{2,1,0:T(8,128)} %broadcast_in_dim.13), calls=%async_computation.3 | async-start | bytes 229376 | tf_op jit(solution)/shard_map/all_to_all | solution.py:273
  86.2 0.6 route.3
  86.8 4.2 %all-to-all-done.3 = f32[4,56,128]{2,1,0:T(8,128)S(1)} async-done(((f32[4,56,128]{2,1,0:T(8,128)}), f32[4,56,128]{2,1,0:T(8,128)S(1)}, u32[]{:S(2)}, u32[]{:S(2)}) %all-to-all-start.3) | async-done | bytes 114720 | tf_op jit(solution)/shard_map/all_to_all | solution.py:273
  90.9 0.1 broadcast_in_dim.14
  91.0 0.1 pad_maximum_fusion.1
  91.1 22.5 %all_to_all.27 = bf16[32,88,128]{2,1,0:T(8,128)(2,1)S(1)} all-to-all(bf16[32,88,128]{2,1,0:T(8,128)(2,1)S(1)} %pad_maximum_fusion.1), channel_id=1, replica_groups=mesh['x'=4,'y'=4,'z'=8,'c'=2] {'y','z'}, dimensions={0} | all-to-all | bytes 1441792 | tf_op jit(solution)/shard_map/all_to_all | solution.py:273
  113.6 5.1 %collective-permute-start.3 = (bf16[1792,128]{1,0:T(8,128)(2,1)S(1)}, bf16[1792,128]{1,0:T(8,128)(2,1)S(1)}, u32[]{:S(2)}, u32[]{:S(2)}) collective-permute-start(bf16[1792,128]{1,0:T(8,128)(2,1)S(1)} %bitcast.27), channel_id=1, source_target_pairs={{0,1},{1,0},{2,3},{3,2},{4,5},{5,4},{6,7},{7,6},{8,9},{9,8},{10,11... | collective-permute-start | bytes 1376264 | tf_op jit(solution)/shard_map/ppermute | solution.py:285
  118.8 2.9 %backward.1 = f32[96,1024]{1,0:T(8,128)} custom-call(bf16[1024,128]{1,0:T(8,128)(2,1)S(1)} %get-tuple-element.21.grad_ref, bf16[1024,128]{1,0:T(8,128)(2,1)S(1)} %bitcast.29, bf16[9,384,128]{2,1,0:T(8,128)(2,1)S(1)} %bitcast.23), custom_call_target="tpu_custom_call" | custom-call | tf_op jit(solution)/shard_map/backward/pallas_call | solution.py:331
  121.7 0.0 collective-permute-done.3.other_ref
  121.7 1.5 %finish.1 = (f32[96,2592]{1,0:T(8,128)}, f32[192,768]{1,0:T(8,128)}) custom-call(s32[1]{0:T(128)} %bitcast.core_ref, bf16[1792,128]{1,0:T(8,128)(2,1)S(1)} %bitcast.28, bf16[1792,128]{1,0:T(8,128)(2,1)S(1)} %collective-permute-done.3.other_ref), custom_call_target="tpu_custom_call" | custom-call | tf_op jit(solution)/shard_map/finish/pallas_call | solution.py:338
  (6 shorter events, 0.1 us)
Async XLA Ops:
  0.6 0.9 copy-start
  1.6 0.7 copy-start.3
  3.0 32.0 %copy-start.6 = (bf16[192,768]{1,0:T(8,128)(2,1)S(1)}, bf16[192,768]{1,0:T(8,128)(2,1)}, u32[]{:S(2)}) copy-start(bf16[192,768]{1,0:T(8,128)(2,1)} %param.8) | copy-start | bytes 884740
  24.7 4.9 %collective-permute-start = (bf16[32,32,128]{2,1,0:T(8,128)(2,1)S(1)}, bf16[32,32,128]{2,1,0:T(8,128)(2,1)S(1)}, u32[]{:S(2)}, u32[]{:S(2)}) collective-permute-start(bf16[32,32,128]{2,1,0:T(8,128)(2,1)S(1)} %all_to_all.25.owner_ref.mine_ref), channel_id=1, source_target_pairs={{0,1},{1,0},{2,3},{3,2},{4,5},{5,4},{6,7},{7,6},{8,9},{9,8},{10,11... | collective-permute-start | bytes 786440 | tf_op jit(solution)/shard_map/ppermute | solution.py:285
  30.8 13.8 %all-to-all-start.1 = ((bf16[32,32,128]{2,1,0:T(8,128)(2,1)}), bf16[32,32,128]{2,1,0:T(8,128)(2,1)S(1)}, u32[]{:S(2)}, u32[]{:S(2)}) async-start(bf16[32,32,128]{2,1,0:T(8,128)(2,1)} %route.2), calls=%async_computation.1 | async-start | bytes 524288 | tf_op jit(solution)/shard_map/all_to_all | solution.py:273
  35.0 1.0 copy-start.5
  36.3 0.8 copy-start.4
  37.4 7.2 %copy-start.1 = (bf16[1,1,96,1024]{3,2,1,0:T(8,128)(2,1)S(1)}, bf16[1,1,96,1024]{3,2,1,0:T(8,128)(2,1)}, u32[]{:S(2)}) copy-start(bf16[1,1,96,1024]{3,2,1,0:T(8,128)(2,1)} %param.5) | copy-start | bytes 589828
  37.4 7.2 %copy-start.2 = (bf16[1,1,192,128]{3,2,1,0:T(8,128)(2,1)S(1)}, bf16[1,1,192,128]{3,2,1,0:T(8,128)(2,1)}, u32[]{:S(2)}) copy-start(bf16[1,1,192,128]{3,2,1,0:T(8,128)(2,1)} %param.6) | copy-start | bytes 147460
  48.4 5.2 %collective-permute-start.1 = (bf16[1792,128]{1,0:T(8,128)(2,1)S(1)}, bf16[1792,128]{1,0:T(8,128)(2,1)S(1)}, u32[]{:S(2)}, u32[]{:S(2)}) collective-permute-start(bf16[1792,128]{1,0:T(8,128)(2,1)S(1)} %get-tuple-element.26), channel_id=1, source_target_pairs={{0,1},{1,0},{2,3},{3,2},{4,5},{5,4},{6,7},{7,6},{8,9},{9,8},{10,11... | collective-permute-start | bytes 1376264 | tf_op jit(solution)/shard_map/ppermute | solution.py:285
  75.6 5.9 %collective-permute-start.2 = (bf16[32,32,128]{2,1,0:T(8,128)(2,1)S(1)}, bf16[32,32,128]{2,1,0:T(8,128)(2,1)S(1)}, u32[]{:S(2)}, u32[]{:S(2)}) collective-permute-start(bf16[32,32,128]{2,1,0:T(8,128)(2,1)S(1)} %slice.16.mine_ref), channel_id=1, source_target_pairs={{0,1},{1,0},{2,3},{3,2},{4,5},{5,4},{6,7},{7,6},{8,9},{9,8},{10,11... | collective-permute-start | bytes 786440 | tf_op jit(solution)/shard_map/ppermute | solution.py:285
  82.2 8.8 %all-to-all-start.3 = ((f32[4,56,128]{2,1,0:T(8,128)}), f32[4,56,128]{2,1,0:T(8,128)S(1)}, u32[]{:S(2)}, u32[]{:S(2)}) async-start(f32[4,56,128]{2,1,0:T(8,128)} %broadcast_in_dim.13), calls=%async_computation.3 | async-start | bytes 229376 | tf_op jit(solution)/shard_map/all_to_all | solution.py:273
  113.6 8.1 %collective-permute-start.3 = (bf16[1792,128]{1,0:T(8,128)(2,1)S(1)}, bf16[1792,128]{1,0:T(8,128)(2,1)S(1)}, u32[]{:S(2)}, u32[]{:S(2)}) collective-permute-start(bf16[1792,128]{1,0:T(8,128)(2,1)S(1)} %bitcast.27), channel_id=1, source_target_pairs={{0,1},{1,0},{2,3},{3,2},{4,5},{5,4},{6,7},{7,6},{8,9},{9,8},{10,11... | collective-permute-start | bytes 1376264 | tf_op jit(solution)/shard_map/ppermute | solution.py:285

commit v4 on v3

--- a/solution.py
+++ b/solution.py
@@ -64,7 +64,38 @@
     out_ref[pl.ds(992, 32), :] = jnp.zeros((32, LANES), F32)
 
 
-def spread_kernel(nbr_ref, f_ref, out_ref, src_ref, row_ref):
+def lanes_of(rows):
+    return lax.broadcasted_iota(jnp.int32, rows.shape, len(rows.shape) - 1)
+
+
+def pack(row_ref, out_ref):
+    extra = row_ref[:, 24:32]
+    for part in range(3):
+        rows = row_ref[:, part * 8 : part * 8 + 8]
+        moved = pltpu.roll(extra, C - 32 * part, 2)
+        out_ref[:, part * 8 : part * 8 + 8] = jnp.where(lanes_of(rows) < C, rows, moved).astype(BF16)
+
+
+def slot_groups(ref):
+    rows = ref[...].astype(F32)
+    count = rows.shape[1] // 8
+    groups = [rows[:, g * 8 : g * 8 + 8] for g in range(count)]
+    if count == 3:
+        lane = lanes_of(groups[0])
+        moved = [pltpu.roll(rows, 32 * (part + 1), 2) for part, rows in enumerate(groups)]
+        groups.append(jnp.where(lane < 32, moved[0], jnp.where(lane < 64, moved[1], moved[2])))
+    return groups
+
+
+def spread_kernel(nbr_hbm, f_hbm, out_ref, nbr_ref, f_ref, sems, src_ref, row_ref):
+    copies = [
+        pltpu.make_async_copy(nbr_hbm, nbr_ref, sems.at[0]),
+        pltpu.make_async_copy(f_hbm, f_ref, sems.at[1]),
+    ]
+    for copy in copies:
+        copy.start()
+    for copy in copies:
+        copy.wait()
     wide = jnp.concatenate([f_ref[...].astype(F32), jnp.zeros((LANES - C, VOX), F32)], axis=0)
     src_ref[...] = wide.T
     spread_rows(src_ref, row_ref, False)
@@ -89,27 +120,27 @@
 
 def route_kernel(core_ref, owner_ref, mine_ref, other_ref, out_ref, row_ref):
     core = core_ref[0]
+    owners, mine, other = slot_groups(owner_ref), slot_groups(mine_ref), slot_groups(other_ref)
     for group in range(4):
-        slots = slice(group * 8, group * 8 + 8)
-
-        def pick(ref):
-            return ref[...].astype(F32)[:, slots].reshape(256, LANES)
-
-        owner = pick(owner_ref)[:, C : C + 1].astype(jnp.int32)
+        owner = owners[group].reshape(256, LANES)[:, C : C + 1].astype(jnp.int32)
         place = lax.broadcasted_iota(jnp.int32, (256, 1), 0) & 7
         held = jnp.bitwise_and(owner, 1)
         spot = lax.shift_right_arithmetic(owner, 1) * 8 + place + jnp.where(held == core, 0, 256)
         spot = jnp.where(owner < 0, -1, spot)
-        source = jnp.concatenate([pick(mine_ref), pick(other_ref)], axis=0).astype(BF16)
-        row_ref[:, slots] = dot(one_hot(spot, 512), source).reshape(32, 8, LANES)
-    out_ref[...] = row_ref[...].astype(BF16)
-
-
-def fill_halo(pad_ref, halo_ref):
+        source = jnp.concatenate(
+            [mine[group].reshape(256, LANES), other[group].reshape(256, LANES)], axis=0
+        ).astype(BF16)
+        row_ref[:, group * 8 : group * 8 + 8] = dot(one_hot(spot, 512), source).reshape(32, 8, LANES)
+    pack(row_ref, out_ref)
+
+
+def fill_halo(pad_ref, packed_ref, row_ref):
+    for group, rows in enumerate(slot_groups(packed_ref)):
+        row_ref[:, group * 8 : group * 8 + 8] = rows
+    halo_ref = row_ref.reshape(SLOTS, LANES)
+
     def put(first, count, place):
-        pad_ref[pl.ds(first * COL, count * COL), :] = halo_ref[
-            pl.ds(place * COL, count * COL), :
-        ].astype(F32)
+        pad_ref[pl.ds(first * COL, count * COL), :] = halo_ref[pl.ds(place * COL, count * COL), :]
 
     put(0, 11, 0)
     for x in range(1, 8):
@@ -117,10 +148,8 @@
     put(89, 11, 25)
     for x in range(SIDE):
         start = ((x + 1) * 10 + 1) * COL
-        pad_ref[pl.ds(start, 8, stride=COL), :] = halo_ref[pl.ds(864 + x * 8, 8), :].astype(F32)
-        pad_ref[pl.ds(start + DEPTH + 1, 8, stride=COL), :] = halo_ref[
-            pl.ds(928 + x * 8, 8), :
-        ].astype(F32)
+        pad_ref[pl.ds(start, 8, stride=COL), :] = halo_ref[pl.ds(864 + x * 8, 8), :]
+        pad_ref[pl.ds(start + DEPTH + 1, 8, stride=COL), :] = halo_ref[pl.ds(928 + x * 8, 8), :]
 
 
 def shifted_columns(pad_ref, cols_ref):
@@ -149,7 +178,7 @@
 def forward_kernel(
     core_ref, f_ref, halo_ref, cot_ref, w_ref, dw_ref,
     grad_ref, patch_ref, keep_ref, send_ref,
-    pad_ref, cols_ref, act_ref, conv_ref, down_ref,
+    pad_ref, cols_ref, act_ref, row_ref, conv_ref, down_ref,
 ):
     wide = jnp.concatenate([f_ref[...].astype(F32), jnp.zeros((LANES - C, VOX), F32)], axis=0)
     own = wide.T
@@ -158,7 +187,7 @@
             pad_ref[pl.ds(((x + 1) * 10 + y + 1) * COL + 1, DEPTH), :] = own[
                 (x * 8 + y) * 16 : (x * 8 + y + 1) * 16, :
             ]
-    fill_halo(pad_ref, halo_ref)
+    fill_halo(pad_ref, halo_ref, row_ref)
     shifted_columns(pad_ref, cols_ref)
     act_ref[...] = conv(cols_ref, w_ref)
     back = dot(cot_ref[...], dw_ref[...], 0, 0)
@@ -200,12 +229,12 @@
 
 def side_kernel(grad_ref, patch_ref, dw_ref, send_ref, coarse_ref, src_ref, row_ref):
     src_ref[...] = grad_ref[...].astype(F32)
-    spread_rows(src_ref, row_ref, True)
-    send_ref[...] = row_ref[...].astype(BF16)
+    spread_rows(src_ref, row_ref.reshape(SLOTS, LANES), True)
+    pack(row_ref, send_ref)
     coarse_ref[...] = dot(dw_ref[...], patch_ref[...], 1, 1).astype(BF16)
 
 
-def backward_kernel(grad_ref, halo_ref, w_ref, out_ref, pad_ref, cols_ref, act_ref):
+def backward_kernel(grad_ref, halo_ref, w_ref, out_ref, pad_ref, cols_ref, act_ref, row_ref):
     for x in range(SIDE):
         for y in range(SIDE):
             base = ((x + 1) * 10 + y + 1) * COL
@@ -213,7 +242,7 @@
                 pad_ref[pl.ds(base + 1 + par, 8, stride=2), :] = grad_ref[
                     pl.ds((x * 8 + y) * 16 + par * 8, 8), :
                 ].astype(F32)
-    fill_halo(pad_ref, halo_ref)
+    fill_halo(pad_ref, halo_ref, row_ref)
     shifted_columns(pad_ref, cols_ref)
     full = conv(cols_ref, w_ref)
     for n in range(64):
@@ -279,18 +308,32 @@
     core = lax.axis_index("c").astype(jnp.int32).reshape(1)
     rows_shape = ((SLOTS, LANES), BF16)
     by_chip = (32, 32, LANES)
-    row_scratch = pltpu.VMEM((SLOTS, LANES), F32)
+    packed = (32, 24, LANES)
+    flat_scratch = pltpu.VMEM((SLOTS, LANES), F32)
+    slot_scratch = pltpu.VMEM(by_chip, F32)
 
     def swap(rows):
         return lax.ppermute(rows, "c", [(0, 1), (1, 0)])
 
-    (spread,) = call(spread_kernel, [rows_shape], [row_scratch, row_scratch], scalars=1, ins=1, name="spread")(
-        neighbours[0], block
-    )
+    (spread,) = pl.pallas_call(
+        spread_kernel,
+        out_shape=[pltpu.VMEM(*rows_shape)],
+        in_specs=[pl.BlockSpec(memory_space=pltpu.HBM)] * 2,
+        out_specs=[pl.BlockSpec(memory_space=pltpu.VMEM)],
+        scratch_shapes=[
+            pltpu.SMEM((1, 26), jnp.int32),
+            pltpu.VMEM((C, VOX), BF16),
+            pltpu.SemaphoreType.DMA((2,)),
+            flat_scratch,
+            flat_scratch,
+        ],
+        compiler_params=PARAMS,
+        name="spread",
+    )(neighbours[0], block)
     middle = here(trade(spread.reshape(by_chip), CHIPS))
-    route = call(route_kernel, [(by_chip, BF16)], [pltpu.VMEM(by_chip, F32)], scalars=1, ins=3, name="route")
+    route = call(route_kernel, [(packed, BF16)], [slot_scratch], scalars=1, ins=3, name="route")
     (routed,) = route(core, middle, middle, here(swap(middle)))
-    halo = trade(routed, CHIPS).reshape(SLOTS, LANES)
+    halo = trade(routed, CHIPS)
 
     taps = conv_weight.reshape(C, 27, C)
     pad = ((0, 0), (0, LANES - C), (0, LANES - C))
@@ -305,33 +348,33 @@
     grad, patch, keep, send = call(
         forward_kernel,
         [rows_shape, ((LANES, 8 * LANES), BF16), ((HALF_ROWS, LANES), F32), ((HALF_ROWS, LANES), BF16)],
-        [pad_scratch, cols_scratch, row_scratch, pltpu.VMEM((C, 21 * LANES), F32), pltpu.VMEM((C2, 8 * C), F32)],
+        [pad_scratch, cols_scratch, flat_scratch, slot_scratch, pltpu.VMEM((C, 21 * LANES), F32), pltpu.VMEM((C2, 8 * C), F32)],
         scalars=1,
         ins=5,
         name="forward",
     )(core, block, here(halo), cot, forward_w, down_w)
     spread2, coarse = call(
-        side_kernel, [rows_shape, ((C2, LANES), BF16, True)], [row_scratch, row_scratch], ins=3, name="side"
+        side_kernel, [(packed, BF16), ((C2, LANES), BF16, True)], [flat_scratch, slot_scratch], ins=3, name="side"
     )(grad, patch, down_w)
 
     pair = (keep + swap(send).astype(F32)).astype(BF16)
-    out = jnp.concatenate([spread2.reshape(by_chip), pair.reshape(32, 56, LANES)], axis=1)
+    out = jnp.concatenate([spread2, pair.reshape(32, 56, LANES)], axis=1)
     got = trade(out, CHIPS)
-    middle2 = got[:, :32]
-    part = jnp.sum(got[:, 32:].astype(F32), axis=0)
+    middle2 = got[:, :24]
+    part = jnp.sum(got[:, 24:].astype(F32), axis=0)
     other2, part = lax.optimization_barrier((swap(middle2), part))
     line = trade(jnp.broadcast_to(part, (4, 56, LANES)), "x")
     whole = jnp.sum(line, axis=0).astype(BF16)
     (routed2,) = route(core, middle, here(middle2), here(other2))
     out = jnp.concatenate([routed2, jnp.broadcast_to(whole, (32, 56, LANES))], axis=1)
     got = trade(out, CHIPS)
-    halo2 = got[:, :32].reshape(SLOTS, LANES)
-    mine = got[:, 32:].reshape(HALF_ROWS, LANES)
+    halo2 = got[:, :24]
+    mine = got[:, 24:].reshape(HALF_ROWS, LANES)
     theirs = swap(mine)
     (grad_features,) = call(
         backward_kernel,
         [((C, VOX), F32, True)],
-        [pad_scratch, cols_scratch, row_scratch],
+        [pad_scratch, cols_scratch, flat_scratch, slot_scratch],
         ins=3,
         name="backward",
     )(grad, here(halo2), backward_w)

time: 124 us -> 119 us (0.960)
  blocking collectives: 65.9 us -> 62.9 us
    all_to_all x3, blocking collectives: 65.9 us -> 62.9 us  [trade(): return lax.all_to_all(rows, axes, 0, 0, tiled=True)]
where the time goes in v4:
time: 119 us
  blocking collectives  62.9 us (53%)
  starting transfers between devices  24.6 us (21%)
  waiting for transfers between devices  12.2 us (10%)
  Pallas kernels  12.1 us (10%)
  local copies, waits for them, and re-layouts  6.13 us (5%)
    all_to_all x3, blocking collectives, trade(): return lax.all_to_all(rows, axes, 0, 0, tiled=True)  62.9 us
    ppermute x4, starting transfers between devices, swap(): return lax.ppermute(rows, 'c', [(0, 1), (1, 0)])  16.4 us
    all_to_all x2, waiting for transfers between devices, trade(): return lax.all_to_all(rows, axes, 0, 0, tiled=True)  9.55 us
    all_to_all x2, starting transfers between devices, trade(): return lax.all_to_all(rows, axes, 0, 0, tiled=True)  8.13 us
    pallas_call x1, Pallas kernels, shards(): call(forward_kernel, [rows_shape, ((LANES, 8 * LANES), BF16), ((HALF_ROWS...  3.77 us
    unnamed x17, local copies, waits for them, and re-layouts  3.19 us
    pallas_call x1, Pallas kernels, shards(): call(backward_kernel, [((C, VOX), F32, True)], [pad_scratch, cols_scratch...  2.97 us
    ppermute x4, waiting for transfers between devices, swap(): return lax.ppermute(rows, 'c', [(0, 1), (1, 0)])  2.66 us
  transfers between devices with their start and end apart: 6, of which 5 were waited for; matrix products, arithmetic and copies ran while one was open for 2% of the time, Pallas kernels for 4%

profile of v4, /device:TPU:1, one launch (start us, length us, event | category | flops | bytes accessed | tf_op | source)
XLA Modules:
  0.0 119.0 jit_solution(14853167120453930725)
XLA Ops:
  0.6 0.0 copy-start
  0.6 0.9 copy-done
  1.6 0.7 copy-done.3
  2.2 0.8 spread.1
  3.0 0.0 copy-start.6
  3.0 21.7 %all_to_all.25.owner_ref.mine_ref = bf16[32,32,128]{2,1,0:T(8,128)(2,1)S(1)} all-to-all(bf16[32,32,128]{2,1,0:T(8,128)(2,1)S(1)} %bitcast.26), channel_id=1, replica_groups=mesh['x'=4,'y'=4,'z'=8,'c'=2] {'y','z'}, dimensions={0} | all-to-all | bytes 524288 | tf_op jit(solution)/shard_map/all_to_all | solution.py:302
  24.7 3.7 %collective-permute-start = (bf16[32,32,128]{2,1,0:T(8,128)(2,1)S(1)}, bf16[32,32,128]{2,1,0:T(8,128)(2,1)S(1)}, u32[]{:S(2)}, u32[]{:S(2)}) collective-permute-start(bf16[32,32,128]{2,1,0:T(8,128)(2,1)S(1)} %all_to_all.25.owner_ref.mine_ref), channel_id=1, source_target_pairs={{0,1},{1,0},{2,3},{3,2},{4,5},{5,4},{6,7},{7,6},{8,9},{9,8},{10,11... | collective-permute-start | bytes 786440 | tf_op jit(solution)/shard_map/ppermute | solution.py:316
  28.4 1.2 collective-permute-done.other_ref
  29.6 1.3 %route.2 = bf16[32,24,128]{2,1,0:T(8,128)(2,1)} custom-call(s32[1]{0:T(128)} %bitcast.core_ref, bf16[32,32,128]{2,1,0:T(8,128)(2,1)S(1)} %all_to_all.25.owner_ref.mine_ref, bf16[32,32,128]{2,1,0:T(8,128)(2,1)S(1)} %all_to_all.25.owner_ref.mine_ref, bf16[32,32,128]{2,1,0:T(8,128)(2,1)S(1)} %collective-permute-done.other_ref), custom_call_target="tpu_custom_call" | custom-call | tf_op jit(solution)/shard_map/route/pallas_call | solution.py:335
  30.9 4.1 %all-to-all-start.1 = ((bf16[32,24,128]{2,1,0:T(8,128)(2,1)}), bf16[32,24,128]{2,1,0:T(8,128)(2,1)S(1)}, u32[]{:S(2)}, u32[]{:S(2)}) async-start(bf16[32,24,128]{2,1,0:T(8,128)(2,1)} %route.2), calls=%async_computation.1 | async-start | bytes 393216 | tf_op jit(solution)/shard_map/all_to_all | solution.py:302
  35.0 0.0 copy-done.6
  35.0 0.0 copy-start.5
  35.0 0.4 reshape.40
  35.5 0.1 pad.13
  35.6 0.1 copy.18
  35.6 0.4 copy-done.5
  36.1 0.3 copy.13
  36.4 0.0 copy-start.4
  36.5 0.3 copy.15
  36.8 0.5 copy-done.4
  37.2 0.2 pad.12.clone
  37.5 0.0 copy-start.1
  37.5 0.0 copy-start.2
  37.5 1.3 %pad.11 = bf16[27,128,128]{2,1,0:T(8,128)(2,1)S(1)} pad(bf16[27,96,96]{2,1,0:T(8,128)(2,1)} %bitcast.32, bf16[]{:T(256)} %constant.2.clone.1), padding=0_0x0_32x0_32 | pad | bytes 1382402 | tf_op jit(solution)/shard_map/jit(_pad)/pad | solution.py:340
  38.8 5.6 %all-to-all-done.1.halo_ref = bf16[32,24,128]{2,1,0:T(8,128)(2,1)S(1)} async-done(((bf16[32,24,128]{2,1,0:T(8,128)(2,1)}), bf16[32,24,128]{2,1,0:T(8,128)(2,1)S(1)}, u32[]{:S(2)}, u32[]{:S(2)}) %all-to-all-start.1) | async-done | bytes 196640 | tf_op jit(solution)/shard_map/all_to_all | solution.py:302
  44.4 0.0 copy-done.1
  44.4 0.0 copy-done.2
  44.4 3.8 %forward.1 = (bf16[1024,128]{1,0:T(8,128)(2,1)S(1)}, bf16[128,1024]{1,0:T(8,128)(2,1)S(1)}, f32[1792,128]{1,0:T(8,128)S(1)}, bf16[1792,128]{1,0:T(8,128)(2,1)S(1)}) custom-call(s32[1]{0:T(128)} %bitcast.core_ref, bf16[96,1024]{1,0:T(8,128)(2,1)S(1)} %bitcast.28, bf16[32,24,128]{2,1,0:T(8,128)(2,1)S(1)} %all-to-all-done.1.halo_ref, ...), custom_call_target="tpu_custom_call" | custom-call | tf_op jit(solution)/shard_map/forward/pallas_call | solution.py:348
  48.2 3.0 %collective-permute-start.1 = (bf16[1792,128]{1,0:T(8,128)(2,1)S(1)}, bf16[1792,128]{1,0:T(8,128)(2,1)S(1)}, u32[]{:S(2)}, u32[]{:S(2)}) collective-permute-start(bf16[1792,128]{1,0:T(8,128)(2,1)S(1)} %get-tuple-element.26), channel_id=1, source_target_pairs={{0,1},{1,0},{2,3},{3,2},{4,5},{5,4},{6,7},{7,6},{8,9},{9,8},{10,11... | collective-permute-start | bytes 1376264 | tf_op jit(solution)/shard_map/ppermute | solution.py:316
  51.2 0.9 side.1
  52.1 0.5 collective-permute-done.1
  52.6 0.1 add_convert_fusion
  52.7 0.1 pad_maximum_fusion
  52.8 20.5 %all_to_all.26 = bf16[32,80,128]{2,1,0:T(8,128)(2,1)S(1)} all-to-all(bf16[32,80,128]{2,1,0:T(8,128)(2,1)S(1)} %pad_maximum_fusion), channel_id=1, replica_groups=mesh['x'=4,'y'=4,'z'=8,'c'=2] {'y','z'}, dimensions={0} | all-to-all | bytes 1310720 | tf_op jit(solution)/shard_map/all_to_all | solution.py:302
  73.3 3.9 %collective-permute-start.2 = (bf16[32,24,128]{2,1,0:T(8,128)(2,1)S(1)}, bf16[32,24,128]{2,1,0:T(8,128)(2,1)S(1)}, u32[]{:S(2)}, u32[]{:S(2)}) collective-permute-start(bf16[32,24,128]{2,1,0:T(8,128)(2,1)S(1)} %slice.16.mine_ref), channel_id=1, source_target_pairs={{0,1},{1,0},{2,3},{3,2},{4,5},{5,4},{6,7},{7,6},{8,9},{9,8},{10,11... | collective-permute-start | bytes 589832 | tf_op jit(solution)/shard_map/ppermute | solution.py:316
  77.2 0.1 convert_reduce_fusion
  77.3 1.0 collective-permute-done.2.other_ref
  78.3 0.7 broadcast_in_dim.13
  78.9 4.0 %all-to-all-start.3 = ((f32[4,56,128]{2,1,0:T(8,128)}), f32[4,56,128]{2,1,0:T(8,128)S(1)}, u32[]{:S(2)}, u32[]{:S(2)}) async-start(f32[4,56,128]{2,1,0:T(8,128)} %broadcast_in_dim.13), calls=%async_computation.3 | async-start | bytes 229376 | tf_op jit(solution)/shard_map/all_to_all | solution.py:302
  82.9 0.7 route.3
  83.7 4.0 %all-to-all-done.3 = f32[4,56,128]{2,1,0:T(8,128)S(1)} async-done(((f32[4,56,128]{2,1,0:T(8,128)}), f32[4,56,128]{2,1,0:T(8,128)S(1)}, u32[]{:S(2)}, u32[]{:S(2)}) %all-to-all-start.3) | async-done | bytes 114720 | tf_op jit(solution)/shard_map/all_to_all | solution.py:302
  87.7 0.1 broadcast_in_dim.14
  87.8 0.1 pad_maximum_fusion.1
  87.8 20.8 %all_to_all.27 = bf16[32,80,128]{2,1,0:T(8,128)(2,1)S(1)} all-to-all(bf16[32,80,128]{2,1,0:T(8,128)(2,1)S(1)} %pad_maximum_fusion.1), channel_id=1, replica_groups=mesh['x'=4,'y'=4,'z'=8,'c'=2] {'y','z'}, dimensions={0} | all-to-all | bytes 1310720 | tf_op jit(solution)/shard_map/all_to_all | solution.py:302
  108.6 5.8 %collective-permute-start.3 = (bf16[1792,128]{1,0:T(8,128)(2,1)S(1)}, bf16[1792,128]{1,0:T(8,128)(2,1)S(1)}, u32[]{:S(2)}, u32[]{:S(2)}) collective-permute-start(bf16[1792,128]{1,0:T(8,128)(2,1)S(1)} %bitcast.24), channel_id=1, source_target_pairs={{0,1},{1,0},{2,3},{3,2},{4,5},{5,4},{6,7},{7,6},{8,9},{9,8},{10,11... | collective-permute-start | bytes 1376264 | tf_op jit(solution)/shard_map/ppermute | solution.py:316
  114.5 3.0 %backward.1 = f32[96,1024]{1,0:T(8,128)} custom-call(bf16[1024,128]{1,0:T(8,128)(2,1)S(1)} %get-tuple-element.21.grad_ref, bf16[32,24,128]{2,1,0:T(8,128)(2,1)S(1)} %slice.18.halo_ref, bf16[9,384,128]{2,1,0:T(8,128)(2,1)S(1)} %bitcast.23), custom_call_target="tpu_custom_call" | custom-call | tf_op jit(solution)/shard_map/backward/pallas_call | solution.py:374
  117.4 0.0 collective-permute-done.3.other_ref
  117.4 1.5 %finish.1 = (f32[96,2592]{1,0:T(8,128)}, f32[192,768]{1,0:T(8,128)}) custom-call(s32[1]{0:T(128)} %bitcast.core_ref, bf16[1792,128]{1,0:T(8,128)(2,1)S(1)} %bitcast.25, bf16[1792,128]{1,0:T(8,128)(2,1)S(1)} %collective-permute-done.3.other_ref), custom_call_target="tpu_custom_call" | custom-call | tf_op jit(solution)/shard_map/finish/pallas_call | solution.py:381
  (6 shorter events, 0.1 us)
Async XLA Ops:
  0.6 0.9 copy-start
  1.6 0.7 copy-start.3
  3.0 32.0 %copy-start.6 = (bf16[192,768]{1,0:T(8,128)(2,1)S(1)}, bf16[192,768]{1,0:T(8,128)(2,1)}, u32[]{:S(2)}) copy-start(bf16[192,768]{1,0:T(8,128)(2,1)} %param.8) | copy-start | bytes 884740
  24.7 4.9 %collective-permute-start = (bf16[32,32,128]{2,1,0:T(8,128)(2,1)S(1)}, bf16[32,32,128]{2,1,0:T(8,128)(2,1)S(1)}, u32[]{:S(2)}, u32[]{:S(2)}) collective-permute-start(bf16[32,32,128]{2,1,0:T(8,128)(2,1)S(1)} %all_to_all.25.owner_ref.mine_ref), channel_id=1, source_target_pairs={{0,1},{1,0},{2,3},{3,2},{4,5},{5,4},{6,7},{7,6},{8,9},{9,8},{10,11... | collective-permute-start | bytes 786440 | tf_op jit(solution)/shard_map/ppermute | solution.py:316
  30.9 13.5 %all-to-all-start.1 = ((bf16[32,24,128]{2,1,0:T(8,128)(2,1)}), bf16[32,24,128]{2,1,0:T(8,128)(2,1)S(1)}, u32[]{:S(2)}, u32[]{:S(2)}) async-start(bf16[32,24,128]{2,1,0:T(8,128)(2,1)} %route.2), calls=%async_computation.1 | async-start | bytes 393216 | tf_op jit(solution)/shard_map/all_to_all | solution.py:302
  35.0 1.0 copy-start.5
  36.4 0.8 copy-start.4
  37.5 6.9 %copy-start.1 = (bf16[1,1,96,1024]{3,2,1,0:T(8,128)(2,1)S(1)}, bf16[1,1,96,1024]{3,2,1,0:T(8,128)(2,1)}, u32[]{:S(2)}) copy-start(bf16[1,1,96,1024]{3,2,1,0:T(8,128)(2,1)} %param.5) | copy-start | bytes 589828
  37.5 6.9 %copy-start.2 = (bf16[1,1,192,128]{3,2,1,0:T(8,128)(2,1)S(1)}, bf16[1,1,192,128]{3,2,1,0:T(8,128)(2,1)}, u32[]{:S(2)}) copy-start(bf16[1,1,192,128]{3,2,1,0:T(8,128)(2,1)} %param.6) | copy-start | bytes 147460
  48.2 4.5 %collective-permute-start.1 = (bf16[1792,128]{1,0:T(8,128)(2,1)S(1)}, bf16[1792,128]{1,0:T(8,128)(2,1)S(1)}, u32[]{:S(2)}, u32[]{:S(2)}) collective-permute-start(bf16[1792,128]{1,0:T(8,128)(2,1)S(1)} %get-tuple-element.26), channel_id=1, source_target_pairs={{0,1},{1,0},{2,3},{3,2},{4,5},{5,4},{6,7},{7,6},{8,9},{9,8},{10,11... | collective-permute-start | bytes 1376264 | tf_op jit(solution)/shard_map/ppermute | solution.py:316
  73.3 5.0 %collective-permute-start.2 = (bf16[32,24,128]{2,1,0:T(8,128)(2,1)S(1)}, bf16[32,24,128]{2,1,0:T(8,128)(2,1)S(1)}, u32[]{:S(2)}, u32[]{:S(2)}) collective-permute-start(bf16[32,24,128]{2,1,0:T(8,128)(2,1)S(1)} %slice.16.mine_ref), channel_id=1, source_target_pairs={{0,1},{1,0},{2,3},{3,2},{4,5},{5,4},{6,7},{7,6},{8,9},{9,8},{10,11... | collective-permute-start | bytes 589832 | tf_op jit(solution)/shard_map/ppermute | solution.py:316
  78.9 8.8 %all-to-all-start.3 = ((f32[4,56,128]{2,1,0:T(8,128)}), f32[4,56,128]{2,1,0:T(8,128)S(1)}, u32[]{:S(2)}, u32[]{:S(2)}) async-start(f32[4,56,128]{2,1,0:T(8,128)} %broadcast_in_dim.13), calls=%async_computation.3 | async-start | bytes 229376 | tf_op jit(solution)/shard_map/all_to_all | solution.py:302
  108.6 8.8 %collective-permute-start.3 = (bf16[1792,128]{1,0:T(8,128)(2,1)S(1)}, bf16[1792,128]{1,0:T(8,128)(2,1)S(1)}, u32[]{:S(2)}, u32[]{:S(2)}) collective-permute-start(bf16[1792,128]{1,0:T(8,128)(2,1)S(1)} %bitcast.24), channel_id=1, source_target_pairs={{0,1},{1,0},{2,3},{3,2},{4,5},{5,4},{6,7},{7,6},{8,9},{9,8},{10,11... | collective-permute-start | bytes 1376264 | tf_op jit(solution)/shard_map/ppermute | solution.py:316

commit v5 on v4

--- a/solution.py
+++ b/solution.py
@@ -276,6 +276,10 @@
     return pltpu.with_memory_space_constraint(rows, pltpu.VMEM)
 
 
+def there(rows):
+    return pltpu.with_memory_space_constraint(rows, pltpu.HBM)
+
+
 def call(body, outs, scratch=(), scalars=0, ins=0, name=None):
     specs = [pl.BlockSpec(memory_space=pltpu.SMEM)] * scalars + [
         pl.BlockSpec(memory_space=pltpu.VMEM)
@@ -329,7 +333,7 @@
         ],
         compiler_params=PARAMS,
         name="spread",
-    )(neighbours[0], block)
+    )(there(neighbours[0]), there(block))
     middle = here(trade(spread.reshape(by_chip), CHIPS))
     route = call(route_kernel, [(packed, BF16)], [slot_scratch], scalars=1, ins=3, name="route")
     (routed,) = route(core, middle, middle, here(swap(middle)))
@@ -362,15 +366,13 @@
     got = trade(out, CHIPS)
     middle2 = got[:, :24]
     part = jnp.sum(got[:, 24:].astype(F32), axis=0)
-    other2, part = lax.optimization_barrier((swap(middle2), part))
-    line = trade(jnp.broadcast_to(part, (4, 56, LANES)), "x")
-    whole = jnp.sum(line, axis=0).astype(BF16)
-    (routed2,) = route(core, middle, here(middle2), here(other2))
-    out = jnp.concatenate([routed2, jnp.broadcast_to(whole, (32, 56, LANES))], axis=1)
-    got = trade(out, CHIPS)
-    halo2 = got[:, :24]
-    mine = got[:, 24:].reshape(HALF_ROWS, LANES)
-    theirs = swap(mine)
+    (routed2,) = route(core, middle, here(middle2), here(swap(middle2)))
+    routed2, part = lax.optimization_barrier((routed2, part))
+    halo2 = trade(routed2, CHIPS)
+    for step in (1, 2):
+        part = part + lax.ppermute(part, "x", [(i, i ^ step) for i in range(4)])
+    halo2, part = lax.optimization_barrier((halo2, part))
+    mine = trade(jnp.broadcast_to(part.astype(BF16), (32, 56, LANES)), CHIPS).reshape(HALF_ROWS, LANES)
     (grad_features,) = call(
         backward_kernel,
         [((C, VOX), F32, True)],
@@ -378,6 +380,8 @@
         ins=3,
         name="backward",
     )(grad, here(halo2), backward_w)
+    mine, grad_features = lax.optimization_barrier((mine, grad_features))
+    theirs = swap(mine)
     grad_conv, grad_down = call(
         finish_kernel, [((C, 27 * C), F32, True), ((C2, 8 * C), F32, True)], scalars=1, ins=2, name="finish"
     )(core, here(mine), here(theirs))

time: 119 us -> 121 us (1.017)
  blocking collectives: 62.9 us -> 42.1 us
  starting transfers between devices: 24.6 us -> 36.9 us
  waiting for transfers between devices: 12.2 us -> 22.9 us
  local copies, waits for them, and re-layouts: 6.13 us -> 4.6 us
    all_to_all x3 -> x2, blocking collectives: 62.9 us -> 42.1 us  [trade(): return lax.all_to_all(rows, axes, 0, 0, tiled=True)]
    all_to_all x2 -> x3, starting transfers between devices: 8.13 us -> 16.6 us  [trade(): return lax.all_to_all(rows, axes, 0, 0, tiled=True)]
    all_to_all x2 -> x3, waiting for transfers between devices: 9.55 us -> 15.5 us  [trade(): return lax.all_to_all(rows, axes, 0, 0, tiled=True)]
    ppermute x0 -> x2, starting transfers between devices: none -> 4.04 us  [shards(): part = part + lax.ppermute(part, 'x', [(i, i ^ step) for i in range(4)])]
    ppermute x0 -> x2, waiting for transfers between devices: none -> 3.28 us  [shards(): part = part + lax.ppermute(part, 'x', [(i, i ^ step) for i in range(4)])]
    unnamed x17 -> x13, local copies, waits for them, and re-layouts: 3.19 us -> 1.62 us
    ppermute x4, waiting for transfers between devices: 2.66 us -> 4.1 us  [swap(): return lax.ppermute(rows, 'c', [(0, 1), (1, 0)])]
  transfers between devices with their start and end apart: 6 -> 9, of which waited for: 5 -> 9; matrix products, arithmetic and copies ran while one was open for 2% -> 2% of each run, Pallas kernels for 4% -> 3%
where the time goes in v5:
time: 121 us
  blocking collectives  42.1 us (35%)
  starting transfers between devices  36.9 us (30%)
  waiting for transfers between devices  22.9 us (19%)
  Pallas kernels  13.1 us (11%)
  local copies, waits for them, and re-layouts  4.6 us (4%)
    all_to_all x2, blocking collectives, trade(): return lax.all_to_all(rows, axes, 0, 0, tiled=True)  42.1 us
    all_to_all x3, starting transfers between devices, trade(): return lax.all_to_all(rows, axes, 0, 0, tiled=True)  16.6 us
    ppermute x4, starting transfers between devices, swap(): return lax.ppermute(rows, 'c', [(0, 1), (1, 0)])  16.2 us
    all_to_all x3, waiting for transfers between devices, trade(): return lax.all_to_all(rows, axes, 0, 0, tiled=True)  15.5 us
    ppermute x4, waiting for transfers between devices, swap(): return lax.ppermute(rows, 'c', [(0, 1), (1, 0)])  4.1 us
    ppermute x2, starting transfers between devices, shards(): part = part + lax.ppermute(part, 'x', [(i, i ^ step) for i in range(4)])  4.04 us
    pallas_call x1, Pallas kernels, shards(): call(forward_kernel, [rows_shape, ((LANES, 8 * LANES), BF16), ((HALF_ROWS...  3.78 us
    ppermute x2, waiting for transfers between devices, shards(): part = part + lax.ppermute(part, 'x', [(i, i ^ step) for i in range(4)])  3.28 us
  transfers between devices with their start and end apart: 9, of which 9 were waited for; matrix products, arithmetic and copies ran while one was open for 2% of the time, Pallas kernels for 3%

profile of v5, /device:TPU:1, one launch (start us, length us, event | category | flops | bytes accessed | tf_op | source)
XLA Modules:
  0.0 120.7 jit_solution(5183677863655983516)
XLA Ops:
  0.6 1.2 spread.1
  1.8 0.0 copy-start.4
  1.8 21.7 %all_to_all.25.owner_ref.mine_ref = bf16[32,32,128]{2,1,0:T(8,128)(2,1)S(1)} all-to-all(bf16[32,32,128]{2,1,0:T(8,128)(2,1)S(1)} %bitcast.26), channel_id=1, replica_groups=mesh['x'=4,'y'=4,'z'=8,'c'=2] {'y','z'}, dimensions={0} | all-to-all | bytes 524288 | tf_op jit(solution)/shard_map/all_to_all | solution.py:306
  23.5 3.7 %collective-permute-start = (bf16[32,32,128]{2,1,0:T(8,128)(2,1)S(1)}, bf16[32,32,128]{2,1,0:T(8,128)(2,1)S(1)}, u32[]{:S(2)}, u32[]{:S(2)}) collective-permute-start(bf16[32,32,128]{2,1,0:T(8,128)(2,1)S(1)} %all_to_all.25.owner_ref.mine_ref), channel_id=1, source_target_pairs={{0,1},{1,0},{2,3},{3,2},{4,5},{5,4},{6,7},{7,6},{8,9},{9,8},{10,11... | collective-permute-start | bytes 786440 | tf_op jit(solution)/shard_map/ppermute | solution.py:320
  27.2 1.2 collective-permute-done.other_ref
  28.4 1.3 %route.2 = bf16[32,24,128]{2,1,0:T(8,128)(2,1)} custom-call(s32[1]{0:T(128)} %bitcast.core_ref, bf16[32,32,128]{2,1,0:T(8,128)(2,1)S(1)} %all_to_all.25.owner_ref.mine_ref, bf16[32,32,128]{2,1,0:T(8,128)(2,1)S(1)} %all_to_all.25.owner_ref.mine_ref, bf16[32,32,128]{2,1,0:T(8,128)(2,1)S(1)} %collective-permute-done.other_ref), custom_call_target="tpu_custom_call" | custom-call | tf_op jit(solution)/shard_map/route/pallas_call | solution.py:339
  29.7 4.1 %all-to-all-start.1 = ((bf16[32,24,128]{2,1,0:T(8,128)(2,1)}), bf16[32,24,128]{2,1,0:T(8,128)(2,1)S(1)}, u32[]{:S(2)}, u32[]{:S(2)}) async-start(bf16[32,24,128]{2,1,0:T(8,128)(2,1)} %route.2), calls=%async_computation.1 | async-start | bytes 393216 | tf_op jit(solution)/shard_map/all_to_all | solution.py:306
  33.8 0.0 copy-done.4
  33.8 0.0 copy-start.3
  33.8 0.4 reshape.40
  34.3 0.1 pad.13
  34.4 0.1 copy.16
  34.4 0.4 copy-done.3
  34.9 0.3 copy.11
  35.2 0.0 copy-start.2
  35.3 0.3 copy.13
  35.6 0.5 copy-done.2
  36.0 0.2 pad.12.clone
  36.3 0.0 copy-start
  36.3 0.0 copy-start.1
  36.3 1.3 %pad.11 = bf16[27,128,128]{2,1,0:T(8,128)(2,1)S(1)} pad(bf16[27,96,96]{2,1,0:T(8,128)(2,1)} %bitcast.31, bf16[]{:T(256)} %constant.2.clone.1), padding=0_0x0_32x0_32 | pad | bytes 1382402 | tf_op jit(solution)/shard_map/jit(_pad)/pad | solution.py:344
  37.6 5.6 %all-to-all-done.1.halo_ref = bf16[32,24,128]{2,1,0:T(8,128)(2,1)S(1)} async-done(((bf16[32,24,128]{2,1,0:T(8,128)(2,1)}), bf16[32,24,128]{2,1,0:T(8,128)(2,1)S(1)}, u32[]{:S(2)}, u32[]{:S(2)}) %all-to-all-start.1) | async-done | bytes 196640 | tf_op jit(solution)/shard_map/all_to_all | solution.py:306
  43.2 0.0 copy-done
  43.2 0.0 copy-done.1
  43.2 3.8 %forward.1 = (bf16[1024,128]{1,0:T(8,128)(2,1)S(1)}, bf16[128,1024]{1,0:T(8,128)(2,1)S(1)}, f32[1792,128]{1,0:T(8,128)S(1)}, bf16[1792,128]{1,0:T(8,128)(2,1)S(1)}) custom-call(s32[1]{0:T(128)} %bitcast.core_ref, bf16[96,1024]{1,0:T(8,128)(2,1)S(1)} %bitcast.28, bf16[32,24,128]{2,1,0:T(8,128)(2,1)S(1)} %all-to-all-done.1.halo_ref, ...), custom_call_target="tpu_custom_call" | custom-call | tf_op jit(solution)/shard_map/forward/pallas_call | solution.py:352
  47.0 3.0 %collective-permute-start.1 = (bf16[1792,128]{1,0:T(8,128)(2,1)S(1)}, bf16[1792,128]{1,0:T(8,128)(2,1)S(1)}, u32[]{:S(2)}, u32[]{:S(2)}) collective-permute-start(bf16[1792,128]{1,0:T(8,128)(2,1)S(1)} %get-tuple-element.30), channel_id=1, source_target_pairs={{0,1},{1,0},{2,3},{3,2},{4,5},{5,4},{6,7},{7,6},{8,9},{9,8},{10,11... | collective-permute-start | bytes 1376264 | tf_op jit(solution)/shard_map/ppermute | solution.py:320
  50.0 0.9 side.1
  50.9 0.5 collective-permute-done.1
  51.5 0.1 add_convert_fusion
  51.5 0.1 pad_maximum_fusion
  51.6 20.5 %all_to_all.26 = bf16[32,80,128]{2,1,0:T(8,128)(2,1)S(1)} all-to-all(bf16[32,80,128]{2,1,0:T(8,128)(2,1)S(1)} %pad_maximum_fusion), channel_id=1, replica_groups=mesh['x'=4,'y'=4,'z'=8,'c'=2] {'y','z'}, dimensions={0} | all-to-all | bytes 1310720 | tf_op jit(solution)/shard_map/all_to_all | solution.py:306
  72.1 3.9 %collective-permute-start.2 = (bf16[32,24,128]{2,1,0:T(8,128)(2,1)S(1)}, bf16[32,24,128]{2,1,0:T(8,128)(2,1)S(1)}, u32[]{:S(2)}, u32[]{:S(2)}) collective-permute-start(bf16[32,24,128]{2,1,0:T(8,128)(2,1)S(1)} %slice.8.mine_ref), channel_id=1, source_target_pairs={{0,1},{1,0},{2,3},{3,2},{4,5},{5,4},{6,7},{7,6},{8,9},{9,8},{10,11... | collective-permute-start | bytes 589832 | tf_op jit(solution)/shard_map/ppermute | solution.py:320
  76.0 0.1 convert_reduce_fusion
  76.1 1.0 collective-permute-done.2.other_ref
  77.1 1.4 %route.3 = bf16[32,24,128]{2,1,0:T(8,128)(2,1)} custom-call(s32[1]{0:T(128)} %bitcast.core_ref, bf16[32,32,128]{2,1,0:T(8,128)(2,1)S(1)} %all_to_all.25.owner_ref.mine_ref, bf16[32,24,128]{2,1,0:T(8,128)(2,1)S(1)} %slice.8.mine_ref, bf16[32,24,128]{2,1,0:T(8,128)(2,1)S(1)} %collective-permute-done.2.other_ref), custom_call_target="tpu_custom_call" | custom-call | tf_op jit(solution)/shard_map/route/pallas_call | solution.py:369
  78.5 5.3 %all-to-all-start.3 = ((bf16[32,24,128]{2,1,0:T(8,128)(2,1)}), bf16[32,24,128]{2,1,0:T(8,128)(2,1)S(1)}, u32[]{:S(2)}, u32[]{:S(2)}) async-start(bf16[32,24,128]{2,1,0:T(8,128)(2,1)} %route.3), calls=%async_computation.3 | async-start | bytes 393216 | tf_op jit(solution)/shard_map/all_to_all | solution.py:306
  83.8 1.3 %collective-permute-start.3 = (f32[56,128]{1,0:T(8,128)S(1)}, f32[56,128]{1,0:T(8,128)S(1)}, u32[]{:S(2)}, u32[]{:S(2)}) collective-permute-start(f32[56,128]{1,0:T(8,128)S(1)} %convert_reduce_fusion), channel_id=1, source_target_pairs={{0,64},{64,0},{128,192},{192,128},{1,65},{65,1},{129,193},{193,129... | collective-permute-start | bytes 86024 | tf_op jit(solution)/shard_map/ppermute | solution.py:373
  85.1 1.5 %collective-permute-done.3 = f32[56,128]{1,0:T(8,128)S(1)} collective-permute-done((f32[56,128]{1,0:T(8,128)S(1)}, f32[56,128]{1,0:T(8,128)S(1)}, u32[]{:S(2)}, u32[]{:S(2)}) %collective-permute-start.3) | collective-permute-done | bytes 28704 | tf_op jit(solution)/shard_map/ppermute | solution.py:373
  86.6 2.7 %collective-permute-start.4 = (f32[56,128]{1,0:T(8,128)S(1)}, f32[56,128]{1,0:T(8,128)S(1)}, u32[]{:S(2)}, u32[]{:S(2)}) collective-permute-start(f32[56,128]{1,0:T(8,128)S(1)} %add.16), channel_id=1, source_target_pairs={{0,128},{64,192},{128,0},{192,64},{1,129},{65,193},{129,1},{193,65... | collective-permute-start | bytes 86024 | tf_op jit(solution)/shard_map/ppermute | solution.py:373
  89.3 1.8 %collective-permute-done.4 = f32[56,128]{1,0:T(8,128)S(1)} collective-permute-done((f32[56,128]{1,0:T(8,128)S(1)}, f32[56,128]{1,0:T(8,128)S(1)}, u32[]{:S(2)}, u32[]{:S(2)}) %collective-permute-start.4) | collective-permute-done | bytes 28704 | tf_op jit(solution)/shard_map/ppermute | solution.py:373
  91.1 2.0 %all-to-all-done.3.halo_ref = bf16[32,24,128]{2,1,0:T(8,128)(2,1)S(1)} async-done(((bf16[32,24,128]{2,1,0:T(8,128)(2,1)}), bf16[32,24,128]{2,1,0:T(8,128)(2,1)S(1)}, u32[]{:S(2)}, u32[]{:S(2)}) %all-to-all-start.3) | async-done | bytes 196640 | tf_op jit(solution)/shard_map/all_to_all | solution.py:306
  93.2 0.8 broadcast_in_dim.10
  94.0 7.2 %all-to-all-start.4 = ((bf16[32,56,128]{2,1,0:T(8,128)(2,1)}), bf16[32,56,128]{2,1,0:T(8,128)(2,1)S(1)}, u32[]{:S(2)}, u32[]{:S(2)}) async-start(bf16[32,56,128]{2,1,0:T(8,128)(2,1)} %broadcast_in_dim.10), calls=%async_computation.4 | async-start | bytes 917504 | tf_op jit(solution)/shard_map/all_to_all | solution.py:306
  101.2 3.0 %backward.1 = f32[96,1024]{1,0:T(8,128)} custom-call(bf16[1024,128]{1,0:T(8,128)(2,1)S(1)} %get-tuple-element.25.grad_ref, bf16[32,24,128]{2,1,0:T(8,128)(2,1)S(1)} %all-to-all-done.3.halo_ref, bf16[9,384,128]{2,1,0:T(8,128)(2,1)S(1)} %bitcast.23), custom_call_target="tpu_custom_call" | custom-call | tf_op jit(solution)/shard_map/backward/pallas_call | solution.py:376
  104.2 7.9 %all-to-all-done.4 = bf16[32,56,128]{2,1,0:T(8,128)(2,1)S(1)} async-done(((bf16[32,56,128]{2,1,0:T(8,128)(2,1)}), bf16[32,56,128]{2,1,0:T(8,128)(2,1)S(1)}, u32[]{:S(2)}, u32[]{:S(2)}) %all-to-all-start.4) | async-done | bytes 458784 | tf_op jit(solution)/shard_map/all_to_all | solution.py:306
  112.1 5.6 %collective-permute-start.5 = (bf16[1792,128]{1,0:T(8,128)(2,1)S(1)}, bf16[1792,128]{1,0:T(8,128)(2,1)S(1)}, u32[]{:S(2)}, u32[]{:S(2)}) collective-permute-start(bf16[1792,128]{1,0:T(8,128)(2,1)S(1)} %bitcast.24), channel_id=1, source_target_pairs={{0,1},{1,0},{2,3},{3,2},{4,5},{5,4},{6,7},{7,6},{8,9},{9,8},{10,11... | collective-permute-start | bytes 1376264 | tf_op jit(solution)/shard_map/ppermute | solution.py:320
  117.7 1.4 %collective-permute-done.5.other_ref = bf16[1792,128]{1,0:T(8,128)(2,1)S(1)} collective-permute-done((bf16[1792,128]{1,0:T(8,128)(2,1)S(1)}, bf16[1792,128]{1,0:T(8,128)(2,1)S(1)}, u32[]{:S(2)}, u32[]{:S(2)}) %collective-permute-start.5) | collective-permute-done | bytes 458784 | tf_op jit(solution)/shard_map/ppermute | solution.py:320
  119.1 1.5 %finish.1 = (f32[96,2592]{1,0:T(8,128)}, f32[192,768]{1,0:T(8,128)}) custom-call(s32[1]{0:T(128)} %bitcast.core_ref, bf16[1792,128]{1,0:T(8,128)(2,1)S(1)} %bitcast.25, bf16[1792,128]{1,0:T(8,128)(2,1)S(1)} %collective-permute-done.5.other_ref), custom_call_target="tpu_custom_call" | custom-call | tf_op jit(solution)/shard_map/finish/pallas_call | solution.py:385
  (4 shorter events, 0.1 us)
Async XLA Ops:
  1.8 32.0 %copy-start.4 = (bf16[192,768]{1,0:T(8,128)(2,1)S(1)}, bf16[192,768]{1,0:T(8,128)(2,1)}, u32[]{:S(2)}) copy-start(bf16[192,768]{1,0:T(8,128)(2,1)} %param.8) | copy-start | bytes 884740
  23.5 4.9 %collective-permute-start = (bf16[32,32,128]{2,1,0:T(8,128)(2,1)S(1)}, bf16[32,32,128]{2,1,0:T(8,128)(2,1)S(1)}, u32[]{:S(2)}, u32[]{:S(2)}) collective-permute-start(bf16[32,32,128]{2,1,0:T(8,128)(2,1)S(1)} %all_to_all.25.owner_ref.mine_ref), channel_id=1, source_target_pairs={{0,1},{1,0},{2,3},{3,2},{4,5},{5,4},{6,7},{7,6},{8,9},{9,8},{10,11... | collective-permute-start | bytes 786440 | tf_op jit(solution)/shard_map/ppermute | solution.py:320
  29.7 13.5 %all-to-all-start.1 = ((bf16[32,24,128]{2,1,0:T(8,128)(2,1)}), bf16[32,24,128]{2,1,0:T(8,128)(2,1)S(1)}, u32[]{:S(2)}, u32[]{:S(2)}) async-start(bf16[32,24,128]{2,1,0:T(8,128)(2,1)} %route.2), calls=%async_computation.1 | async-start | bytes 393216 | tf_op jit(solution)/shard_map/all_to_all | solution.py:306
  33.8 1.0 copy-start.3
  35.2 0.8 copy-start.2
  36.3 6.9 %copy-start = (bf16[1,1,96,1024]{3,2,1,0:T(8,128)(2,1)S(1)}, bf16[1,1,96,1024]{3,2,1,0:T(8,128)(2,1)}, u32[]{:S(2)}) copy-start(bf16[1,1,96,1024]{3,2,1,0:T(8,128)(2,1)} %param.5) | copy-start | bytes 589828
  36.3 6.9 %copy-start.1 = (bf16[1,1,192,128]{3,2,1,0:T(8,128)(2,1)S(1)}, bf16[1,1,192,128]{3,2,1,0:T(8,128)(2,1)}, u32[]{:S(2)}) copy-start(bf16[1,1,192,128]{3,2,1,0:T(8,128)(2,1)} %param.6) | copy-start | bytes 147460
  47.0 4.5 %collective-permute-start.1 = (bf16[1792,128]{1,0:T(8,128)(2,1)S(1)}, bf16[1792,128]{1,0:T(8,128)(2,1)S(1)}, u32[]{:S(2)}, u32[]{:S(2)}) collective-permute-start(bf16[1792,128]{1,0:T(8,128)(2,1)S(1)} %get-tuple-element.30), channel_id=1, source_target_pairs={{0,1},{1,0},{2,3},{3,2},{4,5},{5,4},{6,7},{7,6},{8,9},{9,8},{10,11... | collective-permute-start | bytes 1376264 | tf_op jit(solution)/shard_map/ppermute | solution.py:320
  72.1 5.0 %collective-permute-start.2 = (bf16[32,24,128]{2,1,0:T(8,128)(2,1)S(1)}, bf16[32,24,128]{2,1,0:T(8,128)(2,1)S(1)}, u32[]{:S(2)}, u32[]{:S(2)}) collective-permute-start(bf16[32,24,128]{2,1,0:T(8,128)(2,1)S(1)} %slice.8.mine_ref), channel_id=1, source_target_pairs={{0,1},{1,0},{2,3},{3,2},{4,5},{5,4},{6,7},{7,6},{8,9},{9,8},{10,11... | collective-permute-start | bytes 589832 | tf_op jit(solution)/shard_map/ppermute | solution.py:320
  78.5 14.7 %all-to-all-start.3 = ((bf16[32,24,128]{2,1,0:T(8,128)(2,1)}), bf16[32,24,128]{2,1,0:T(8,128)(2,1)S(1)}, u32[]{:S(2)}, u32[]{:S(2)}) async-start(bf16[32,24,128]{2,1,0:T(8,128)(2,1)} %route.3), calls=%async_computation.3 | async-start | bytes 393216 | tf_op jit(solution)/shard_map/all_to_all | solution.py:306
  83.8 2.8 %collective-permute-start.3 = (f32[56,128]{1,0:T(8,128)S(1)}, f32[56,128]{1,0:T(8,128)S(1)}, u32[]{:S(2)}, u32[]{:S(2)}) collective-permute-start(f32[56,128]{1,0:T(8,128)S(1)} %convert_reduce_fusion), channel_id=1, source_target_pairs={{0,64},{64,0},{128,192},{192,128},{1,65},{65,1},{129,193},{193,129... | collective-permute-start | bytes 86024 | tf_op jit(solution)/shard_map/ppermute | solution.py:373
  86.6 4.5 %collective-permute-start.4 = (f32[56,128]{1,0:T(8,128)S(1)}, f32[56,128]{1,0:T(8,128)S(1)}, u32[]{:S(2)}, u32[]{:S(2)}) collective-permute-start(f32[56,128]{1,0:T(8,128)S(1)} %add.16), channel_id=1, source_target_pairs={{0,128},{64,192},{128,0},{192,64},{1,129},{65,193},{129,1},{193,65... | collective-permute-start | bytes 86024 | tf_op jit(solution)/shard_map/ppermute | solution.py:373
  94.0 18.1 %all-to-all-start.4 = ((bf16[32,56,128]{2,1,0:T(8,128)(2,1)}), bf16[32,56,128]{2,1,0:T(8,128)(2,1)S(1)}, u32[]{:S(2)}, u32[]{:S(2)}) async-start(bf16[32,56,128]{2,1,0:T(8,128)(2,1)} %broadcast_in_dim.10), calls=%async_computation.4 | async-start | bytes 917504 | tf_op jit(solution)/shard_map/all_to_all | solution.py:306
  112.1 7.1 %collective-permute-start.5 = (bf16[1792,128]{1,0:T(8,128)(2,1)S(1)}, bf16[1792,128]{1,0:T(8,128)(2,1)S(1)}, u32[]{:S(2)}, u32[]{:S(2)}) collective-permute-start(bf16[1792,128]{1,0:T(8,128)(2,1)S(1)} %bitcast.24), channel_id=1, source_target_pairs={{0,1},{1,0},{2,3},{3,2},{4,5},{5,4},{6,7},{7,6},{8,9},{9,8},{10,11... | collective-permute-start | bytes 1376264 | tf_op jit(solution)/shard_map/ppermute | solution.py:320

commit v6 on v4

--- a/solution.py
+++ b/solution.py
@@ -1,5 +1,6 @@
 import jax
 import jax.numpy as jnp
+import numpy as np
 from jax import lax
 from jax.experimental import pallas as pl
 from jax.experimental.pallas import tpu as pltpu
@@ -11,10 +12,11 @@
 DEPTH = 16
 VOX = 1024
 LANES = 128
-SLOTS = 1024
+SLOTS = 992
 COL = 24
-HALF_ROWS = 1792
-CONV_ROWS = 1008
+MAIN_ROWS = 1536
+HALF_ROWS = MAIN_ROWS + 128
+CONV_CHIPS = 20
 EPSILON = 1e-06
 F32 = jnp.float32
 BF16 = jnp.bfloat16
@@ -35,6 +37,22 @@
 def direction(ex, ey, ez):
     place = ((ex + 1) * 3 + ey + 1) * 3 + ez + 1
     return place - (place > 13)
+
+
+def direction_table():
+    table = np.full((32, LANES), -1, np.int32)
+
+    def put(slot, px, py, pz):
+        steps = (side(px, SIDE)[0], side(py, SIDE)[0], side(pz, DEPTH)[0])
+        table[slot // 31, slot % 31] = direction(*steps)
+
+    for place, (px, py) in enumerate(RIM):
+        for pz in range(DEPTH + 2):
+            put(place * COL + pz, px, py, pz)
+    for n in range(64):
+        put(864 + n, n // 8 + 1, n % 8 + 1, 0)
+        put(928 + n, n // 8 + 1, n % 8 + 1, DEPTH + 1)
+    return table
 
 
 def one_hot(index, count):
@@ -61,7 +79,16 @@
     for x in range(SIDE):
         out_ref[pl.ds(864 + x * 8, 8), :] = src_ref[pl.ds(x * 128 + 15, 8, stride=DEPTH), :]
         out_ref[pl.ds(928 + x * 8, 8), :] = src_ref[pl.ds(x * 128, 8, stride=DEPTH), :]
-    out_ref[pl.ds(992, 32), :] = jnp.zeros((32, LANES), F32)
+
+
+def to_chips(flat_ref, row_ref):
+    for chip in range(32):
+        row_ref[chip, 0:31, :] = flat_ref[pl.ds(chip * 31, 31), :]
+
+
+def from_chips(row_ref, flat_ref):
+    for chip in range(32):
+        flat_ref[pl.ds(chip * 31, 31), :] = row_ref[chip, 0:31, :]
 
 
 def lanes_of(rows):
@@ -78,19 +105,18 @@
 
 def slot_groups(ref):
     rows = ref[...].astype(F32)
-    count = rows.shape[1] // 8
-    groups = [rows[:, g * 8 : g * 8 + 8] for g in range(count)]
-    if count == 3:
-        lane = lanes_of(groups[0])
-        moved = [pltpu.roll(rows, 32 * (part + 1), 2) for part, rows in enumerate(groups)]
-        groups.append(jnp.where(lane < 32, moved[0], jnp.where(lane < 64, moved[1], moved[2])))
+    groups = [rows[:, g * 8 : g * 8 + 8] for g in range(3)]
+    lane = lanes_of(groups[0])
+    moved = [pltpu.roll(rows, 32 * (part + 1), 2) for part, rows in enumerate(groups)]
+    groups.append(jnp.where(lane < 32, moved[0], jnp.where(lane < 64, moved[1], moved[2])))
     return groups
 
 
-def spread_kernel(nbr_hbm, f_hbm, out_ref, nbr_ref, f_ref, sems, src_ref, row_ref):
+def spread_kernel(nbr_hbm, f_hbm, table_hbm, out_ref, nbr_ref, f_ref, table_ref, sems, src_ref, flat_ref, row_ref):
     copies = [
         pltpu.make_async_copy(nbr_hbm, nbr_ref, sems.at[0]),
         pltpu.make_async_copy(f_hbm, f_ref, sems.at[1]),
+        pltpu.make_async_copy(table_hbm, table_ref, sems.at[2]),
     ]
     for copy in copies:
         copy.start()
@@ -98,31 +124,24 @@
         copy.wait()
     wide = jnp.concatenate([f_ref[...].astype(F32), jnp.zeros((LANES - C, VOX), F32)], axis=0)
     src_ref[...] = wide.T
-    spread_rows(src_ref, row_ref, False)
-
-    def owner(ex, ey, ez):
-        return nbr_ref[0, direction(ex, ey, ez)].astype(F32)
-
-    lane = lax.broadcasted_iota(jnp.int32, (COL, LANES), 1)
-    z = lax.broadcasted_iota(jnp.int32, (COL, LANES), 0)
-    for place, (px, py) in enumerate(RIM):
-        ex, ey = side(px, SIDE)[0], side(py, SIDE)[0]
-        low, mid, high = (owner(ex, ey, ez) for ez in (-1, 0, 1))
-        held = jnp.where(z == 0, low, jnp.where(z < 17, mid, jnp.where(z == 17, high, -1.0)))
-        rows = pl.ds(place * COL, COL)
-        row_ref[rows, :] = jnp.where(lane >= C, held, row_ref[rows, :])
-    lane = lax.broadcasted_iota(jnp.int32, (64, LANES), 1)
-    for first, ez in ((864, -1), (928, 1)):
-        rows = pl.ds(first, 64)
-        row_ref[rows, :] = jnp.where(lane >= C, owner(0, 0, ez), row_ref[rows, :])
-    out_ref[...] = row_ref[...].astype(BF16)
+    spread_rows(src_ref, flat_ref, False)
+    to_chips(flat_ref, row_ref)
+    table = table_ref[...]
+    owner = jnp.full((32, LANES), -1, jnp.int32)
+    for number in range(26):
+        owner = jnp.where(table == number, nbr_ref[0, number], owner)
+    row_ref[:, 31:32, :] = owner.astype(F32).reshape(32, 1, LANES)
+    pack(row_ref, out_ref)
 
 
 def route_kernel(core_ref, owner_ref, mine_ref, other_ref, out_ref, row_ref):
     core = core_ref[0]
-    owners, mine, other = slot_groups(owner_ref), slot_groups(mine_ref), slot_groups(other_ref)
+    mine, other = slot_groups(mine_ref), slot_groups(other_ref)
+    owners = jnp.broadcast_to(slot_groups(owner_ref)[3][:, 7:8, :], (32, 8, LANES))
+    slot = lax.broadcasted_iota(jnp.int32, (32, 8, LANES), 1)
     for group in range(4):
-        owner = owners[group].reshape(256, LANES)[:, C : C + 1].astype(jnp.int32)
+        held = jnp.where(lanes_of(owners) == slot + group * 8, owners, 0.0)
+        owner = jnp.sum(held, axis=2, keepdims=True).reshape(256, 1).astype(jnp.int32)
         place = lax.broadcasted_iota(jnp.int32, (256, 1), 0) & 7
         held = jnp.bitwise_and(owner, 1)
         spot = lax.shift_right_arithmetic(owner, 1) * 8 + place + jnp.where(held == core, 0, 256)
@@ -134,10 +153,10 @@
     pack(row_ref, out_ref)
 
 
-def fill_halo(pad_ref, packed_ref, row_ref):
+def fill_halo(pad_ref, packed_ref, row_ref, halo_ref):
     for group, rows in enumerate(slot_groups(packed_ref)):
         row_ref[:, group * 8 : group * 8 + 8] = rows
-    halo_ref = row_ref.reshape(SLOTS, LANES)
+    from_chips(row_ref, halo_ref)
 
     def put(first, count, place):
         pad_ref[pl.ds(first * COL, count * COL), :] = halo_ref[pl.ds(place * COL, count * COL), :]
@@ -178,7 +197,7 @@
 def forward_kernel(
     core_ref, f_ref, halo_ref, cot_ref, w_ref, dw_ref,
     grad_ref, patch_ref, keep_ref, send_ref,
-    pad_ref, cols_ref, act_ref, row_ref, conv_ref, down_ref,
+    pad_ref, cols_ref, act_ref, row_ref, flat_ref, conv_ref, down_ref, free_ref,
 ):
     wide = jnp.concatenate([f_ref[...].astype(F32), jnp.zeros((LANES - C, VOX), F32)], axis=0)
     own = wide.T
@@ -187,7 +206,7 @@
             pad_ref[pl.ds(((x + 1) * 10 + y + 1) * COL + 1, DEPTH), :] = own[
                 (x * 8 + y) * 16 : (x * 8 + y + 1) * 16, :
             ]
-    fill_halo(pad_ref, halo_ref, row_ref)
+    fill_halo(pad_ref, halo_ref, row_ref, flat_ref)
     shifted_columns(pad_ref, cols_ref)
     act_ref[...] = conv(cols_ref, w_ref)
     back = dot(cot_ref[...], dw_ref[...], 0, 0)
@@ -216,25 +235,32 @@
         down_ref[:, pl.ds(j * C, C)] = part[:, j * LANES : j * LANES + C]
     core = core_ref[0]
     for ref, half in ((keep_ref, core), (send_ref, 1 - core)):
-        for lt in range(21):
+        for lt in range(20):
             ref[pl.ds(lt * 48, 48), :] = conv_ref[
                 pl.ds(pl.multiple_of(half * 48, 16), 48), pl.ds(lt * LANES, LANES)
             ].astype(ref.dtype)
         for lt in range(6):
-            ref[pl.ds(CONV_ROWS + lt * 96, 96), :] = down_ref[
+            ref[pl.ds(960 + lt * 96, 96), :] = down_ref[
                 pl.ds(pl.multiple_of(half * 96, 32), 96), pl.ds(lt * LANES, LANES)
             ].astype(ref.dtype)
-        ref[pl.ds(1584, HALF_ROWS - 1584), :] = jnp.zeros((HALF_ROWS - 1584, LANES), ref.dtype)
-
-
-def side_kernel(grad_ref, patch_ref, dw_ref, send_ref, coarse_ref, src_ref, row_ref):
+        last = conv_ref[pl.ds(pl.multiple_of(half * 48, 16), 48), pl.ds(20 * LANES, LANES)]
+        last = pltpu.roll(last, C, 1)
+        free_ref[...] = jnp.zeros((16, 8, LANES), F32)
+        for part in range(3):
+            free_ref[:, part : part + 1, :] = last[part * 16 : part * 16 + 16, :].reshape(16, 1, LANES)
+        ref[pl.ds(MAIN_ROWS, 128), :] = free_ref[...].reshape(128, LANES).astype(ref.dtype)
+
+
+def side_kernel(grad_ref, patch_ref, dw_ref, send_ref, coarse_ref, src_ref, flat_ref, row_ref):
     src_ref[...] = grad_ref[...].astype(F32)
-    spread_rows(src_ref, row_ref.reshape(SLOTS, LANES), True)
+    spread_rows(src_ref, flat_ref, True)
+    to_chips(flat_ref, row_ref)
+    row_ref[:, 31:32, :] = jnp.zeros((32, 1, LANES), F32)
     pack(row_ref, send_ref)
     coarse_ref[...] = dot(dw_ref[...], patch_ref[...], 1, 1).astype(BF16)
 
 
-def backward_kernel(grad_ref, halo_ref, w_ref, out_ref, pad_ref, cols_ref, act_ref, row_ref):
+def backward_kernel(grad_ref, halo_ref, w_ref, out_ref, pad_ref, cols_ref, act_ref, row_ref, flat_ref):
     for x in range(SIDE):
         for y in range(SIDE):
             base = ((x + 1) * 10 + y + 1) * COL
@@ -242,7 +268,7 @@
                 pad_ref[pl.ds(base + 1 + par, 8, stride=2), :] = grad_ref[
                     pl.ds((x * 8 + y) * 16 + par * 8, 8), :
                 ].astype(F32)
-    fill_halo(pad_ref, halo_ref, row_ref)
+    fill_halo(pad_ref, halo_ref, row_ref, flat_ref)
     shifted_columns(pad_ref, cols_ref)
     full = conv(cols_ref, w_ref)
     for n in range(64):
@@ -251,25 +277,38 @@
     out_ref[...] = act_ref[...].T[:C, :]
 
 
-def finish_kernel(core_ref, mine_ref, other_ref, conv_ref, down_ref):
-    def scale(first, last, count):
-        total = jnp.zeros((8, LANES), F32)
-        for ref in (mine_ref, other_ref):
-            values = ref[pl.ds(first, last - first), :].astype(F32)
-            total = total + jnp.sum((values * values).reshape(-1, 8, LANES), axis=0)
-        return lax.rsqrt(jnp.sum(total, keepdims=True) * (1.0 / count) + EPSILON)
-
-    conv_scale = scale(0, CONV_ROWS, C * 27 * C)
-    down_scale = scale(CONV_ROWS, 1584, C2 * 8 * C)
+def finish_kernel(core_ref, mine_ref, other_ref, conv_ref, down_ref, last_ref):
+    def squares(values):
+        return jnp.sum((values * values).reshape(-1, 8, LANES), axis=0)
+
+    conv_sum = jnp.zeros((8, LANES), F32)
+    down_sum = jnp.zeros((8, LANES), F32)
+    for n, ref in enumerate((mine_ref, other_ref)):
+        conv_sum += squares(ref[0:CONV_CHIPS, 24:72, :].astype(F32))
+        down_sum += squares(ref[CONV_CHIPS:32, 24:72, :].astype(F32))
+        for part in range(3):
+            rows = ref[0:16, part * 8 : part * 8 + 8, :].astype(F32)
+            rows = pltpu.roll(rows, 32, 2)[:, 7:8, :].reshape(16, LANES)
+            rows = jnp.where(lanes_of(rows) < 32, rows, 0.0)
+            last_ref[n, pl.ds(part * 16, 16), :] = rows
+            conv_sum += squares(rows)
+    conv_scale = lax.rsqrt(jnp.sum(conv_sum, keepdims=True) * (1.0 / (C * 27 * C)) + EPSILON)
+    down_scale = lax.rsqrt(jnp.sum(down_sum, keepdims=True) * (1.0 / (C2 * 8 * C)) + EPSILON)
     core = core_ref[0]
-    for ref, half in ((mine_ref, core), (other_ref, 1 - core)):
-        for lt in range(21):
-            width = min(LANES, 27 * C - lt * LANES)
-            values = ref[pl.ds(lt * 48, 48), :].astype(F32) * conv_scale
-            conv_ref[pl.ds(pl.multiple_of(half * 48, 16), 48), pl.ds(lt * LANES, width)] = values[:, :width]
+    for n, (ref, half) in enumerate(((mine_ref, core), (other_ref, 1 - core))):
+        rows = pl.ds(pl.multiple_of(half * 48, 16), 48)
+        for lt in range(20):
+            conv_ref[rows, pl.ds(lt * LANES, LANES)] = ref[lt, 24:72, :].astype(F32) * conv_scale
+        conv_ref[rows, pl.ds(20 * LANES, 32)] = (last_ref[n] * conv_scale)[:, :32]
         for lt in range(6):
-            values = ref[pl.ds(CONV_ROWS + lt * 96, 96), :].astype(F32) * down_scale
-            down_ref[pl.ds(pl.multiple_of(half * 96, 32), 96), pl.ds(lt * LANES, LANES)] = values
+            for part in range(2):
+                rows = pl.ds(pl.multiple_of(half * 96 + part * 48, 16), 48)
+                values = ref[CONV_CHIPS + lt * 2 + part, 24:72, :].astype(F32) * down_scale
+                down_ref[rows, pl.ds(lt * LANES, LANES)] = values
+
+
+def there(rows):
+    return pltpu.with_memory_space_constraint(rows, pltpu.HBM)
 
 
 def here(rows):
@@ -306,10 +345,10 @@
     block = features[0, 0]
     cot = cotangent[0, 0]
     core = lax.axis_index("c").astype(jnp.int32).reshape(1)
-    rows_shape = ((SLOTS, LANES), BF16)
+    rows_shape = ((VOX, LANES), BF16)
     by_chip = (32, 32, LANES)
     packed = (32, 24, LANES)
-    flat_scratch = pltpu.VMEM((SLOTS, LANES), F32)
+    flat_scratch = pltpu.VMEM((VOX, LANES), F32)
     slot_scratch = pltpu.VMEM(by_chip, F32)
 
     def swap(rows):
@@ -317,20 +356,22 @@
 
     (spread,) = pl.pallas_call(
         spread_kernel,
-        out_shape=[pltpu.VMEM(*rows_shape)],
-        in_specs=[pl.BlockSpec(memory_space=pltpu.HBM)] * 2,
+        out_shape=[pltpu.VMEM(packed, BF16)],
+        in_specs=[pl.BlockSpec(memory_space=pltpu.HBM)] * 3,
         out_specs=[pl.BlockSpec(memory_space=pltpu.VMEM)],
         scratch_shapes=[
             pltpu.SMEM((1, 26), jnp.int32),
             pltpu.VMEM((C, VOX), BF16),
-            pltpu.SemaphoreType.DMA((2,)),
+            pltpu.VMEM((32, LANES), jnp.int32),
+            pltpu.SemaphoreType.DMA((3,)),
             flat_scratch,
             flat_scratch,
+            slot_scratch,
         ],
         compiler_params=PARAMS,
         name="spread",
-    )(neighbours[0], block)
-    middle = here(trade(spread.reshape(by_chip), CHIPS))
+    )(there(neighbours[0]), there(block), there(jnp.asarray(direction_table())))
+    middle = here(trade(spread, CHIPS))
     route = call(route_kernel, [(packed, BF16)], [slot_scratch], scalars=1, ins=3, name="route")
     (routed,) = route(core, middle, middle, here(swap(middle)))
     halo = trade(routed, CHIPS)
@@ -348,39 +389,56 @@
     grad, patch, keep, send = call(
         forward_kernel,
         [rows_shape, ((LANES, 8 * LANES), BF16), ((HALF_ROWS, LANES), F32), ((HALF_ROWS, LANES), BF16)],
-        [pad_scratch, cols_scratch, flat_scratch, slot_scratch, pltpu.VMEM((C, 21 * LANES), F32), pltpu.VMEM((C2, 8 * C), F32)],
+        [
+            pad_scratch,
+            cols_scratch,
+            flat_scratch,
+            slot_scratch,
+            flat_scratch,
+            pltpu.VMEM((C, 21 * LANES), F32),
+            pltpu.VMEM((C2, 8 * C), F32),
+            pltpu.VMEM((16, 8, LANES), F32),
+        ],
         scalars=1,
         ins=5,
         name="forward",
     )(core, block, here(halo), cot, forward_w, down_w)
     spread2, coarse = call(
-        side_kernel, [(packed, BF16), ((C2, LANES), BF16, True)], [flat_scratch, slot_scratch], ins=3, name="side"
+        side_kernel, [(packed, BF16), ((C2, LANES), BF16, True)], [flat_scratch, flat_scratch, slot_scratch], ins=3, name="side"
     )(grad, patch, down_w)
 
     pair = (keep + swap(send).astype(F32)).astype(BF16)
-    out = jnp.concatenate([spread2, pair.reshape(32, 56, LANES)], axis=1)
-    got = trade(out, CHIPS)
+    main = pair[:MAIN_ROWS].reshape(32, 48, LANES)
+    free = pair[MAIN_ROWS:].reshape(16, 8, LANES)[:, :3].reshape(16, 3, 1, LANES)
+    free = jnp.pad(free, ((0, 16), (0, 0), (7, 0), (0, 0))).reshape(packed)
+    got = trade(jnp.concatenate([spread2 + free, main], axis=1), CHIPS)
     middle2 = got[:, :24]
-    part = jnp.sum(got[:, 24:].astype(F32), axis=0)
+    part = jnp.sum(got.astype(F32), axis=0)
     other2, part = lax.optimization_barrier((swap(middle2), part))
-    line = trade(jnp.broadcast_to(part, (4, 56, LANES)), "x")
+    line = trade(jnp.broadcast_to(part, (4, 72, LANES)), "x")
     whole = jnp.sum(line, axis=0).astype(BF16)
     (routed2,) = route(core, middle, here(middle2), here(other2))
-    out = jnp.concatenate([routed2, jnp.broadcast_to(whole, (32, 56, LANES))], axis=1)
-    got = trade(out, CHIPS)
-    halo2 = got[:, :24]
-    mine = got[:, 24:].reshape(HALF_ROWS, LANES)
-    theirs = swap(mine)
+    row = lax.broadcasted_iota(jnp.int32, (24, LANES), 0)
+    lane = lax.broadcasted_iota(jnp.int32, (24, LANES), 1)
+    inside = (row % 8 == 7) & (lane >= C)
+    routed2 = jnp.where(inside, whole[:24], routed2)
+    got = trade(jnp.concatenate([routed2, jnp.broadcast_to(whole[24:], (32, 48, LANES))], axis=1), CHIPS)
+    theirs = swap(got)
     (grad_features,) = call(
         backward_kernel,
         [((C, VOX), F32, True)],
-        [pad_scratch, cols_scratch, flat_scratch, slot_scratch],
+        [pad_scratch, cols_scratch, flat_scratch, slot_scratch, flat_scratch],
         ins=3,
         name="backward",
-    )(grad, here(halo2), backward_w)
+    )(grad, here(got[:, :24]), backward_w)
     grad_conv, grad_down = call(
-        finish_kernel, [((C, 27 * C), F32, True), ((C2, 8 * C), F32, True)], scalars=1, ins=2, name="finish"
-    )(core, here(mine), here(theirs))
+        finish_kernel,
+        [((C, 27 * C), F32, True), ((C2, 8 * C), F32, True)],
+        [pltpu.VMEM((2, 48, LANES), F32)],
+        scalars=1,
+        ins=2,
+        name="finish",
+    )(core, here(got), here(theirs))
     return coarse[None, None], grad_features[None, None], grad_conv, grad_down
 
 

time: 119 us -> 116 us (0.975)
  blocking collectives: 62.9 us -> 40.7 us
  waiting for transfers between devices: 12.2 us -> 28.4 us
  local copies, waits for them, and re-layouts: 6.13 us -> 3.58 us
  starting transfers between devices: 24.6 us -> 26.6 us
  Pallas kernels: 12.1 us -> 13.8 us
    all_to_all x3 -> x2, blocking collectives: 62.9 us -> 40.7 us  [trade(): return lax.all_to_all(rows, axes, 0, 0, tiled=True)]
    all_to_all x2 -> x3, waiting for transfers between devices: 9.55 us -> 25.9 us  [trade(): return lax.all_to_all(rows, axes, 0, 0, tiled=True)]
    all_to_all x2 -> x3, starting transfers between devices: 8.13 us -> 11.8 us  [trade(): return lax.all_to_all(rows, axes, 0, 0, tiled=True)]
    unnamed x17 -> x11, local copies, waits for them, and re-layouts: 3.19 us -> 0.75 us
    ppermute x4, starting transfers between devices: 16.4 us -> 14.8 us  [swap(): return lax.ppermute(rows, 'c', [(0, 1), (1, 0)])]
  transfers between devices with their start and end apart: 6 -> 7, of which waited for: 5 -> 6; matrix products, arithmetic and copies ran while one was open for 2% -> 3% of each run, Pallas kernels for 4% -> 4%
where the time goes in v6:
time: 116 us; the launch traced here: 115 us
  blocking collectives  40.7 us (35%)
  waiting for transfers between devices  28.4 us (24%)
  starting transfers between devices  26.6 us (23%)
  Pallas kernels  13.8 us (12%)
  local copies, waits for them, and re-layouts  3.58 us (3%)
  other arithmetic  1.27 us (1%)
    all_to_all x2, blocking collectives, trade(): return lax.all_to_all(rows, axes, 0, 0, tiled=True)  40.7 us
    all_to_all x3, waiting for transfers between devices, trade(): return lax.all_to_all(rows, axes, 0, 0, tiled=True)  25.9 us
    ppermute x4, starting transfers between devices, swap(): return lax.ppermute(rows, 'c', [(0, 1), (1, 0)])  14.8 us
    all_to_all x3, starting transfers between devices, trade(): return lax.all_to_all(rows, axes, 0, 0, tiled=True)  11.8 us
    pallas_call x1, Pallas kernels, shards(): call(forward_kernel, [rows_shape, ((LANES, 8 * LANES), BF16), ((HALF_ROWS...  3.94 us
    pallas_call x1, Pallas kernels, shards(): call(backward_kernel, [((C, VOX), F32, True)], [pad_scratch, cols_scratch...  3.02 us
    ppermute x4, waiting for transfers between devices, swap(): return lax.ppermute(rows, 'c', [(0, 1), (1, 0)])  2.49 us
  transfers between devices with their start and end apart: 7, of which 6 were waited for; matrix products, arithmetic and copies ran while one was open for 3% of the time, Pallas kernels for 4%

profile of v6, /device:TPU:1, one launch (start us, length us, event | category | flops | bytes accessed | tf_op | source)
XLA Modules:
  0.0 115.3 jit_solution(14684533985183076636)
XLA Ops:
  0.6 0.0 copy-start.2
  0.6 1.4 %spread.1 = bf16[32,24,128]{2,1,0:T(8,128)(2,1)S(1)} custom-call(s32[1,26]{1,0:T(1,128)} %bitcast.40, bf16[96,1024]{1,0:T(8,128)(2,1)} %bitcast.31, s32[32,128]{1,0:T(8,128)} %constant.30.clone.table_hbm), custom_call_target="tpu_custom_call" | custom-call | tf_op jit(solution)/shard_map/spread/pallas_call | solution.py:357
  2.0 21.2 %all_to_all.25.owner_ref.mine_ref = bf16[32,24,128]{2,1,0:T(8,128)(2,1)S(1)} all-to-all(bf16[32,24,128]{2,1,0:T(8,128)(2,1)S(1)} %spread.1), channel_id=1, replica_groups=mesh['x'=4,'y'=4,'z'=8,'c'=2] {'y','z'}, dimensions={0} | all-to-all | bytes 393216 | tf_op jit(solution)/shard_map/all_to_all | solution.py:341
  23.2 2.8 %collective-permute-start = (bf16[32,24,128]{2,1,0:T(8,128)(2,1)S(1)}, bf16[32,24,128]{2,1,0:T(8,128)(2,1)S(1)}, u32[]{:S(2)}, u32[]{:S(2)}) collective-permute-start(bf16[32,24,128]{2,1,0:T(8,128)(2,1)S(1)} %all_to_all.25.owner_ref.mine_ref), channel_id=1, source_target_pairs={{0,1},{1,0},{2,3},{3,2},{4,5},{5,4},{6,7},{7,6},{8,9},{9,8},{10,11... | collective-permute-start | bytes 589832 | tf_op jit(solution)/shard_map/ppermute | solution.py:355
  26.1 1.1 collective-permute-done.other_ref
  27.2 1.8 %route.2 = bf16[32,24,128]{2,1,0:T(8,128)(2,1)} custom-call(s32[1]{0:T(128)} %bitcast.core_ref, bf16[32,24,128]{2,1,0:T(8,128)(2,1)S(1)} %all_to_all.25.owner_ref.mine_ref, bf16[32,24,128]{2,1,0:T(8,128)(2,1)S(1)} %all_to_all.25.owner_ref.mine_ref, bf16[32,24,128]{2,1,0:T(8,128)(2,1)S(1)} %collective-permute-done.other_ref), custom_call_target="tpu_custom_call" | custom-call | tf_op jit(solution)/shard_map/route/pallas_call | solution.py:376
  29.0 3.9 %all-to-all-start.1 = ((bf16[32,24,128]{2,1,0:T(8,128)(2,1)}), bf16[32,24,128]{2,1,0:T(8,128)(2,1)S(1)}, u32[]{:S(2)}, u32[]{:S(2)}) async-start(bf16[32,24,128]{2,1,0:T(8,128)(2,1)} %route.2), calls=%async_computation.1 | async-start | bytes 393216 | tf_op jit(solution)/shard_map/all_to_all | solution.py:341
  32.8 0.0 copy-done.2
  32.9 0.3 copy.16
  33.2 0.3 copy.21
  33.6 0.2 pad.16.clone
  33.8 0.2 pad.15
  34.0 0.0 copy-start
  34.0 0.0 copy-start.1
  34.1 1.4 %reshape.42 = bf16[192,8,96]{2,1,0:T(8,128)(2,1)S(1)} reshape(bf16[192,768]{1,0:T(8,128)(2,1)} %param.9) | data formatting | bytes 589824 | tf_op jit(solution)/shard_map/reshape | solution.py:383
  35.5 0.1 pad.17
  35.6 0.1 copy.26
  35.7 6.6 %all-to-all-done.1.halo_ref = bf16[32,24,128]{2,1,0:T(8,128)(2,1)S(1)} async-done(((bf16[32,24,128]{2,1,0:T(8,128)(2,1)}), bf16[32,24,128]{2,1,0:T(8,128)(2,1)S(1)}, u32[]{:S(2)}, u32[]{:S(2)}) %all-to-all-start.1) | async-done | bytes 196640 | tf_op jit(solution)/shard_map/all_to_all | solution.py:341
  42.2 0.0 copy-done
  42.2 0.0 copy-done.1
  42.2 3.9 %forward.1 = (bf16[1024,128]{1,0:T(8,128)(2,1)S(1)}, bf16[128,1024]{1,0:T(8,128)(2,1)S(1)}, f32[1664,128]{1,0:T(8,128)S(1)}, bf16[1664,128]{1,0:T(8,128)(2,1)S(1)}) custom-call(s32[1]{0:T(128)} %bitcast.core_ref, bf16[96,1024]{1,0:T(8,128)(2,1)S(1)} %bitcast.32, bf16[32,24,128]{2,1,0:T(8,128)(2,1)S(1)} %all-to-all-done.1.halo_ref, ...), custom_call_target="tpu_custom_call" | custom-call | tf_op jit(solution)/shard_map/forward/pallas_call | solution.py:389
  46.2 3.0 %collective-permute-start.1 = (bf16[1664,128]{1,0:T(8,128)(2,1)S(1)}, bf16[1664,128]{1,0:T(8,128)(2,1)S(1)}, u32[]{:S(2)}, u32[]{:S(2)}) collective-permute-start(bf16[1664,128]{1,0:T(8,128)(2,1)S(1)} %get-tuple-element.26), channel_id=1, source_target_pairs={{0,1},{1,0},{2,3},{3,2},{4,5},{5,4},{6,7},{7,6},{8,9},{9,8},{10,11... | collective-permute-start | bytes 1277960 | tf_op jit(solution)/shard_map/ppermute | solution.py:355
  49.2 1.0 side.1
  50.2 0.4 collective-permute-done.1
  50.6 0.1 add_convert_fusion
  50.8 0.1 fusion
  50.9 0.9 pad_maximum_fusion
  51.7 3.9 %all-to-all-start.2 = ((bf16[32,72,128]{2,1,0:T(8,128)(2,1)}), bf16[32,72,128]{2,1,0:T(8,128)(2,1)S(1)}, u32[]{:S(2)}, u32[]{:S(2)}) async-start(bf16[32,72,128]{2,1,0:T(8,128)(2,1)} %pad_maximum_fusion), calls=%async_computation.2 | async-start | bytes 1179648 | tf_op jit(solution)/shard_map/all_to_all | solution.py:341
  55.6 15.6 %all-to-all-done.2 = bf16[32,72,128]{2,1,0:T(8,128)(2,1)S(1)} async-done(((bf16[32,72,128]{2,1,0:T(8,128)(2,1)}), bf16[32,72,128]{2,1,0:T(8,128)(2,1)S(1)}, u32[]{:S(2)}, u32[]{:S(2)}) %all-to-all-start.2) | async-done | bytes 589856 | tf_op jit(solution)/shard_map/all_to_all | solution.py:341
  71.3 3.5 %collective-permute-start.2 = (bf16[32,24,128]{2,1,0:T(8,128)(2,1)S(1)}, bf16[32,24,128]{2,1,0:T(8,128)(2,1)S(1)}, u32[]{:S(2)}, u32[]{:S(2)}) collective-permute-start(bf16[32,24,128]{2,1,0:T(8,128)(2,1)S(1)} %slice.31.mine_ref), channel_id=1, source_target_pairs={{0,1},{1,0},{2,3},{3,2},{4,5},{5,4},{6,7},{7,6},{8,9},{9,8},{10,11... | collective-permute-start | bytes 589832 | tf_op jit(solution)/shard_map/ppermute | solution.py:355
  74.8 0.1 convert_reduce_fusion
  74.9 1.0 collective-permute-done.2.other_ref
  75.8 0.7 broadcast_in_dim.22
  76.5 4.0 %all-to-all-start.3 = ((f32[4,72,128]{2,1,0:T(8,128)}), f32[4,72,128]{2,1,0:T(8,128)S(1)}, u32[]{:S(2)}, u32[]{:S(2)}) async-start(f32[4,72,128]{2,1,0:T(8,128)} %broadcast_in_dim.22), calls=%async_computation.3 | async-start | bytes 294912 | tf_op jit(solution)/shard_map/all_to_all | solution.py:341
  80.6 0.1 fusion.1
  80.6 1.1 route.3
  81.8 3.7 %all-to-all-done.3 = f32[4,72,128]{2,1,0:T(8,128)S(1)} async-done(((f32[4,72,128]{2,1,0:T(8,128)}), f32[4,72,128]{2,1,0:T(8,128)S(1)}, u32[]{:S(2)}, u32[]{:S(2)}) %all-to-all-start.3) | async-done | bytes 147488 | tf_op jit(solution)/shard_map/all_to_all | solution.py:341
  85.5 0.1 broadcast_in_dim.24
  85.7 19.5 %all_to_all.26.mine_ref = bf16[32,72,128]{2,1,0:T(8,128)(2,1)S(1)} all-to-all(bf16[32,72,128]{2,1,0:T(8,128)(2,1)S(1)} %pad_maximum_fusion.1), channel_id=1, replica_groups=mesh['x'=4,'y'=4,'z'=8,'c'=2] {'y','z'}, dimensions={0} | all-to-all | bytes 1179648 | tf_op jit(solution)/shard_map/all_to_all | solution.py:341
  105.1 5.5 %collective-permute-start.3 = (bf16[32,72,128]{2,1,0:T(8,128)(2,1)S(1)}, bf16[32,72,128]{2,1,0:T(8,128)(2,1)S(1)}, u32[]{:S(2)}, u32[]{:S(2)}) collective-permute-start(bf16[32,72,128]{2,1,0:T(8,128)(2,1)S(1)} %all_to_all.26.mine_ref), channel_id=1, source_target_pairs={{0,1},{1,0},{2,3},{3,2},{4,5},{5,4},{6,7},{7,6},{8,9},{9,8},{10,11... | collective-permute-start | bytes 1769480 | tf_op jit(solution)/shard_map/ppermute | solution.py:355
  110.6 3.0 %backward.1 = f32[96,1024]{1,0:T(8,128)} custom-call(bf16[1024,128]{1,0:T(8,128)(2,1)S(1)} %get-tuple-element.21.grad_ref, bf16[32,24,128]{2,1,0:T(8,128)(2,1)S(1)} %slice.34.halo_ref, bf16[9,384,128]{2,1,0:T(8,128)(2,1)S(1)} %bitcast.30), custom_call_target="tpu_custom_call" | custom-call | tf_op jit(solution)/shard_map/backward/pallas_call | solution.py:427
  113.7 0.0 collective-permute-done.3.other_ref
  113.7 1.6 %finish.1 = (f32[96,2592]{1,0:T(8,128)}, f32[192,768]{1,0:T(8,128)}) custom-call(s32[1]{0:T(128)} %bitcast.core_ref, bf16[32,72,128]{2,1,0:T(8,128)(2,1)S(1)} %all_to_all.26.mine_ref, bf16[32,72,128]{2,1,0:T(8,128)(2,1)S(1)} %collective-permute-done.3.other_ref), custom_call_target="tpu_custom_call" | custom-call | tf_op jit(solution)/shard_map/finish/pallas_call | solution.py:434
  (16 shorter events, 0.2 us)
Async XLA Ops:
  0.6 32.2 %copy-start.2 = (bf16[96,2592]{1,0:T(8,128)(2,1)S(1)}, bf16[96,2592]{1,0:T(8,128)(2,1)}, u32[]{:S(2)}) copy-start(bf16[96,2592]{1,0:T(8,128)(2,1)} %param.8) | copy-start | bytes 1492996
  23.2 3.9 %collective-permute-start = (bf16[32,24,128]{2,1,0:T(8,128)(2,1)S(1)}, bf16[32,24,128]{2,1,0:T(8,128)(2,1)S(1)}, u32[]{:S(2)}, u32[]{:S(2)}) collective-permute-start(bf16[32,24,128]{2,1,0:T(8,128)(2,1)S(1)} %all_to_all.25.owner_ref.mine_ref), channel_id=1, source_target_pairs={{0,1},{1,0},{2,3},{3,2},{4,5},{5,4},{6,7},{7,6},{8,9},{9,8},{10,11... | collective-permute-start | bytes 589832 | tf_op jit(solution)/shard_map/ppermute | solution.py:355
  29.0 13.3 %all-to-all-start.1 = ((bf16[32,24,128]{2,1,0:T(8,128)(2,1)}), bf16[32,24,128]{2,1,0:T(8,128)(2,1)S(1)}, u32[]{:S(2)}, u32[]{:S(2)}) async-start(bf16[32,24,128]{2,1,0:T(8,128)(2,1)} %route.2), calls=%async_computation.1 | async-start | bytes 393216 | tf_op jit(solution)/shard_map/all_to_all | solution.py:341
  34.0 8.2 %copy-start = (bf16[1,1,96,1024]{3,2,1,0:T(8,128)(2,1)S(1)}, bf16[1,1,96,1024]{3,2,1,0:T(8,128)(2,1)}, u32[]{:S(2)}) copy-start(bf16[1,1,96,1024]{3,2,1,0:T(8,128)(2,1)} %param.6) | copy-start | bytes 589828
  34.0 8.2 %copy-start.1 = (bf16[1,1,192,128]{3,2,1,0:T(8,128)(2,1)S(1)}, bf16[1,1,192,128]{3,2,1,0:T(8,128)(2,1)}, u32[]{:S(2)}) copy-start(bf16[1,1,192,128]{3,2,1,0:T(8,128)(2,1)} %param.7) | copy-start | bytes 147460
  46.2 4.4 %collective-permute-start.1 = (bf16[1664,128]{1,0:T(8,128)(2,1)S(1)}, bf16[1664,128]{1,0:T(8,128)(2,1)S(1)}, u32[]{:S(2)}, u32[]{:S(2)}) collective-permute-start(bf16[1664,128]{1,0:T(8,128)(2,1)S(1)} %get-tuple-element.26), channel_id=1, source_target_pairs={{0,1},{1,0},{2,3},{3,2},{4,5},{5,4},{6,7},{7,6},{8,9},{9,8},{10,11... | collective-permute-start | bytes 1277960 | tf_op jit(solution)/shard_map/ppermute | solution.py:355
  51.7 19.6 %all-to-all-start.2 = ((bf16[32,72,128]{2,1,0:T(8,128)(2,1)}), bf16[32,72,128]{2,1,0:T(8,128)(2,1)S(1)}, u32[]{:S(2)}, u32[]{:S(2)}) async-start(bf16[32,72,128]{2,1,0:T(8,128)(2,1)} %pad_maximum_fusion), calls=%async_computation.2 | async-start | bytes 1179648 | tf_op jit(solution)/shard_map/all_to_all | solution.py:341
  71.3 4.5 %collective-permute-start.2 = (bf16[32,24,128]{2,1,0:T(8,128)(2,1)S(1)}, bf16[32,24,128]{2,1,0:T(8,128)(2,1)S(1)}, u32[]{:S(2)}, u32[]{:S(2)}) collective-permute-start(bf16[32,24,128]{2,1,0:T(8,128)(2,1)S(1)} %slice.31.mine_ref), channel_id=1, source_target_pairs={{0,1},{1,0},{2,3},{3,2},{4,5},{5,4},{6,7},{7,6},{8,9},{9,8},{10,11... | collective-permute-start | bytes 589832 | tf_op jit(solution)/shard_map/ppermute | solution.py:355
  76.5 9.0 %all-to-all-start.3 = ((f32[4,72,128]{2,1,0:T(8,128)}), f32[4,72,128]{2,1,0:T(8,128)S(1)}, u32[]{:S(2)}, u32[]{:S(2)}) async-start(f32[4,72,128]{2,1,0:T(8,128)} %broadcast_in_dim.22), calls=%async_computation.3 | async-start | bytes 294912 | tf_op jit(solution)/shard_map/all_to_all | solution.py:341
  105.1 8.5 %collective-permute-start.3 = (bf16[32,72,128]{2,1,0:T(8,128)(2,1)S(1)}, bf16[32,72,128]{2,1,0:T(8,128)(2,1)S(1)}, u32[]{:S(2)}, u32[]{:S(2)}) collective-permute-start(bf16[32,72,128]{2,1,0:T(8,128)(2,1)S(1)} %all_to_all.26.mine_ref), channel_id=1, source_target_pairs={{0,1},{1,0},{2,3},{3,2},{4,5},{5,4},{6,7},{7,6},{8,9},{9,8},{10,11... | collective-permute-start | bytes 1769480 | tf_op jit(solution)/shard_map/ppermute | solution.py:355

commit v7 on v6

--- a/solution.py
+++ b/solution.py
@@ -104,7 +104,7 @@
 
 
 def slot_groups(ref):
-    rows = ref[...].astype(F32)
+    rows = ref[:, 0:24].astype(F32)
     groups = [rows[:, g * 8 : g * 8 + 8] for g in range(3)]
     lane = lanes_of(groups[0])
     moved = [pltpu.roll(rows, 32 * (part + 1), 2) for part, rows in enumerate(groups)]
@@ -120,18 +120,52 @@
     ]
     for copy in copies:
         copy.start()
-    for copy in copies:
-        copy.wait()
-    wide = jnp.concatenate([f_ref[...].astype(F32), jnp.zeros((LANES - C, VOX), F32)], axis=0)
-    src_ref[...] = wide.T
-    spread_rows(src_ref, flat_ref, False)
-    to_chips(flat_ref, row_ref)
+    copies[0].wait()
+    copies[2].wait()
     table = table_ref[...]
     owner = jnp.full((32, LANES), -1, jnp.int32)
     for number in range(26):
         owner = jnp.where(table == number, nbr_ref[0, number], owner)
     row_ref[:, 31:32, :] = owner.astype(F32).reshape(32, 1, LANES)
+    copies[1].wait()
+    wide = jnp.concatenate([f_ref[...].astype(F32), jnp.zeros((LANES - C, VOX), F32)], axis=0)
+    src_ref[...] = wide.T
+    spread_rows(src_ref, flat_ref, False)
+    to_chips(flat_ref, row_ref)
     pack(row_ref, out_ref)
+
+
+def prepare_kernel(f_ref, own_ref):
+    wide = jnp.concatenate([f_ref[...].astype(F32), jnp.zeros((LANES - C, VOX), F32)], axis=0)
+    own_ref[...] = wide.T
+
+
+def merge_kernel(halo_ref, keep_ref, other_ref, out_ref):
+    pair = keep_ref[...] + other_ref[...].astype(F32)
+    out_ref[:, 24:72] = pair[:MAIN_ROWS].reshape(32, 48, LANES).astype(BF16)
+    free = pair[MAIN_ROWS:].reshape(16, 8, LANES)
+    place = lax.broadcasted_iota(jnp.int32, (16, 8, LANES), 1)
+    for part in range(3):
+        rows = halo_ref[:, part * 8 : part * 8 + 8].astype(F32)
+        added = jnp.where(place == 7, jnp.broadcast_to(free[:, part : part + 1], (16, 8, LANES)), 0.0)
+        out_ref[0:16, part * 8 : part * 8 + 8] = (rows[:16] + added).astype(BF16)
+        out_ref[16:32, part * 8 : part * 8 + 8] = rows[16:].astype(BF16)
+
+
+def total_kernel(got_ref, part_ref, rows_ref):
+    total = jnp.sum(got_ref[...].astype(F32), axis=0)
+    for n in range(4):
+        part_ref[n] = total
+    rows_ref[...] = got_ref[:, 0:24]
+
+
+def join_kernel(line_ref, rows_ref, out_ref):
+    whole = line_ref[0] + line_ref[1] + line_ref[2] + line_ref[3]
+    out_ref[:, 24:72] = jnp.broadcast_to(whole[24:], (32, 48, LANES)).astype(BF16)
+    place = lax.broadcasted_iota(jnp.int32, (32, 24, LANES), 1) & 7
+    rows = rows_ref[...].astype(F32)
+    free = (place == 7) & (lanes_of(rows) >= C)
+    out_ref[:, 0:24] = jnp.where(free, jnp.broadcast_to(whole[:24], rows.shape), rows).astype(BF16)
 
 
 def route_kernel(core_ref, owner_ref, mine_ref, other_ref, out_ref, row_ref):
@@ -195,16 +229,14 @@
 
 
 def forward_kernel(
-    core_ref, f_ref, halo_ref, cot_ref, w_ref, dw_ref,
+    core_ref, own_ref, halo_ref, cot_ref, w_ref, dw_ref,
     grad_ref, patch_ref, keep_ref, send_ref,
     pad_ref, cols_ref, act_ref, row_ref, flat_ref, conv_ref, down_ref, free_ref,
 ):
-    wide = jnp.concatenate([f_ref[...].astype(F32), jnp.zeros((LANES - C, VOX), F32)], axis=0)
-    own = wide.T
     for x in range(SIDE):
         for y in range(SIDE):
-            pad_ref[pl.ds(((x + 1) * 10 + y + 1) * COL + 1, DEPTH), :] = own[
-                (x * 8 + y) * 16 : (x * 8 + y + 1) * 16, :
+            pad_ref[pl.ds(((x + 1) * 10 + y + 1) * COL + 1, DEPTH), :] = own_ref[
+                pl.ds((x * 8 + y) * 16, 16), :
             ]
     fill_halo(pad_ref, halo_ref, row_ref, flat_ref)
     shifted_columns(pad_ref, cols_ref)
@@ -381,7 +413,10 @@
     forward_w = jnp.pad(taps.transpose(1, 2, 0), pad).reshape(9, 3 * LANES, LANES)
     backward_w = jnp.pad(taps.transpose(1, 0, 2)[::-1], pad).reshape(9, 3 * LANES, LANES)
     down_w = jnp.pad(down_weight.reshape(C2, 8, C), ((0, 0), (0, 0), (0, LANES - C))).reshape(C2, 8 * LANES)
-    halo, forward_w, backward_w, down_w = lax.optimization_barrier((halo, forward_w, backward_w, down_w))
+    (own,) = call(prepare_kernel, [((VOX, LANES), F32)], ins=1, name="prepare")(block)
+    halo, forward_w, backward_w, down_w, own = lax.optimization_barrier(
+        (halo, forward_w, backward_w, down_w, own)
+    )
     forward_w, backward_w, down_w = here(forward_w), here(backward_w), here(down_w)
 
     pad_scratch = pltpu.VMEM((100 * COL, LANES), F32)
@@ -402,27 +437,21 @@
         scalars=1,
         ins=5,
         name="forward",
-    )(core, block, here(halo), cot, forward_w, down_w)
+    )(core, here(own), here(halo), cot, forward_w, down_w)
     spread2, coarse = call(
         side_kernel, [(packed, BF16), ((C2, LANES), BF16, True)], [flat_scratch, flat_scratch, slot_scratch], ins=3, name="side"
     )(grad, patch, down_w)
 
-    pair = (keep + swap(send).astype(F32)).astype(BF16)
-    main = pair[:MAIN_ROWS].reshape(32, 48, LANES)
-    free = pair[MAIN_ROWS:].reshape(16, 8, LANES)[:, :3].reshape(16, 3, 1, LANES)
-    free = jnp.pad(free, ((0, 16), (0, 0), (7, 0), (0, 0))).reshape(packed)
-    got = trade(jnp.concatenate([spread2 + free, main], axis=1), CHIPS)
-    middle2 = got[:, :24]
-    part = jnp.sum(got.astype(F32), axis=0)
+    message = (32, 72, LANES)
+    (out,) = call(merge_kernel, [(message, BF16)], ins=3, name="merge")(spread2, keep, here(swap(send)))
+    part, middle2 = call(total_kernel, [((4, 72, LANES), F32), (packed, BF16)], ins=1, name="total")(
+        here(trade(out, CHIPS))
+    )
     other2, part = lax.optimization_barrier((swap(middle2), part))
-    line = trade(jnp.broadcast_to(part, (4, 72, LANES)), "x")
-    whole = jnp.sum(line, axis=0).astype(BF16)
-    (routed2,) = route(core, middle, here(middle2), here(other2))
-    row = lax.broadcasted_iota(jnp.int32, (24, LANES), 0)
-    lane = lax.broadcasted_iota(jnp.int32, (24, LANES), 1)
-    inside = (row % 8 == 7) & (lane >= C)
-    routed2 = jnp.where(inside, whole[:24], routed2)
-    got = trade(jnp.concatenate([routed2, jnp.broadcast_to(whole[24:], (32, 48, LANES))], axis=1), CHIPS)
+    line = trade(part, "x")
+    (routed2,) = route(core, middle, middle2, here(other2))
+    (out,) = call(join_kernel, [(message, BF16)], ins=2, name="join")(here(line), routed2)
+    got = trade(out, CHIPS)
     theirs = swap(got)
     (grad_features,) = call(
         backward_kernel,
@@ -430,7 +459,7 @@
         [pad_scratch, cols_scratch, flat_scratch, slot_scratch, flat_scratch],
         ins=3,
         name="backward",
-    )(grad, here(got[:, :24]), backward_w)
+    )(grad, here(got), backward_w)
     grad_conv, grad_down = call(
         finish_kernel,
         [((C, 27 * C), F32, True), ((C2, 8 * C), F32, True)],

time: 116 us -> 115 us (level)
  blocking collectives: 40.7 us -> 61 us
  waiting for transfers between devices: 28.4 us -> 9.32 us
  starting transfers between devices: 26.6 us -> 22.8 us
  local copies, waits for them, and re-layouts: 3.58 us -> 6.22 us
  other arithmetic: 1.27 us -> 0 us
    all_to_all x2 -> x3, blocking collectives: 40.7 us -> 61 us  [trade(): return lax.all_to_all(rows, axes, 0, 0, tiled=True)]
    all_to_all x3 -> x2, waiting for transfers between devices: 25.9 us -> 6.74 us  [trade(): return lax.all_to_all(rows, axes, 0, 0, tiled=True)]
    all_to_all x3 -> x2, starting transfers between devices: 11.8 us -> 8.01 us  [trade(): return lax.all_to_all(rows, axes, 0, 0, tiled=True)]
    unnamed x11 -> x15, local copies, waits for them, and re-layouts: 0.75 us -> 4.06 us
  transfers between devices with their start and end apart: 7 -> 6, of which waited for: 6 -> 5; matrix products, arithmetic and copies ran while one was open for 3% -> 3% of each run, Pallas kernels for 4% -> 5%
where the time goes in v7:
time: 115 us
  blocking collectives  61 us (53%)
  starting transfers between devices  22.8 us (20%)
  Pallas kernels  14.8 us (13%)
  waiting for transfers between devices  9.32 us (8%)
  local copies, waits for them, and re-layouts  6.22 us (5%)
    all_to_all x3, blocking collectives, trade(): return lax.all_to_all(rows, axes, 0, 0, tiled=True)  61 us
    ppermute x4, starting transfers between devices, swap(): return lax.ppermute(rows, 'c', [(0, 1), (1, 0)])  14.7 us
    all_to_all x2, starting transfers between devices, trade(): return lax.all_to_all(rows, axes, 0, 0, tiled=True)  8.01 us
    all_to_all x2, waiting for transfers between devices, trade(): return lax.all_to_all(rows, axes, 0, 0, tiled=True)  6.74 us
    unnamed x15, local copies, waits for them, and re-layouts  4.06 us
    pallas_call x1, Pallas kernels, shards(): call(forward_kernel, [rows_shape, ((LANES, 8 * LANES), BF16), ((HALF_ROWS...  3.89 us
    pallas_call x1, Pallas kernels, shards(): call(backward_kernel, [((C, VOX), F32, True)], [pad_scratch, cols_scratch...  3.01 us
    ppermute x4, waiting for transfers between devices, swap(): return lax.ppermute(rows, 'c', [(0, 1), (1, 0)])  2.59 us
  transfers between devices with their start and end apart: 6, of which 5 were waited for; matrix products, arithmetic and copies ran while one was open for 3% of the time, Pallas kernels for 5%

profile of v7, /device:TPU:1, one launch (start us, length us, event | category | flops | bytes accessed | tf_op | source)
XLA Modules:
  0.0 114.8 jit_solution(14777811075518898243)
XLA Ops:
  0.6 1.3 %spread.1 = bf16[32,24,128]{2,1,0:T(8,128)(2,1)S(1)} custom-call(s32[1,26]{1,0:T(1,128)} %bitcast.28, bf16[96,1024]{1,0:T(8,128)(2,1)} %bitcast.21, s32[32,128]{1,0:T(8,128)} %constant.9.clone.table_hbm), custom_call_target="tpu_custom_call" | custom-call | tf_op jit(solution)/shard_map/spread/pallas_call | solution.py:389
  1.9 21.2 %all_to_all.25.owner_ref.mine_ref = bf16[32,24,128]{2,1,0:T(8,128)(2,1)S(1)} all-to-all(bf16[32,24,128]{2,1,0:T(8,128)(2,1)S(1)} %spread.1), channel_id=1, replica_groups=mesh['x'=4,'y'=4,'z'=8,'c'=2] {'y','z'}, dimensions={0} | all-to-all | bytes 393216 | tf_op jit(solution)/shard_map/all_to_all | solution.py:373
  23.2 2.8 %collective-permute-start = (bf16[32,24,128]{2,1,0:T(8,128)(2,1)S(1)}, bf16[32,24,128]{2,1,0:T(8,128)(2,1)S(1)}, u32[]{:S(2)}, u32[]{:S(2)}) collective-permute-start(bf16[32,24,128]{2,1,0:T(8,128)(2,1)S(1)} %all_to_all.25.owner_ref.mine_ref), channel_id=1, source_target_pairs={{0,1},{1,0},{2,3},{3,2},{4,5},{5,4},{6,7},{7,6},{8,9},{9,8},{10,11... | collective-permute-start | bytes 589832 | tf_op jit(solution)/shard_map/ppermute | solution.py:387
  26.0 1.1 collective-permute-done.other_ref
  27.1 1.8 %route.2 = bf16[32,24,128]{2,1,0:T(8,128)(2,1)} custom-call(s32[1]{0:T(128)} %bitcast.core_ref, bf16[32,24,128]{2,1,0:T(8,128)(2,1)S(1)} %all_to_all.25.owner_ref.mine_ref, bf16[32,24,128]{2,1,0:T(8,128)(2,1)S(1)} %all_to_all.25.owner_ref.mine_ref, bf16[32,24,128]{2,1,0:T(8,128)(2,1)S(1)} %collective-permute-done.other_ref), custom_call_target="tpu_custom_call" | custom-call | tf_op jit(solution)/shard_map/route/pallas_call | solution.py:408
  28.9 0.0 copy-start
  28.9 4.0 %all-to-all-start.1 = ((bf16[32,24,128]{2,1,0:T(8,128)(2,1)}), bf16[32,24,128]{2,1,0:T(8,128)(2,1)S(1)}, u32[]{:S(2)}, u32[]{:S(2)}) async-start(bf16[32,24,128]{2,1,0:T(8,128)(2,1)} %route.2), calls=%async_computation.1 | async-start | bytes 393216 | tf_op jit(solution)/shard_map/all_to_all | solution.py:373
  32.9 0.0 copy-done
  32.9 0.0 copy-start.5
  32.9 0.1 prepare.1.own_ref
  33.1 0.8 copy-done.5
  33.9 0.4 reshape.30
  34.3 0.1 pad.13
  34.4 0.0 copy-start.4
  34.4 0.1 copy.17
  34.5 1.0 copy-done.4
  35.5 0.3 copy.12
  35.8 0.0 copy-start.2
  35.8 0.8 copy-done.2
  36.6 1.1 copy.14
  37.7 0.0 copy-start.3
  37.7 1.4 %pad.12.clone = bf16[27,128,128]{2,1,0:T(8,128)(2,1)S(1)} pad(bf16[27,96,96]{2,1,0:T(8,128)(2,1)} %copy.14, bf16[]{:T(256)} %constant.8.clone.1), padding=0_0x0_32x0_32 | pad | bytes 1382402 | tf_op jit(solution)/shard_map/jit(_pad)/pad | solution.py:414
  39.1 0.0 copy-done.3
  39.1 0.0 copy-start.1
  39.1 0.2 pad.11
  39.4 2.9 %all-to-all-done.1.halo_ref = bf16[32,24,128]{2,1,0:T(8,128)(2,1)S(1)} async-done(((bf16[32,24,128]{2,1,0:T(8,128)(2,1)}), bf16[32,24,128]{2,1,0:T(8,128)(2,1)S(1)}, u32[]{:S(2)}, u32[]{:S(2)}) %all-to-all-start.1) | async-done | bytes 196640 | tf_op jit(solution)/shard_map/all_to_all | solution.py:373
  42.3 0.0 copy-done.1
  42.3 3.9 %forward.1 = (bf16[1024,128]{1,0:T(8,128)(2,1)S(1)}, bf16[128,1024]{1,0:T(8,128)(2,1)S(1)}, f32[1664,128]{1,0:T(8,128)S(1)}, bf16[1664,128]{1,0:T(8,128)(2,1)S(1)}) custom-call(s32[1]{0:T(128)} %bitcast.core_ref, f32[1024,128]{1,0:T(8,128)S(1)} %prepare.1.own_ref, bf16[32,24,128]{2,1,0:T(8,128)(2,1)S(1)} %all-to-all-done.1.halo_ref, ...), custom_call_target="tpu_custom_call" | custom-call | tf_op jit(solution)/shard_map/forward/pallas_call | solution.py:424
  46.2 3.0 %collective-permute-start.1 = (bf16[1664,128]{1,0:T(8,128)(2,1)S(1)}, bf16[1664,128]{1,0:T(8,128)(2,1)S(1)}, u32[]{:S(2)}, u32[]{:S(2)}) collective-permute-start(bf16[1664,128]{1,0:T(8,128)(2,1)S(1)} %get-tuple-element.30), channel_id=1, source_target_pairs={{0,1},{1,0},{2,3},{3,2},{4,5},{5,4},{6,7},{7,6},{8,9},{9,8},{10,11... | collective-permute-start | bytes 1277960 | tf_op jit(solution)/shard_map/ppermute | solution.py:387
  49.2 1.0 side.1
  50.2 0.4 collective-permute-done.1.other_ref
  50.6 0.1 merge.1
  50.7 20.2 %all_to_all.26.got_ref = bf16[32,72,128]{2,1,0:T(8,128)(2,1)S(1)} all-to-all(bf16[32,72,128]{2,1,0:T(8,128)(2,1)S(1)} %merge.1), channel_id=1, replica_groups=mesh['x'=4,'y'=4,'z'=8,'c'=2] {'y','z'}, dimensions={0} | all-to-all | bytes 1179648 | tf_op jit(solution)/shard_map/all_to_all | solution.py:373
  70.9 0.8 total.1
  71.7 3.4 %collective-permute-start.2 = (bf16[32,24,128]{2,1,0:T(8,128)(2,1)S(1)}, bf16[32,24,128]{2,1,0:T(8,128)(2,1)S(1)}, u32[]{:S(2)}, u32[]{:S(2)}) collective-permute-start(bf16[32,24,128]{2,1,0:T(8,128)(2,1)S(1)} %get-tuple-element.31.mine_ref), channel_id=1, source_target_pairs={{0,1},{1,0},{2,3},{3,2},{4,5},{5,4},{6,7},{7,6},{8,9},{9,8},{10,11... | collective-permute-start | bytes 589832 | tf_op jit(solution)/shard_map/ppermute | solution.py:387
  75.1 1.1 collective-permute-done.2.other_ref
  76.2 4.0 %all-to-all-start.3 = ((f32[4,72,128]{2,1,0:T(8,128)}), f32[4,72,128]{2,1,0:T(8,128)S(1)}, u32[]{:S(2)}, u32[]{:S(2)}) async-start(f32[4,72,128]{2,1,0:T(8,128)} %get-tuple-element.33), calls=%async_computation.3 | async-start | bytes 294912 | tf_op jit(solution)/shard_map/all_to_all | solution.py:373
  80.2 1.1 route.3.rows_ref
  81.3 3.8 %all-to-all-done.3.line_ref = f32[4,72,128]{2,1,0:T(8,128)S(1)} async-done(((f32[4,72,128]{2,1,0:T(8,128)}), f32[4,72,128]{2,1,0:T(8,128)S(1)}, u32[]{:S(2)}, u32[]{:S(2)}) %all-to-all-start.3) | async-done | bytes 147488 | tf_op jit(solution)/shard_map/all_to_all | solution.py:373
  85.1 0.1 join.1
  85.1 19.6 %all_to_all.27.halo_ref.mine_ref = bf16[32,72,128]{2,1,0:T(8,128)(2,1)S(1)} all-to-all(bf16[32,72,128]{2,1,0:T(8,128)(2,1)S(1)} %join.1), channel_id=1, replica_groups=mesh['x'=4,'y'=4,'z'=8,'c'=2] {'y','z'}, dimensions={0} | all-to-all | bytes 1179648 | tf_op jit(solution)/shard_map/all_to_all | solution.py:373
  104.7 5.5 %collective-permute-start.3 = (bf16[32,72,128]{2,1,0:T(8,128)(2,1)S(1)}, bf16[32,72,128]{2,1,0:T(8,128)(2,1)S(1)}, u32[]{:S(2)}, u32[]{:S(2)}) collective-permute-start(bf16[32,72,128]{2,1,0:T(8,128)(2,1)S(1)} %all_to_all.27.halo_ref.mine_ref), channel_id=1, source_target_pairs={{0,1},{1,0},{2,3},{3,2},{4,5},{5,4},{6,7},{7,6},{8,9},{9,8},{10,11... | collective-permute-start | bytes 1769480 | tf_op jit(solution)/shard_map/ppermute | solution.py:387
  110.2 3.0 %backward.1 = f32[96,1024]{1,0:T(8,128)} custom-call(bf16[1024,128]{1,0:T(8,128)(2,1)S(1)} %get-tuple-element.25.grad_ref, bf16[32,72,128]{2,1,0:T(8,128)(2,1)S(1)} %all_to_all.27.halo_ref.mine_ref, bf16[9,384,128]{2,1,0:T(8,128)(2,1)S(1)} %bitcast.20), custom_call_target="tpu_custom_call" | custom-call | tf_op jit(solution)/shard_map/backward/pallas_call | solution.py:456
  113.2 0.0 collective-permute-done.3.other_ref
  113.2 1.6 %finish.1 = (f32[96,2592]{1,0:T(8,128)}, f32[192,768]{1,0:T(8,128)}) custom-call(s32[1]{0:T(128)} %bitcast.core_ref, bf16[32,72,128]{2,1,0:T(8,128)(2,1)S(1)} %all_to_all.27.halo_ref.mine_ref, bf16[32,72,128]{2,1,0:T(8,128)(2,1)S(1)} %collective-permute-done.3.other_ref), custom_call_target="tpu_custom_call" | custom-call | tf_op jit(solution)/shard_map/finish/pallas_call | solution.py:463
  (1 shorter events, 0.0 us)
Async XLA Ops:
  23.2 3.9 %collective-permute-start = (bf16[32,24,128]{2,1,0:T(8,128)(2,1)S(1)}, bf16[32,24,128]{2,1,0:T(8,128)(2,1)S(1)}, u32[]{:S(2)}, u32[]{:S(2)}) collective-permute-start(bf16[32,24,128]{2,1,0:T(8,128)(2,1)S(1)} %all_to_all.25.owner_ref.mine_ref), channel_id=1, source_target_pairs={{0,1},{1,0},{2,3},{3,2},{4,5},{5,4},{6,7},{7,6},{8,9},{9,8},{10,11... | collective-permute-start | bytes 589832 | tf_op jit(solution)/shard_map/ppermute | solution.py:387
  28.9 4.0 %copy-start = (bf16[1,1,96,1024]{3,2,1,0:T(8,128)(2,1)S(1)}, bf16[1,1,96,1024]{3,2,1,0:T(8,128)(2,1)}, u32[]{:S(2)}) copy-start(bf16[1,1,96,1024]{3,2,1,0:T(8,128)(2,1)} %param.6) | copy-start | bytes 589828
  28.9 13.4 %all-to-all-start.1 = ((bf16[32,24,128]{2,1,0:T(8,128)(2,1)}), bf16[32,24,128]{2,1,0:T(8,128)(2,1)S(1)}, u32[]{:S(2)}, u32[]{:S(2)}) async-start(bf16[32,24,128]{2,1,0:T(8,128)(2,1)} %route.2), calls=%async_computation.1 | async-start | bytes 393216 | tf_op jit(solution)/shard_map/all_to_all | solution.py:373
  32.9 1.0 copy-start.5
  34.4 1.0 copy-start.4
  35.8 0.8 copy-start.2
  37.7 1.4 %copy-start.3 = (bf16[96,2592]{0,1:T(8,128)(2,1)S(1)}, bf16[96,2592]{0,1:T(8,128)(2,1)}, u32[]{:S(2)}) copy-start(bf16[96,2592]{0,1:T(8,128)(2,1)} %copy-done.2) | copy-start | bytes 1492996
  39.1 3.2 %copy-start.1 = (bf16[1,1,192,128]{3,2,1,0:T(8,128)(2,1)S(1)}, bf16[1,1,192,128]{3,2,1,0:T(8,128)(2,1)}, u32[]{:S(2)}) copy-start(bf16[1,1,192,128]{3,2,1,0:T(8,128)(2,1)} %param.7) | copy-start | bytes 147460
  46.2 4.4 %collective-permute-start.1 = (bf16[1664,128]{1,0:T(8,128)(2,1)S(1)}, bf16[1664,128]{1,0:T(8,128)(2,1)S(1)}, u32[]{:S(2)}, u32[]{:S(2)}) collective-permute-start(bf16[1664,128]{1,0:T(8,128)(2,1)S(1)} %get-tuple-element.30), channel_id=1, source_target_pairs={{0,1},{1,0},{2,3},{3,2},{4,5},{5,4},{6,7},{7,6},{8,9},{9,8},{10,11... | collective-permute-start | bytes 1277960 | tf_op jit(solution)/shard_map/ppermute | solution.py:387
  71.7 4.5 %collective-permute-start.2 = (bf16[32,24,128]{2,1,0:T(8,128)(2,1)S(1)}, bf16[32,24,128]{2,1,0:T(8,128)(2,1)S(1)}, u32[]{:S(2)}, u32[]{:S(2)}) collective-permute-start(bf16[32,24,128]{2,1,0:T(8,128)(2,1)S(1)} %get-tuple-element.31.mine_ref), channel_id=1, source_target_pairs={{0,1},{1,0},{2,3},{3,2},{4,5},{5,4},{6,7},{7,6},{8,9},{9,8},{10,11... | collective-permute-start | bytes 589832 | tf_op jit(solution)/shard_map/ppermute | solution.py:387
  76.2 8.9 %all-to-all-start.3 = ((f32[4,72,128]{2,1,0:T(8,128)}), f32[4,72,128]{2,1,0:T(8,128)S(1)}, u32[]{:S(2)}, u32[]{:S(2)}) async-start(f32[4,72,128]{2,1,0:T(8,128)} %get-tuple-element.33), calls=%async_computation.3 | async-start | bytes 294912 | tf_op jit(solution)/shard_map/all_to_all | solution.py:373
  104.7 8.5 %collective-permute-start.3 = (bf16[32,72,128]{2,1,0:T(8,128)(2,1)S(1)}, bf16[32,72,128]{2,1,0:T(8,128)(2,1)S(1)}, u32[]{:S(2)}, u32[]{:S(2)}) collective-permute-start(bf16[32,72,128]{2,1,0:T(8,128)(2,1)S(1)} %all_to_all.27.halo_ref.mine_ref), channel_id=1, source_target_pairs={{0,1},{1,0},{2,3},{3,2},{4,5},{5,4},{6,7},{7,6},{8,9},{9,8},{10,11... | collective-permute-start | bytes 1769480 | tf_op jit(solution)/shard_map/ppermute | solution.py:387

commit v8 on v7

--- a/solution.py
+++ b/solution.py
@@ -292,6 +292,12 @@
     coarse_ref[...] = dot(dw_ref[...], patch_ref[...], 1, 1).astype(BF16)
 
 
+def fetch_kernel(got_hbm, got_ref, sem):
+    copy = pltpu.make_async_copy(got_hbm, got_ref, sem)
+    copy.start()
+    copy.wait()
+
+
 def backward_kernel(grad_ref, halo_ref, w_ref, out_ref, pad_ref, cols_ref, act_ref, row_ref, flat_ref):
     for x in range(SIDE):
         for y in range(SIDE):
@@ -445,13 +451,21 @@
     message = (32, 72, LANES)
     (out,) = call(merge_kernel, [(message, BF16)], ins=3, name="merge")(spread2, keep, here(swap(send)))
     part, middle2 = call(total_kernel, [((4, 72, LANES), F32), (packed, BF16)], ins=1, name="total")(
-        here(trade(out, CHIPS))
+        there(trade(out, CHIPS))
     )
     other2, part = lax.optimization_barrier((swap(middle2), part))
     line = trade(part, "x")
     (routed2,) = route(core, middle, middle2, here(other2))
     (out,) = call(join_kernel, [(message, BF16)], ins=2, name="join")(here(line), routed2)
-    got = trade(out, CHIPS)
+    (got,) = pl.pallas_call(
+        fetch_kernel,
+        out_shape=[pltpu.VMEM(message, BF16)],
+        in_specs=[pl.BlockSpec(memory_space=pltpu.HBM)],
+        out_specs=[pl.BlockSpec(memory_space=pltpu.VMEM)],
+        scratch_shapes=[pltpu.SemaphoreType.DMA],
+        compiler_params=PARAMS,
+        name="fetch",
+    )(there(trade(out, CHIPS)))
     theirs = swap(got)
     (grad_features,) = call(
         backward_kernel,

time: 115 us -> 118 us (1.026)
  Pallas kernels: 14.8 us -> 16.9 us
  transfers between devices with their start and end apart: 6 -> 6, of which waited for: 5 -> 5; matrix products, arithmetic and copies ran while one was open for 3% -> 3% of each run, Pallas kernels for 5% -> 4%
where the time goes in v8:
time: 118 us; the launch traced here: 117 us
  blocking collectives  61.2 us (52%)
  starting transfers between devices  23 us (19%)
  Pallas kernels  16.9 us (14%)
  waiting for transfers between devices  9.32 us (8%)
  local copies, waits for them, and re-layouts  6.22 us (5%)
    all_to_all x3, blocking collectives, trade(): return lax.all_to_all(rows, axes, 0, 0, tiled=True)  61.2 us
    ppermute x4, starting transfers between devices, swap(): return lax.ppermute(rows, 'c', [(0, 1), (1, 0)])  15 us
    all_to_all x2, starting transfers between devices, trade(): return lax.all_to_all(rows, axes, 0, 0, tiled=True)  8.01 us
    all_to_all x2, waiting for transfers between devices, trade(): return lax.all_to_all(rows, axes, 0, 0, tiled=True)  6.73 us
    unnamed x15, local copies, waits for them, and re-layouts  4.06 us
    pallas_call x1, Pallas kernels, shards(): call(forward_kernel, [rows_shape, ((LANES, 8 * LANES), BF16), ((HALF_ROWS...  3.89 us
    pallas_call x1, Pallas kernels, shards(): call(backward_kernel, [((C, VOX), F32, True)], [pad_scratch, cols_scratch...  3.01 us
    ppermute x4, waiting for transfers between devices, swap(): return lax.ppermute(rows, 'c', [(0, 1), (1, 0)])  2.59 us
  transfers between devices with their start and end apart: 6, of which 5 were waited for; matrix products, arithmetic and copies ran while one was open for 3% of the time, Pallas kernels for 4%

profile of v8, /device:TPU:1, one launch (start us, length us, event | category | flops | bytes accessed | tf_op | source)
XLA Modules:
  0.0 117.4 jit_solution(656428562023952244)
XLA Ops:
  0.6 1.3 %spread.1 = bf16[32,24,128]{2,1,0:T(8,128)(2,1)S(1)} custom-call(s32[1,26]{1,0:T(1,128)} %bitcast.28, bf16[96,1024]{1,0:T(8,128)(2,1)} %bitcast.21, s32[32,128]{1,0:T(8,128)} %constant.9.clone.table_hbm), custom_call_target="tpu_custom_call" | custom-call | tf_op jit(solution)/shard_map/spread/pallas_call | solution.py:395
  1.9 21.2 %all_to_all.25.owner_ref.mine_ref = bf16[32,24,128]{2,1,0:T(8,128)(2,1)S(1)} all-to-all(bf16[32,24,128]{2,1,0:T(8,128)(2,1)S(1)} %spread.1), channel_id=1, replica_groups=mesh['x'=4,'y'=4,'z'=8,'c'=2] {'y','z'}, dimensions={0} | all-to-all | bytes 393216 | tf_op jit(solution)/shard_map/all_to_all | solution.py:379
  23.2 2.8 %collective-permute-start = (bf16[32,24,128]{2,1,0:T(8,128)(2,1)S(1)}, bf16[32,24,128]{2,1,0:T(8,128)(2,1)S(1)}, u32[]{:S(2)}, u32[]{:S(2)}) collective-permute-start(bf16[32,24,128]{2,1,0:T(8,128)(2,1)S(1)} %all_to_all.25.owner_ref.mine_ref), channel_id=1, source_target_pairs={{0,1},{1,0},{2,3},{3,2},{4,5},{5,4},{6,7},{7,6},{8,9},{9,8},{10,11... | collective-permute-start | bytes 589832 | tf_op jit(solution)/shard_map/ppermute | solution.py:393
  26.0 1.1 collective-permute-done.other_ref
  27.1 1.8 %route.2 = bf16[32,24,128]{2,1,0:T(8,128)(2,1)} custom-call(s32[1]{0:T(128)} %bitcast.core_ref, bf16[32,24,128]{2,1,0:T(8,128)(2,1)S(1)} %all_to_all.25.owner_ref.mine_ref, bf16[32,24,128]{2,1,0:T(8,128)(2,1)S(1)} %all_to_all.25.owner_ref.mine_ref, bf16[32,24,128]{2,1,0:T(8,128)(2,1)S(1)} %collective-permute-done.other_ref), custom_call_target="tpu_custom_call" | custom-call | tf_op jit(solution)/shard_map/route/pallas_call | solution.py:414
  28.9 0.0 copy-start
  28.9 4.0 %all-to-all-start.1 = ((bf16[32,24,128]{2,1,0:T(8,128)(2,1)}), bf16[32,24,128]{2,1,0:T(8,128)(2,1)S(1)}, u32[]{:S(2)}, u32[]{:S(2)}) async-start(bf16[32,24,128]{2,1,0:T(8,128)(2,1)} %route.2), calls=%async_computation.1 | async-start | bytes 393216 | tf_op jit(solution)/shard_map/all_to_all | solution.py:379
  32.9 0.0 copy-done
  32.9 0.0 copy-start.5
  32.9 0.1 prepare.1.own_ref
  33.1 0.8 copy-done.5
  33.9 0.4 reshape.30
  34.3 0.1 pad.13
  34.4 0.0 copy-start.4
  34.4 0.1 copy.17
  34.5 1.0 copy-done.4
  35.5 0.3 copy.12
  35.8 0.0 copy-start.2
  35.8 0.8 copy-done.2
  36.6 1.1 copy.14
  37.7 0.0 copy-start.3
  37.7 1.4 %pad.12.clone = bf16[27,128,128]{2,1,0:T(8,128)(2,1)S(1)} pad(bf16[27,96,96]{2,1,0:T(8,128)(2,1)} %copy.14, bf16[]{:T(256)} %constant.8.clone.1), padding=0_0x0_32x0_32 | pad | bytes 1382402 | tf_op jit(solution)/shard_map/jit(_pad)/pad | solution.py:420
  39.1 0.0 copy-done.3
  39.1 0.0 copy-start.1
  39.1 0.2 pad.11
  39.4 2.9 %all-to-all-done.1.halo_ref = bf16[32,24,128]{2,1,0:T(8,128)(2,1)S(1)} async-done(((bf16[32,24,128]{2,1,0:T(8,128)(2,1)}), bf16[32,24,128]{2,1,0:T(8,128)(2,1)S(1)}, u32[]{:S(2)}, u32[]{:S(2)}) %all-to-all-start.1) | async-done | bytes 196640 | tf_op jit(solution)/shard_map/all_to_all | solution.py:379
  42.3 0.0 copy-done.1
  42.3 3.9 %forward.1 = (bf16[1024,128]{1,0:T(8,128)(2,1)S(1)}, bf16[128,1024]{1,0:T(8,128)(2,1)S(1)}, f32[1664,128]{1,0:T(8,128)S(1)}, bf16[1664,128]{1,0:T(8,128)(2,1)S(1)}) custom-call(s32[1]{0:T(128)} %bitcast.core_ref, f32[1024,128]{1,0:T(8,128)S(1)} %prepare.1.own_ref, bf16[32,24,128]{2,1,0:T(8,128)(2,1)S(1)} %all-to-all-done.1.halo_ref, ...), custom_call_target="tpu_custom_call" | custom-call | tf_op jit(solution)/shard_map/forward/pallas_call | solution.py:430
  46.2 3.0 %collective-permute-start.1 = (bf16[1664,128]{1,0:T(8,128)(2,1)S(1)}, bf16[1664,128]{1,0:T(8,128)(2,1)S(1)}, u32[]{:S(2)}, u32[]{:S(2)}) collective-permute-start(bf16[1664,128]{1,0:T(8,128)(2,1)S(1)} %get-tuple-element.30), channel_id=1, source_target_pairs={{0,1},{1,0},{2,3},{3,2},{4,5},{5,4},{6,7},{7,6},{8,9},{9,8},{10,11... | collective-permute-start | bytes 1277960 | tf_op jit(solution)/shard_map/ppermute | solution.py:393
  49.2 1.0 side.1
  50.2 0.4 collective-permute-done.1.other_ref
  50.6 0.1 merge.1
  50.7 20.3 %all_to_all.26.got_ref = bf16[32,72,128]{2,1,0:T(8,128)(2,1)} all-to-all(bf16[32,72,128]{2,1,0:T(8,128)(2,1)S(1)} %merge.1), channel_id=1, replica_groups=mesh['x'=4,'y'=4,'z'=8,'c'=2] {'y','z'}, dimensions={0} | all-to-all | bytes 1179648 | tf_op jit(solution)/shard_map/all_to_all | solution.py:379
  71.0 1.8 %total.1 = (f32[4,72,128]{2,1,0:T(8,128)}, bf16[32,24,128]{2,1,0:T(8,128)(2,1)S(1)}) custom-call(bf16[32,72,128]{2,1,0:T(8,128)(2,1)} %all_to_all.26.got_ref), custom_call_target="tpu_custom_call" | custom-call | tf_op jit(solution)/shard_map/total/pallas_call | solution.py:453
  72.8 3.4 %collective-permute-start.2 = (bf16[32,24,128]{2,1,0:T(8,128)(2,1)S(1)}, bf16[32,24,128]{2,1,0:T(8,128)(2,1)S(1)}, u32[]{:S(2)}, u32[]{:S(2)}) collective-permute-start(bf16[32,24,128]{2,1,0:T(8,128)(2,1)S(1)} %get-tuple-element.31.mine_ref), channel_id=1, source_target_pairs={{0,1},{1,0},{2,3},{3,2},{4,5},{5,4},{6,7},{7,6},{8,9},{9,8},{10,11... | collective-permute-start | bytes 589832 | tf_op jit(solution)/shard_map/ppermute | solution.py:393
  76.2 1.1 collective-permute-done.2.other_ref
  77.3 4.0 %all-to-all-start.3 = ((f32[4,72,128]{2,1,0:T(8,128)}), f32[4,72,128]{2,1,0:T(8,128)S(1)}, u32[]{:S(2)}, u32[]{:S(2)}) async-start(f32[4,72,128]{2,1,0:T(8,128)} %get-tuple-element.33), calls=%async_computation.3 | async-start | bytes 294912 | tf_op jit(solution)/shard_map/all_to_all | solution.py:379
  81.3 1.1 route.3.rows_ref
  82.4 3.8 %all-to-all-done.3.line_ref = f32[4,72,128]{2,1,0:T(8,128)S(1)} async-done(((f32[4,72,128]{2,1,0:T(8,128)}), f32[4,72,128]{2,1,0:T(8,128)S(1)}, u32[]{:S(2)}, u32[]{:S(2)}) %all-to-all-start.3) | async-done | bytes 147488 | tf_op jit(solution)/shard_map/all_to_all | solution.py:379
  86.2 0.1 join.1
  86.3 19.7 %all_to_all.27.got_hbm = bf16[32,72,128]{2,1,0:T(8,128)(2,1)} all-to-all(bf16[32,72,128]{2,1,0:T(8,128)(2,1)S(1)} %join.1), channel_id=1, replica_groups=mesh['x'=4,'y'=4,'z'=8,'c'=2] {'y','z'}, dimensions={0} | all-to-all | bytes 1179648 | tf_op jit(solution)/shard_map/all_to_all | solution.py:379
  106.0 1.1 fetch.1.halo_ref.mine_ref
  107.1 5.7 %collective-permute-start.3 = (bf16[32,72,128]{2,1,0:T(8,128)(2,1)S(1)}, bf16[32,72,128]{2,1,0:T(8,128)(2,1)S(1)}, u32[]{:S(2)}, u32[]{:S(2)}) collective-permute-start(bf16[32,72,128]{2,1,0:T(8,128)(2,1)S(1)} %fetch.1.halo_ref.mine_ref), channel_id=1, source_target_pairs={{0,1},{1,0},{2,3},{3,2},{4,5},{5,4},{6,7},{7,6},{8,9},{9,8},{10,11... | collective-permute-start | bytes 1769480 | tf_op jit(solution)/shard_map/ppermute | solution.py:393
  112.8 3.0 %backward.1 = f32[96,1024]{1,0:T(8,128)} custom-call(bf16[1024,128]{1,0:T(8,128)(2,1)S(1)} %get-tuple-element.25.grad_ref, bf16[32,72,128]{2,1,0:T(8,128)(2,1)S(1)} %fetch.1.halo_ref.mine_ref, bf16[9,384,128]{2,1,0:T(8,128)(2,1)S(1)} %bitcast.20), custom_call_target="tpu_custom_call" | custom-call | tf_op jit(solution)/shard_map/backward/pallas_call | solution.py:470
  115.8 0.0 collective-permute-done.3.other_ref
  115.8 1.6 %finish.1 = (f32[96,2592]{1,0:T(8,128)}, f32[192,768]{1,0:T(8,128)}) custom-call(s32[1]{0:T(128)} %bitcast.core_ref, bf16[32,72,128]{2,1,0:T(8,128)(2,1)S(1)} %fetch.1.halo_ref.mine_ref, bf16[32,72,128]{2,1,0:T(8,128)(2,1)S(1)} %collective-permute-done.3.other_ref), custom_call_target="tpu_custom_call" | custom-call | tf_op jit(solution)/shard_map/finish/pallas_call | solution.py:477
  (1 shorter events, 0.0 us)
Async XLA Ops:
  23.2 3.9 %collective-permute-start = (bf16[32,24,128]{2,1,0:T(8,128)(2,1)S(1)}, bf16[32,24,128]{2,1,0:T(8,128)(2,1)S(1)}, u32[]{:S(2)}, u32[]{:S(2)}) collective-permute-start(bf16[32,24,128]{2,1,0:T(8,128)(2,1)S(1)} %all_to_all.25.owner_ref.mine_ref), channel_id=1, source_target_pairs={{0,1},{1,0},{2,3},{3,2},{4,5},{5,4},{6,7},{7,6},{8,9},{9,8},{10,11... | collective-permute-start | bytes 589832 | tf_op jit(solution)/shard_map/ppermute | solution.py:393
  28.9 4.0 %copy-start = (bf16[1,1,96,1024]{3,2,1,0:T(8,128)(2,1)S(1)}, bf16[1,1,96,1024]{3,2,1,0:T(8,128)(2,1)}, u32[]{:S(2)}) copy-start(bf16[1,1,96,1024]{3,2,1,0:T(8,128)(2,1)} %param.6) | copy-start | bytes 589828
  28.9 13.4 %all-to-all-start.1 = ((bf16[32,24,128]{2,1,0:T(8,128)(2,1)}), bf16[32,24,128]{2,1,0:T(8,128)(2,1)S(1)}, u32[]{:S(2)}, u32[]{:S(2)}) async-start(bf16[32,24,128]{2,1,0:T(8,128)(2,1)} %route.2), calls=%async_computation.1 | async-start | bytes 393216 | tf_op jit(solution)/shard_map/all_to_all | solution.py:379
  32.9 1.0 copy-start.5
  34.4 1.0 copy-start.4
  35.8 0.8 copy-start.2
  37.7 1.4 %copy-start.3 = (bf16[96,2592]{0,1:T(8,128)(2,1)S(1)}, bf16[96,2592]{0,1:T(8,128)(2,1)}, u32[]{:S(2)}) copy-start(bf16[96,2592]{0,1:T(8,128)(2,1)} %copy-done.2) | copy-start | bytes 1492996
  39.1 3.2 %copy-start.1 = (bf16[1,1,192,128]{3,2,1,0:T(8,128)(2,1)S(1)}, bf16[1,1,192,128]{3,2,1,0:T(8,128)(2,1)}, u32[]{:S(2)}) copy-start(bf16[1,1,192,128]{3,2,1,0:T(8,128)(2,1)} %param.7) | copy-start | bytes 147460
  46.2 4.4 %collective-permute-start.1 = (bf16[1664,128]{1,0:T(8,128)(2,1)S(1)}, bf16[1664,128]{1,0:T(8,128)(2,1)S(1)}, u32[]{:S(2)}, u32[]{:S(2)}) collective-permute-start(bf16[1664,128]{1,0:T(8,128)(2,1)S(1)} %get-tuple-element.30), channel_id=1, source_target_pairs={{0,1},{1,0},{2,3},{3,2},{4,5},{5,4},{6,7},{7,6},{8,9},{9,8},{10,11... | collective-permute-start | bytes 1277960 | tf_op jit(solution)/shard_map/ppermute | solution.py:393
  72.8 4.5 %collective-permute-start.2 = (bf16[32,24,128]{2,1,0:T(8,128)(2,1)S(1)}, bf16[32,24,128]{2,1,0:T(8,128)(2,1)S(1)}, u32[]{:S(2)}, u32[]{:S(2)}) collective-permute-start(bf16[32,24,128]{2,1,0:T(8,128)(2,1)S(1)} %get-tuple-element.31.mine_ref), channel_id=1, source_target_pairs={{0,1},{1,0},{2,3},{3,2},{4,5},{5,4},{6,7},{7,6},{8,9},{9,8},{10,11... | collective-permute-start | bytes 589832 | tf_op jit(solution)/shard_map/ppermute | solution.py:393
  77.3 8.9 %all-to-all-start.3 = ((f32[4,72,128]{2,1,0:T(8,128)}), f32[4,72,128]{2,1,0:T(8,128)S(1)}, u32[]{:S(2)}, u32[]{:S(2)}) async-start(f32[4,72,128]{2,1,0:T(8,128)} %get-tuple-element.33), calls=%async_computation.3 | async-start | bytes 294912 | tf_op jit(solution)/shard_map/all_to_all | solution.py:379
  107.1 8.8 %collective-permute-start.3 = (bf16[32,72,128]{2,1,0:T(8,128)(2,1)S(1)}, bf16[32,72,128]{2,1,0:T(8,128)(2,1)S(1)}, u32[]{:S(2)}, u32[]{:S(2)}) collective-permute-start(bf16[32,72,128]{2,1,0:T(8,128)(2,1)S(1)} %fetch.1.halo_ref.mine_ref), channel_id=1, source_target_pairs={{0,1},{1,0},{2,3},{3,2},{4,5},{5,4},{6,7},{7,6},{8,9},{9,8},{10,11... | collective-permute-start | bytes 1769480 | tf_op jit(solution)/shard_map/ppermute | solution.py:393

commit v9 on v7

--- a/solution.py
+++ b/solution.py
@@ -226,6 +226,19 @@
         part = dot(window(cols_ref, tap // 3, tap % 3), w_ref[tap])
         total = part if total is None else total + part
     return total
+
+
+def planes(cols_ref, first, last, dy):
+    return cols_ref[first:last, dy : dy + 8].reshape((last - first) * LANES, 3 * LANES)
+
+
+def conv_wide(cols_ref, w_ref):
+    both = last = 0.0
+    for dy in range(3):
+        pair = jnp.concatenate([w_ref[dy], w_ref[3 + dy]], axis=1)
+        both = both + dot(planes(cols_ref, 0, 9, dy), pair)
+        last = last + dot(planes(cols_ref, 2, 10, dy), w_ref[6 + dy])
+    return both[:VOX, :LANES] + both[LANES:, LANES:] + last
 
 
 def forward_kernel(
@@ -302,7 +315,7 @@
                 ].astype(F32)
     fill_halo(pad_ref, halo_ref, row_ref, flat_ref)
     shifted_columns(pad_ref, cols_ref)
-    full = conv(cols_ref, w_ref)
+    full = conv_wide(cols_ref, w_ref)
     for n in range(64):
         for par in range(2):
             act_ref[pl.ds(n * 16 + par, 8, stride=2), :] = full[n * 16 + par * 8 : n * 16 + par * 8 + 8, :]
@@ -447,7 +460,7 @@
     part, middle2 = call(total_kernel, [((4, 72, LANES), F32), (packed, BF16)], ins=1, name="total")(
         here(trade(out, CHIPS))
     )
-    other2, part = lax.optimization_barrier((swap(middle2), part))
+    other2 = swap(middle2)
     line = trade(part, "x")
     (routed2,) = route(core, middle, middle2, here(other2))
     (out,) = call(join_kernel, [(message, BF16)], ins=2, name="join")(here(line), routed2)

time: 115 us -> 114 us (level)
  transfers between devices with their start and end apart: 6 -> 6, of which waited for: 5 -> 4; matrix products, arithmetic and copies ran while one was open for 3% -> 3% of each run, Pallas kernels for 5% -> 4%
where the time goes in v9:
time: 114 us
  blocking collectives  61.9 us (54%)
  starting transfers between devices  22.1 us (19%)
  Pallas kernels  14.5 us (13%)
  waiting for transfers between devices  8.33 us (7%)
  local copies, waits for them, and re-layouts  6.22 us (5%)
    all_to_all x3, blocking collectives, trade(): return lax.all_to_all(rows, axes, 0, 0, tiled=True)  61.9 us
    ppermute x4, starting transfers between devices, swap(): return lax.ppermute(rows, 'c', [(0, 1), (1, 0)])  14.1 us
    all_to_all x2, starting transfers between devices, trade(): return lax.all_to_all(rows, axes, 0, 0, tiled=True)  8.01 us
    all_to_all x2, waiting for transfers between devices, trade(): return lax.all_to_all(rows, axes, 0, 0, tiled=True)  6.81 us
    unnamed x15, local copies, waits for them, and re-layouts  4.06 us
    pallas_call x1, Pallas kernels, shards(): call(forward_kernel, [rows_shape, ((LANES, 8 * LANES), BF16), ((HALF_ROWS...  3.89 us
    pallas_call x1, Pallas kernels, shards(): call(backward_kernel, [((C, VOX), F32, True)], [pad_scratch, cols_scratch...  2.76 us
  transfers between devices with their start and end apart: 6, of which 4 were waited for; matrix products, arithmetic and copies ran while one was open for 3% of the time, Pallas kernels for 4%

profile of v9, /device:TPU:1, one launch (start us, length us, event | category | flops | bytes accessed | tf_op | source)
XLA Modules:
  0.0 113.8 jit_solution(17287033847716552033)
XLA Ops:
  0.6 1.3 %spread.1 = bf16[32,24,128]{2,1,0:T(8,128)(2,1)S(1)} custom-call(s32[1,26]{1,0:T(1,128)} %bitcast.28, bf16[96,1024]{1,0:T(8,128)(2,1)} %bitcast.21, s32[32,128]{1,0:T(8,128)} %constant.9.clone.table_hbm), custom_call_target="tpu_custom_call" | custom-call | tf_op jit(solution)/shard_map/spread/pallas_call | solution.py:402
  1.9 21.2 %all_to_all.25.owner_ref.mine_ref = bf16[32,24,128]{2,1,0:T(8,128)(2,1)S(1)} all-to-all(bf16[32,24,128]{2,1,0:T(8,128)(2,1)S(1)} %spread.1), channel_id=1, replica_groups=mesh['x'=4,'y'=4,'z'=8,'c'=2] {'y','z'}, dimensions={0} | all-to-all | bytes 393216 | tf_op jit(solution)/shard_map/all_to_all | solution.py:386
  23.2 2.8 %collective-permute-start = (bf16[32,24,128]{2,1,0:T(8,128)(2,1)S(1)}, bf16[32,24,128]{2,1,0:T(8,128)(2,1)S(1)}, u32[]{:S(2)}, u32[]{:S(2)}) collective-permute-start(bf16[32,24,128]{2,1,0:T(8,128)(2,1)S(1)} %all_to_all.25.owner_ref.mine_ref), channel_id=1, source_target_pairs={{0,1},{1,0},{2,3},{3,2},{4,5},{5,4},{6,7},{7,6},{8,9},{9,8},{10,11... | collective-permute-start | bytes 589832 | tf_op jit(solution)/shard_map/ppermute | solution.py:400
  26.0 1.1 collective-permute-done.other_ref
  27.1 1.8 %route.2 = bf16[32,24,128]{2,1,0:T(8,128)(2,1)} custom-call(s32[1]{0:T(128)} %bitcast.core_ref, bf16[32,24,128]{2,1,0:T(8,128)(2,1)S(1)} %all_to_all.25.owner_ref.mine_ref, bf16[32,24,128]{2,1,0:T(8,128)(2,1)S(1)} %all_to_all.25.owner_ref.mine_ref, bf16[32,24,128]{2,1,0:T(8,128)(2,1)S(1)} %collective-permute-done.other_ref), custom_call_target="tpu_custom_call" | custom-call | tf_op jit(solution)/shard_map/route/pallas_call | solution.py:421
  28.9 0.0 copy-start
  28.9 4.0 %all-to-all-start.1 = ((bf16[32,24,128]{2,1,0:T(8,128)(2,1)}), bf16[32,24,128]{2,1,0:T(8,128)(2,1)S(1)}, u32[]{:S(2)}, u32[]{:S(2)}) async-start(bf16[32,24,128]{2,1,0:T(8,128)(2,1)} %route.2), calls=%async_computation.1 | async-start | bytes 393216 | tf_op jit(solution)/shard_map/all_to_all | solution.py:386
  32.9 0.0 copy-done
  32.9 0.0 copy-start.5
  32.9 0.1 prepare.1.own_ref
  33.1 0.8 copy-done.5
  33.9 0.4 reshape.30
  34.3 0.1 pad.13
  34.4 0.0 copy-start.4
  34.4 0.1 copy.17
  34.5 1.0 copy-done.4
  35.5 0.3 copy.12
  35.8 0.0 copy-start.2
  35.8 0.8 copy-done.2
  36.6 1.1 copy.14
  37.7 0.0 copy-start.3
  37.7 1.4 %pad.12.clone = bf16[27,128,128]{2,1,0:T(8,128)(2,1)S(1)} pad(bf16[27,96,96]{2,1,0:T(8,128)(2,1)} %copy.14, bf16[]{:T(256)} %constant.8.clone.1), padding=0_0x0_32x0_32 | pad | bytes 1382402 | tf_op jit(solution)/shard_map/jit(_pad)/pad | solution.py:427
  39.1 0.0 copy-done.3
  39.1 0.0 copy-start.1
  39.1 0.2 pad.11
  39.4 2.9 %all-to-all-done.1.halo_ref = bf16[32,24,128]{2,1,0:T(8,128)(2,1)S(1)} async-done(((bf16[32,24,128]{2,1,0:T(8,128)(2,1)}), bf16[32,24,128]{2,1,0:T(8,128)(2,1)S(1)}, u32[]{:S(2)}, u32[]{:S(2)}) %all-to-all-start.1) | async-done | bytes 196640 | tf_op jit(solution)/shard_map/all_to_all | solution.py:386
  42.3 0.0 copy-done.1
  42.3 3.9 %forward.1 = (bf16[1024,128]{1,0:T(8,128)(2,1)S(1)}, bf16[128,1024]{1,0:T(8,128)(2,1)S(1)}, f32[1664,128]{1,0:T(8,128)S(1)}, bf16[1664,128]{1,0:T(8,128)(2,1)S(1)}) custom-call(s32[1]{0:T(128)} %bitcast.core_ref, f32[1024,128]{1,0:T(8,128)S(1)} %prepare.1.own_ref, bf16[32,24,128]{2,1,0:T(8,128)(2,1)S(1)} %all-to-all-done.1.halo_ref, ...), custom_call_target="tpu_custom_call" | custom-call | tf_op jit(solution)/shard_map/forward/pallas_call | solution.py:437
  46.2 3.0 %collective-permute-start.1 = (bf16[1664,128]{1,0:T(8,128)(2,1)S(1)}, bf16[1664,128]{1,0:T(8,128)(2,1)S(1)}, u32[]{:S(2)}, u32[]{:S(2)}) collective-permute-start(bf16[1664,128]{1,0:T(8,128)(2,1)S(1)} %get-tuple-element.28), channel_id=1, source_target_pairs={{0,1},{1,0},{2,3},{3,2},{4,5},{5,4},{6,7},{7,6},{8,9},{9,8},{10,11... | collective-permute-start | bytes 1277960 | tf_op jit(solution)/shard_map/ppermute | solution.py:400
  49.2 1.0 side.1
  50.2 0.4 collective-permute-done.1.other_ref
  50.6 0.1 merge.1
  50.7 20.2 %all_to_all.26.got_ref = bf16[32,72,128]{2,1,0:T(8,128)(2,1)S(1)} all-to-all(bf16[32,72,128]{2,1,0:T(8,128)(2,1)S(1)} %merge.1), channel_id=1, replica_groups=mesh['x'=4,'y'=4,'z'=8,'c'=2] {'y','z'}, dimensions={0} | all-to-all | bytes 1179648 | tf_op jit(solution)/shard_map/all_to_all | solution.py:386
  70.9 0.8 total.1
  71.7 3.4 %collective-permute-start.2 = (bf16[32,24,128]{2,1,0:T(8,128)(2,1)S(1)}, bf16[32,24,128]{2,1,0:T(8,128)(2,1)S(1)}, u32[]{:S(2)}, u32[]{:S(2)}) collective-permute-start(bf16[32,24,128]{2,1,0:T(8,128)(2,1)S(1)} %get-tuple-element.30.mine_ref), channel_id=1, source_target_pairs={{0,1},{1,0},{2,3},{3,2},{4,5},{5,4},{6,7},{7,6},{8,9},{9,8},{10,11... | collective-permute-start | bytes 589832 | tf_op jit(solution)/shard_map/ppermute | solution.py:400
  75.1 4.0 %all-to-all-start.3 = ((f32[4,72,128]{2,1,0:T(8,128)}), f32[4,72,128]{2,1,0:T(8,128)S(1)}, u32[]{:S(2)}, u32[]{:S(2)}) async-start(f32[4,72,128]{2,1,0:T(8,128)} %get-tuple-element.29), calls=%async_computation.3 | async-start | bytes 294912 | tf_op jit(solution)/shard_map/all_to_all | solution.py:386
  79.1 0.0 collective-permute-done.2.other_ref
  79.1 1.1 route.3.rows_ref
  80.2 3.9 %all-to-all-done.3.line_ref = f32[4,72,128]{2,1,0:T(8,128)S(1)} async-done(((f32[4,72,128]{2,1,0:T(8,128)}), f32[4,72,128]{2,1,0:T(8,128)S(1)}, u32[]{:S(2)}, u32[]{:S(2)}) %all-to-all-start.3) | async-done | bytes 147488 | tf_op jit(solution)/shard_map/all_to_all | solution.py:386
  84.1 0.1 join.1
  84.1 20.4 %all_to_all.27.halo_ref.mine_ref = bf16[32,72,128]{2,1,0:T(8,128)(2,1)S(1)} all-to-all(bf16[32,72,128]{2,1,0:T(8,128)(2,1)S(1)} %join.1), channel_id=1, replica_groups=mesh['x'=4,'y'=4,'z'=8,'c'=2] {'y','z'}, dimensions={0} | all-to-all | bytes 1179648 | tf_op jit(solution)/shard_map/all_to_all | solution.py:386
  104.6 4.8 %collective-permute-start.3 = (bf16[32,72,128]{2,1,0:T(8,128)(2,1)S(1)}, bf16[32,72,128]{2,1,0:T(8,128)(2,1)S(1)}, u32[]{:S(2)}, u32[]{:S(2)}) collective-permute-start(bf16[32,72,128]{2,1,0:T(8,128)(2,1)S(1)} %all_to_all.27.halo_ref.mine_ref), channel_id=1, source_target_pairs={{0,1},{1,0},{2,3},{3,2},{4,5},{5,4},{6,7},{7,6},{8,9},{9,8},{10,11... | collective-permute-start | bytes 1769480 | tf_op jit(solution)/shard_map/ppermute | solution.py:400
  109.4 2.8 %backward.1 = f32[96,1024]{1,0:T(8,128)} custom-call(bf16[1024,128]{1,0:T(8,128)(2,1)S(1)} %get-tuple-element.23.grad_ref, bf16[32,72,128]{2,1,0:T(8,128)(2,1)S(1)} %all_to_all.27.halo_ref.mine_ref, bf16[9,384,128]{2,1,0:T(8,128)(2,1)S(1)} %bitcast.20), custom_call_target="tpu_custom_call" | custom-call | tf_op jit(solution)/shard_map/backward/pallas_call | solution.py:469
  112.2 0.0 collective-permute-done.3.other_ref
  112.2 1.6 %finish.1 = (f32[96,2592]{1,0:T(8,128)}, f32[192,768]{1,0:T(8,128)}) custom-call(s32[1]{0:T(128)} %bitcast.core_ref, bf16[32,72,128]{2,1,0:T(8,128)(2,1)S(1)} %all_to_all.27.halo_ref.mine_ref, bf16[32,72,128]{2,1,0:T(8,128)(2,1)S(1)} %collective-permute-done.3.other_ref), custom_call_target="tpu_custom_call" | custom-call | tf_op jit(solution)/shard_map/finish/pallas_call | solution.py:476
  (1 shorter events, 0.0 us)
Async XLA Ops:
  23.2 3.9 %collective-permute-start = (bf16[32,24,128]{2,1,0:T(8,128)(2,1)S(1)}, bf16[32,24,128]{2,1,0:T(8,128)(2,1)S(1)}, u32[]{:S(2)}, u32[]{:S(2)}) collective-permute-start(bf16[32,24,128]{2,1,0:T(8,128)(2,1)S(1)} %all_to_all.25.owner_ref.mine_ref), channel_id=1, source_target_pairs={{0,1},{1,0},{2,3},{3,2},{4,5},{5,4},{6,7},{7,6},{8,9},{9,8},{10,11... | collective-permute-start | bytes 589832 | tf_op jit(solution)/shard_map/ppermute | solution.py:400
  28.9 4.0 %copy-start = (bf16[1,1,96,1024]{3,2,1,0:T(8,128)(2,1)S(1)}, bf16[1,1,96,1024]{3,2,1,0:T(8,128)(2,1)}, u32[]{:S(2)}) copy-start(bf16[1,1,96,1024]{3,2,1,0:T(8,128)(2,1)} %param.6) | copy-start | bytes 589828
  28.9 13.4 %all-to-all-start.1 = ((bf16[32,24,128]{2,1,0:T(8,128)(2,1)}), bf16[32,24,128]{2,1,0:T(8,128)(2,1)S(1)}, u32[]{:S(2)}, u32[]{:S(2)}) async-start(bf16[32,24,128]{2,1,0:T(8,128)(2,1)} %route.2), calls=%async_computation.1 | async-start | bytes 393216 | tf_op jit(solution)/shard_map/all_to_all | solution.py:386
  32.9 1.0 copy-start.5
  34.4 1.0 copy-start.4
  35.8 0.8 copy-start.2
  37.7 1.4 %copy-start.3 = (bf16[96,2592]{0,1:T(8,128)(2,1)S(1)}, bf16[96,2592]{0,1:T(8,128)(2,1)}, u32[]{:S(2)}) copy-start(bf16[96,2592]{0,1:T(8,128)(2,1)} %copy-done.2) | copy-start | bytes 1492996
  39.1 3.2 %copy-start.1 = (bf16[1,1,192,128]{3,2,1,0:T(8,128)(2,1)S(1)}, bf16[1,1,192,128]{3,2,1,0:T(8,128)(2,1)}, u32[]{:S(2)}) copy-start(bf16[1,1,192,128]{3,2,1,0:T(8,128)(2,1)} %param.7) | copy-start | bytes 147460
  46.2 4.4 %collective-permute-start.1 = (bf16[1664,128]{1,0:T(8,128)(2,1)S(1)}, bf16[1664,128]{1,0:T(8,128)(2,1)S(1)}, u32[]{:S(2)}, u32[]{:S(2)}) collective-permute-start(bf16[1664,128]{1,0:T(8,128)(2,1)S(1)} %get-tuple-element.28), channel_id=1, source_target_pairs={{0,1},{1,0},{2,3},{3,2},{4,5},{5,4},{6,7},{7,6},{8,9},{9,8},{10,11... | collective-permute-start | bytes 1277960 | tf_op jit(solution)/shard_map/ppermute | solution.py:400
  71.7 7.4 %collective-permute-start.2 = (bf16[32,24,128]{2,1,0:T(8,128)(2,1)S(1)}, bf16[32,24,128]{2,1,0:T(8,128)(2,1)S(1)}, u32[]{:S(2)}, u32[]{:S(2)}) collective-permute-start(bf16[32,24,128]{2,1,0:T(8,128)(2,1)S(1)} %get-tuple-element.30.mine_ref), channel_id=1, source_target_pairs={{0,1},{1,0},{2,3},{3,2},{4,5},{5,4},{6,7},{7,6},{8,9},{9,8},{10,11... | collective-permute-start | bytes 589832 | tf_op jit(solution)/shard_map/ppermute | solution.py:400
  75.1 9.0 %all-to-all-start.3 = ((f32[4,72,128]{2,1,0:T(8,128)}), f32[4,72,128]{2,1,0:T(8,128)S(1)}, u32[]{:S(2)}, u32[]{:S(2)}) async-start(f32[4,72,128]{2,1,0:T(8,128)} %get-tuple-element.29), calls=%async_computation.3 | async-start | bytes 294912 | tf_op jit(solution)/shard_map/all_to_all | solution.py:386
  104.6 7.6 %collective-permute-start.3 = (bf16[32,72,128]{2,1,0:T(8,128)(2,1)S(1)}, bf16[32,72,128]{2,1,0:T(8,128)(2,1)S(1)}, u32[]{:S(2)}, u32[]{:S(2)}) collective-permute-start(bf16[32,72,128]{2,1,0:T(8,128)(2,1)S(1)} %all_to_all.27.halo_ref.mine_ref), channel_id=1, source_target_pairs={{0,1},{1,0},{2,3},{3,2},{4,5},{5,4},{6,7},{7,6},{8,9},{9,8},{10,11... | collective-permute-start | bytes 1769480 | tf_op jit(solution)/shard_map/ppermute | solution.py:400

commit v10 on v9

--- a/solution.py
+++ b/solution.py
@@ -155,17 +155,22 @@
 def total_kernel(got_ref, part_ref, rows_ref):
     total = jnp.sum(got_ref[...].astype(F32), axis=0)
     for n in range(4):
-        part_ref[n] = total
+        part_ref[n, 0:48] = total[24:]
+        part_ref[n, 48:56] = jnp.zeros((8, LANES), F32)
+        for part in range(3):
+            part_ref[n, 48 + part : 49 + part] = total[part * 8 + 7 : part * 8 + 8]
     rows_ref[...] = got_ref[:, 0:24]
 
 
 def join_kernel(line_ref, rows_ref, out_ref):
     whole = line_ref[0] + line_ref[1] + line_ref[2] + line_ref[3]
-    out_ref[:, 24:72] = jnp.broadcast_to(whole[24:], (32, 48, LANES)).astype(BF16)
-    place = lax.broadcasted_iota(jnp.int32, (32, 24, LANES), 1) & 7
-    rows = rows_ref[...].astype(F32)
-    free = (place == 7) & (lanes_of(rows) >= C)
-    out_ref[:, 0:24] = jnp.where(free, jnp.broadcast_to(whole[:24], rows.shape), rows).astype(BF16)
+    out_ref[:, 24:72] = jnp.broadcast_to(whole[:48], (32, 48, LANES)).astype(BF16)
+    place = lax.broadcasted_iota(jnp.int32, (32, 8, LANES), 1)
+    for part in range(3):
+        rows = rows_ref[:, part * 8 : part * 8 + 8].astype(F32)
+        free = (place == 7) & (lanes_of(rows) >= C)
+        last = jnp.broadcast_to(whole[48 + part : 49 + part], rows.shape)
+        out_ref[:, part * 8 : part * 8 + 8] = jnp.where(free, last, rows).astype(BF16)
 
 
 def route_kernel(core_ref, owner_ref, mine_ref, other_ref, out_ref, row_ref):
@@ -457,7 +462,7 @@
 
     message = (32, 72, LANES)
     (out,) = call(merge_kernel, [(message, BF16)], ins=3, name="merge")(spread2, keep, here(swap(send)))
-    part, middle2 = call(total_kernel, [((4, 72, LANES), F32), (packed, BF16)], ins=1, name="total")(
+    part, middle2 = call(total_kernel, [((4, 56, LANES), F32), (packed, BF16)], ins=1, name="total")(
         here(trade(out, CHIPS))
     )
     other2 = swap(middle2)

time: 114 us -> 114 us (level)
  no operation moved by 1% of the time
where the time goes in v10:
time: 114 us
  blocking collectives  61.9 us (54%)
  starting transfers between devices  22.1 us (19%)
  Pallas kernels  14.5 us (13%)
  waiting for transfers between devices  8.09 us (7%)
  local copies, waits for them, and re-layouts  6.22 us (5%)
    all_to_all x3, blocking collectives, trade(): return lax.all_to_all(rows, axes, 0, 0, tiled=True)  61.9 us
    ppermute x4, starting transfers between devices, swap(): return lax.ppermute(rows, 'c', [(0, 1), (1, 0)])  14.1 us
    all_to_all x2, starting transfers between devices, trade(): return lax.all_to_all(rows, axes, 0, 0, tiled=True)  8.01 us
    all_to_all x2, waiting for transfers between devices, trade(): return lax.all_to_all(rows, axes, 0, 0, tiled=True)  6.57 us
    unnamed x15, local copies, waits for them, and re-layouts  4.06 us
    pallas_call x1, Pallas kernels, shards(): call(forward_kernel, [rows_shape, ((LANES, 8 * LANES), BF16), ((HALF_ROWS...  3.89 us
    pallas_call x1, Pallas kernels, shards(): call(backward_kernel, [((C, VOX), F32, True)], [pad_scratch, cols_scratch...  2.76 us
  transfers between devices with their start and end apart: 6, of which 4 were waited for; matrix products, arithmetic and copies ran while one was open for 3% of the time, Pallas kernels for 4%

profile of v10, /device:TPU:1, one launch (start us, length us, event | category | flops | bytes accessed | tf_op | source)
XLA Modules:
  0.0 113.5 jit_solution(12650715907606550521)
XLA Ops:
  0.6 1.3 %spread.1 = bf16[32,24,128]{2,1,0:T(8,128)(2,1)S(1)} custom-call(s32[1,26]{1,0:T(1,128)} %bitcast.28, bf16[96,1024]{1,0:T(8,128)(2,1)} %bitcast.21, s32[32,128]{1,0:T(8,128)} %constant.9.clone.table_hbm), custom_call_target="tpu_custom_call" | custom-call | tf_op jit(solution)/shard_map/spread/pallas_call | solution.py:407
  1.9 21.2 %all_to_all.25.owner_ref.mine_ref = bf16[32,24,128]{2,1,0:T(8,128)(2,1)S(1)} all-to-all(bf16[32,24,128]{2,1,0:T(8,128)(2,1)S(1)} %spread.1), channel_id=1, replica_groups=mesh['x'=4,'y'=4,'z'=8,'c'=2] {'y','z'}, dimensions={0} | all-to-all | bytes 393216 | tf_op jit(solution)/shard_map/all_to_all | solution.py:391
  23.2 2.8 %collective-permute-start = (bf16[32,24,128]{2,1,0:T(8,128)(2,1)S(1)}, bf16[32,24,128]{2,1,0:T(8,128)(2,1)S(1)}, u32[]{:S(2)}, u32[]{:S(2)}) collective-permute-start(bf16[32,24,128]{2,1,0:T(8,128)(2,1)S(1)} %all_to_all.25.owner_ref.mine_ref), channel_id=1, source_target_pairs={{0,1},{1,0},{2,3},{3,2},{4,5},{5,4},{6,7},{7,6},{8,9},{9,8},{10,11... | collective-permute-start | bytes 589832 | tf_op jit(solution)/shard_map/ppermute | solution.py:405
  26.0 1.1 collective-permute-done.other_ref
  27.1 1.8 %route.2 = bf16[32,24,128]{2,1,0:T(8,128)(2,1)} custom-call(s32[1]{0:T(128)} %bitcast.core_ref, bf16[32,24,128]{2,1,0:T(8,128)(2,1)S(1)} %all_to_all.25.owner_ref.mine_ref, bf16[32,24,128]{2,1,0:T(8,128)(2,1)S(1)} %all_to_all.25.owner_ref.mine_ref, bf16[32,24,128]{2,1,0:T(8,128)(2,1)S(1)} %collective-permute-done.other_ref), custom_call_target="tpu_custom_call" | custom-call | tf_op jit(solution)/shard_map/route/pallas_call | solution.py:426
  28.9 0.0 copy-start
  28.9 4.0 %all-to-all-start.1 = ((bf16[32,24,128]{2,1,0:T(8,128)(2,1)}), bf16[32,24,128]{2,1,0:T(8,128)(2,1)S(1)}, u32[]{:S(2)}, u32[]{:S(2)}) async-start(bf16[32,24,128]{2,1,0:T(8,128)(2,1)} %route.2), calls=%async_computation.1 | async-start | bytes 393216 | tf_op jit(solution)/shard_map/all_to_all | solution.py:391
  32.9 0.0 copy-done
  32.9 0.0 copy-start.5
  32.9 0.1 prepare.1.own_ref
  33.1 0.8 copy-done.5
  33.9 0.4 reshape.30
  34.3 0.1 pad.13
  34.4 0.0 copy-start.4
  34.4 0.1 copy.17
  34.5 1.0 copy-done.4
  35.5 0.3 copy.12
  35.8 0.0 copy-start.2
  35.8 0.8 copy-done.2
  36.6 1.1 copy.14
  37.7 0.0 copy-start.3
  37.7 1.4 %pad.12.clone = bf16[27,128,128]{2,1,0:T(8,128)(2,1)S(1)} pad(bf16[27,96,96]{2,1,0:T(8,128)(2,1)} %copy.14, bf16[]{:T(256)} %constant.8.clone.1), padding=0_0x0_32x0_32 | pad | bytes 1382402 | tf_op jit(solution)/shard_map/jit(_pad)/pad | solution.py:432
  39.1 0.0 copy-done.3
  39.1 0.0 copy-start.1
  39.1 0.2 pad.11
  39.4 2.9 %all-to-all-done.1.halo_ref = bf16[32,24,128]{2,1,0:T(8,128)(2,1)S(1)} async-done(((bf16[32,24,128]{2,1,0:T(8,128)(2,1)}), bf16[32,24,128]{2,1,0:T(8,128)(2,1)S(1)}, u32[]{:S(2)}, u32[]{:S(2)}) %all-to-all-start.1) | async-done | bytes 196640 | tf_op jit(solution)/shard_map/all_to_all | solution.py:391
  42.3 0.0 copy-done.1
  42.3 3.9 %forward.1 = (bf16[1024,128]{1,0:T(8,128)(2,1)S(1)}, bf16[128,1024]{1,0:T(8,128)(2,1)S(1)}, f32[1664,128]{1,0:T(8,128)S(1)}, bf16[1664,128]{1,0:T(8,128)(2,1)S(1)}) custom-call(s32[1]{0:T(128)} %bitcast.core_ref, f32[1024,128]{1,0:T(8,128)S(1)} %prepare.1.own_ref, bf16[32,24,128]{2,1,0:T(8,128)(2,1)S(1)} %all-to-all-done.1.halo_ref, ...), custom_call_target="tpu_custom_call" | custom-call | tf_op jit(solution)/shard_map/forward/pallas_call | solution.py:442
  46.2 3.0 %collective-permute-start.1 = (bf16[1664,128]{1,0:T(8,128)(2,1)S(1)}, bf16[1664,128]{1,0:T(8,128)(2,1)S(1)}, u32[]{:S(2)}, u32[]{:S(2)}) collective-permute-start(bf16[1664,128]{1,0:T(8,128)(2,1)S(1)} %get-tuple-element.28), channel_id=1, source_target_pairs={{0,1},{1,0},{2,3},{3,2},{4,5},{5,4},{6,7},{7,6},{8,9},{9,8},{10,11... | collective-permute-start | bytes 1277960 | tf_op jit(solution)/shard_map/ppermute | solution.py:405
  49.2 1.0 side.1
  50.2 0.4 collective-permute-done.1.other_ref
  50.6 0.1 merge.1
  50.7 20.2 %all_to_all.26.got_ref = bf16[32,72,128]{2,1,0:T(8,128)(2,1)S(1)} all-to-all(bf16[32,72,128]{2,1,0:T(8,128)(2,1)S(1)} %merge.1), channel_id=1, replica_groups=mesh['x'=4,'y'=4,'z'=8,'c'=2] {'y','z'}, dimensions={0} | all-to-all | bytes 1179648 | tf_op jit(solution)/shard_map/all_to_all | solution.py:391
  70.9 0.7 total.1
  71.7 3.4 %collective-permute-start.2 = (bf16[32,24,128]{2,1,0:T(8,128)(2,1)S(1)}, bf16[32,24,128]{2,1,0:T(8,128)(2,1)S(1)}, u32[]{:S(2)}, u32[]{:S(2)}) collective-permute-start(bf16[32,24,128]{2,1,0:T(8,128)(2,1)S(1)} %get-tuple-element.30.mine_ref), channel_id=1, source_target_pairs={{0,1},{1,0},{2,3},{3,2},{4,5},{5,4},{6,7},{7,6},{8,9},{9,8},{10,11... | collective-permute-start | bytes 589832 | tf_op jit(solution)/shard_map/ppermute | solution.py:405
  75.1 4.0 %all-to-all-start.3 = ((f32[4,56,128]{2,1,0:T(8,128)}), f32[4,56,128]{2,1,0:T(8,128)S(1)}, u32[]{:S(2)}, u32[]{:S(2)}) async-start(f32[4,56,128]{2,1,0:T(8,128)} %get-tuple-element.29), calls=%async_computation.3 | async-start | bytes 229376 | tf_op jit(solution)/shard_map/all_to_all | solution.py:391
  79.1 0.0 collective-permute-done.2.other_ref
  79.1 1.1 route.3.rows_ref
  80.2 3.6 %all-to-all-done.3.line_ref = f32[4,56,128]{2,1,0:T(8,128)S(1)} async-done(((f32[4,56,128]{2,1,0:T(8,128)}), f32[4,56,128]{2,1,0:T(8,128)S(1)}, u32[]{:S(2)}, u32[]{:S(2)}) %all-to-all-start.3) | async-done | bytes 114720 | tf_op jit(solution)/shard_map/all_to_all | solution.py:391
  83.8 0.1 join.1
  83.9 20.4 %all_to_all.27.halo_ref.mine_ref = bf16[32,72,128]{2,1,0:T(8,128)(2,1)S(1)} all-to-all(bf16[32,72,128]{2,1,0:T(8,128)(2,1)S(1)} %join.1), channel_id=1, replica_groups=mesh['x'=4,'y'=4,'z'=8,'c'=2] {'y','z'}, dimensions={0} | all-to-all | bytes 1179648 | tf_op jit(solution)/shard_map/all_to_all | solution.py:391
  104.3 4.8 %collective-permute-start.3 = (bf16[32,72,128]{2,1,0:T(8,128)(2,1)S(1)}, bf16[32,72,128]{2,1,0:T(8,128)(2,1)S(1)}, u32[]{:S(2)}, u32[]{:S(2)}) collective-permute-start(bf16[32,72,128]{2,1,0:T(8,128)(2,1)S(1)} %all_to_all.27.halo_ref.mine_ref), channel_id=1, source_target_pairs={{0,1},{1,0},{2,3},{3,2},{4,5},{5,4},{6,7},{7,6},{8,9},{9,8},{10,11... | collective-permute-start | bytes 1769480 | tf_op jit(solution)/shard_map/ppermute | solution.py:405
  109.1 2.8 %backward.1 = f32[96,1024]{1,0:T(8,128)} custom-call(bf16[1024,128]{1,0:T(8,128)(2,1)S(1)} %get-tuple-element.23.grad_ref, bf16[32,72,128]{2,1,0:T(8,128)(2,1)S(1)} %all_to_all.27.halo_ref.mine_ref, bf16[9,384,128]{2,1,0:T(8,128)(2,1)S(1)} %bitcast.20), custom_call_target="tpu_custom_call" | custom-call | tf_op jit(solution)/shard_map/backward/pallas_call | solution.py:474
  111.9 0.0 collective-permute-done.3.other_ref
  111.9 1.6 %finish.1 = (f32[96,2592]{1,0:T(8,128)}, f32[192,768]{1,0:T(8,128)}) custom-call(s32[1]{0:T(128)} %bitcast.core_ref, bf16[32,72,128]{2,1,0:T(8,128)(2,1)S(1)} %all_to_all.27.halo_ref.mine_ref, bf16[32,72,128]{2,1,0:T(8,128)(2,1)S(1)} %collective-permute-done.3.other_ref), custom_call_target="tpu_custom_call" | custom-call | tf_op jit(solution)/shard_map/finish/pallas_call | solution.py:481
  (1 shorter events, 0.0 us)
Async XLA Ops:
  23.2 3.9 %collective-permute-start = (bf16[32,24,128]{2,1,0:T(8,128)(2,1)S(1)}, bf16[32,24,128]{2,1,0:T(8,128)(2,1)S(1)}, u32[]{:S(2)}, u32[]{:S(2)}) collective-permute-start(bf16[32,24,128]{2,1,0:T(8,128)(2,1)S(1)} %all_to_all.25.owner_ref.mine_ref), channel_id=1, source_target_pairs={{0,1},{1,0},{2,3},{3,2},{4,5},{5,4},{6,7},{7,6},{8,9},{9,8},{10,11... | collective-permute-start | bytes 589832 | tf_op jit(solution)/shard_map/ppermute | solution.py:405
  28.9 4.0 %copy-start = (bf16[1,1,96,1024]{3,2,1,0:T(8,128)(2,1)S(1)}, bf16[1,1,96,1024]{3,2,1,0:T(8,128)(2,1)}, u32[]{:S(2)}) copy-start(bf16[1,1,96,1024]{3,2,1,0:T(8,128)(2,1)} %param.6) | copy-start | bytes 589828
  28.9 13.4 %all-to-all-start.1 = ((bf16[32,24,128]{2,1,0:T(8,128)(2,1)}), bf16[32,24,128]{2,1,0:T(8,128)(2,1)S(1)}, u32[]{:S(2)}, u32[]{:S(2)}) async-start(bf16[32,24,128]{2,1,0:T(8,128)(2,1)} %route.2), calls=%async_computation.1 | async-start | bytes 393216 | tf_op jit(solution)/shard_map/all_to_all | solution.py:391
  32.9 1.0 copy-start.5
  34.4 1.0 copy-start.4
  35.8 0.8 copy-start.2
  37.7 1.4 %copy-start.3 = (bf16[96,2592]{0,1:T(8,128)(2,1)S(1)}, bf16[96,2592]{0,1:T(8,128)(2,1)}, u32[]{:S(2)}) copy-start(bf16[96,2592]{0,1:T(8,128)(2,1)} %copy-done.2) | copy-start | bytes 1492996
  39.1 3.2 %copy-start.1 = (bf16[1,1,192,128]{3,2,1,0:T(8,128)(2,1)S(1)}, bf16[1,1,192,128]{3,2,1,0:T(8,128)(2,1)}, u32[]{:S(2)}) copy-start(bf16[1,1,192,128]{3,2,1,0:T(8,128)(2,1)} %param.7) | copy-start | bytes 147460
  46.2 4.4 %collective-permute-start.1 = (bf16[1664,128]{1,0:T(8,128)(2,1)S(1)}, bf16[1664,128]{1,0:T(8,128)(2,1)S(1)}, u32[]{:S(2)}, u32[]{:S(2)}) collective-permute-start(bf16[1664,128]{1,0:T(8,128)(2,1)S(1)} %get-tuple-element.28), channel_id=1, source_target_pairs={{0,1},{1,0},{2,3},{3,2},{4,5},{5,4},{6,7},{7,6},{8,9},{9,8},{10,11... | collective-permute-start | bytes 1277960 | tf_op jit(solution)/shard_map/ppermute | solution.py:405
  71.7 7.4 %collective-permute-start.2 = (bf16[32,24,128]{2,1,0:T(8,128)(2,1)S(1)}, bf16[32,24,128]{2,1,0:T(8,128)(2,1)S(1)}, u32[]{:S(2)}, u32[]{:S(2)}) collective-permute-start(bf16[32,24,128]{2,1,0:T(8,128)(2,1)S(1)} %get-tuple-element.30.mine_ref), channel_id=1, source_target_pairs={{0,1},{1,0},{2,3},{3,2},{4,5},{5,4},{6,7},{7,6},{8,9},{9,8},{10,11... | collective-permute-start | bytes 589832 | tf_op jit(solution)/shard_map/ppermute | solution.py:405
  75.1 8.8 %all-to-all-start.3 = ((f32[4,56,128]{2,1,0:T(8,128)}), f32[4,56,128]{2,1,0:T(8,128)S(1)}, u32[]{:S(2)}, u32[]{:S(2)}) async-start(f32[4,56,128]{2,1,0:T(8,128)} %get-tuple-element.29), calls=%async_computation.3 | async-start | bytes 229376 | tf_op jit(solution)/shard_map/all_to_all | solution.py:391
  104.3 7.6 %collective-permute-start.3 = (bf16[32,72,128]{2,1,0:T(8,128)(2,1)S(1)}, bf16[32,72,128]{2,1,0:T(8,128)(2,1)S(1)}, u32[]{:S(2)}, u32[]{:S(2)}) collective-permute-start(bf16[32,72,128]{2,1,0:T(8,128)(2,1)S(1)} %all_to_all.27.halo_ref.mine_ref), channel_id=1, source_target_pairs={{0,1},{1,0},{2,3},{3,2},{4,5},{5,4},{6,7},{7,6},{8,9},{9,8},{10,11... | collective-permute-start | bytes 1769480 | tf_op jit(solution)/shard_map/ppermute | solution.py:405
